TPU v7x, 32 devices: a whole 2x2x4 slice. The times are simulated.
32 devices in a mesh: dp: 8 (over z, x), narrow: 4 (over y, core).
Axes of the slice: x: 2, y: 2, z: 4, core: 2. Of those that a mesh axis runs over, the one named last changes fastest.
Arguments:
- wave: float32 [1313280], P(('dp', 'narrow')), may hold values from -6 to 6
- clip_ids: int32 [4096], P(('dp', 'narrow')), may hold values from 0 to 95, never falling along the last dimension, each value on 1 to 128 neighbouring positions
- span_starts: int32 [4096], P(('dp', 'narrow')), may hold values 0 or 1
- step_count: int32 [1], replicated, may hold values from 2 to 20
- conv_small: float32 [12, 512], replicated, as said below
- conv_stack: float32 [8192, 512], P(('dp', 'narrow')), may hold values from -0.25 to 0.25
- side: float32 [768, 2192], P('dp', 'narrow'), may hold values from -0.21875 to 0.21875
- vectors: float32 [10, 768], replicated, as said below
- block: float32 [3, 768, 3072], P(None, 'dp', 'narrow')
- teacher_block: float32 [3, 768, 3072], P(None, 'dp', 'narrow')
- teacher_vectors: float32 [10, 768], replicated, as said below
- small_mean: float32 [12, 512], replicated, may hold values from -4.4428212e-05 to 4.4428212e-05
- small_square: float32 [12, 512], replicated, may hold values from 1.2336662e-10 to 4.934665e-10
- stack_mean: float32 [8192, 512], P(('dp', 'narrow')), may hold values from -1.1107053e-05 to 1.1107053e-05
- stack_square: float32 [8192, 512], P(('dp', 'narrow')), may hold values from 7.710414e-12 to 3.0841656e-11
- side_mean: float32 [768, 2192], P('dp', 'narrow'), may hold values from -1.1107053e-05 to 1.1107053e-05
- side_square: float32 [768, 2192], P('dp', 'narrow'), may hold values from 7.710414e-12 to 3.0841656e-11
- vector_mean: float32 [10, 768], replicated, may hold values from -4.4428212e-05 to 4.4428212e-05
- vector_square: float32 [10, 768], replicated, may hold values from 1.2336662e-10 to 4.934665e-10
- block_momentum: float32 [3, 768, 3072], P(None, 'dp', 'narrow'), may hold values from -1.1107053e-05 to 1.1107053e-05
Outputs:
- loss: float32 [], replicated
- grad_norm: float32 [], replicated
- conv_small_next: float32 [12, 512], replicated
- small_mean_next: float32 [12, 512], replicated
- small_square_next: float32 [12, 512], replicated
- conv_stack_next: float32 [8192, 512], P(('dp', 'narrow'))
- stack_mean_next: float32 [8192, 512], P(('dp', 'narrow'))
- stack_square_next: float32 [8192, 512], P(('dp', 'narrow'))
- side_next: float32 [768, 2192], P('dp', 'narrow')
- side_mean_next: float32 [768, 2192], P('dp', 'narrow')
- side_square_next: float32 [768, 2192], P('dp', 'narrow')
- vectors_next: float32 [10, 768], replicated
- vector_mean_next: float32 [10, 768], replicated
- vector_square_next: float32 [10, 768], replicated
- block_next: float32 [3, 768, 3072], P(None, 'dp', 'narrow')
- momentum_next: float32 [3, 768, 3072], P(None, 'dp', 'narrow')
- teacher_block_next: float32 [3, 768, 3072], P(None, 'dp', 'narrow')
- teacher_vectors_next: float32 [10, 768], replicated
- block_copy: bfloat16 [3, 768, 3072], P(None, 'dp', 'narrow')
Inputs may be any that keep to these rules, and one draw needn't show every extreme that they name: `clip_ids`: clip numbers never fall along the frames; a clip has 1 to 128 frames, and some clip has exactly 128. `conv_small`: rows 10 are positive gains. `vectors`: rows 0, 2, 4 are positive gains. `teacher_vectors`: rows 0, 2, 4 are positive gains.
All inputs are finite; a program needn't handle non-finite values. No bound on the sum of `span_starts` on one device may be relied on, other than what follows from the above.
Results may differ from a plain program's by a relative error of at most 0.0025.
The roundings to bfloat16 on the way count: a program that leaves them out, or rounds other values in their place, can miss the bound.
Values may be sent and summed in bfloat16 or wider, within the bound.
No kernel may reach another device: no remote copies, remote signals or barrier semaphores. Data moves between devices by JAX's collectives and lax.ppermute only.
A program may use at most 448 MiB of HBM per device.

v0:
```python
import math

import jax
import jax.numpy as jnp
from jax import lax
from jax.sharding import PartitionSpec as P

D = 768
HEADS = 12
HEAD_DIM = 64
CH = 512
GROUPS = 16
POS_K = 19
SPAN = 10


EPS = 1e-05
VAR_FLOOR = 0.1
CLIP_LIMIT = 0.01
LR_ADAM = 0.03
LR_MUON = 2.0
DECAY = 0.5
WEIGHT_DECAY = 0.01
EMA_RATE = 0.5
KERNELS = (3, 3, 3, 3, 2, 2)
COEFF_A = 3.4445
COEFF_B = -4.775
COEFF_C = 2.0315
HIGHEST = lax.Precision.HIGHEST


def rounded(values):
    return lax.optimization_barrier(values.astype(jnp.bfloat16)).astype(jnp.float32)


def low(values):
    return values + lax.stop_gradient(rounded(values) - values)


def low_back(values):
    return rounded(values) + lax.stop_gradient(values - rounded(values))


def bprod(left_side, right_side):
    return low_back(jnp.einsum("bmk,bkn->bmn", left_side, right_side, precision=HIGHEST))


def matmul(left_side, right_side):
    return bprod(left_side[None], right_side[None])[0]


def layer_norm(values, gain, shift):
    center = values - jnp.mean(values, axis=-1, keepdims=True)
    spread = jnp.mean(center * center, axis=-1, keepdims=True)
    return center * lax.rsqrt(spread + EPS) * gain + shift


def strided_taps(values, kernel, stride, rows_out):
    return jnp.concatenate(
        [
            lax.slice_in_dim(values, offset, offset + stride * (rows_out - 1) + 1, stride, 0)
            for offset in range(kernel)
        ],
        axis=1,
    )


def encode(conv_small, conv_stack, side, vectors, wave):
    frames = (wave.shape[0] - 80) // 320
    length = 64 * frames + 15
    hidden = strided_taps(low(wave)[:, None], 10, 5, length)
    hidden = low(jax.nn.gelu(matmul(hidden, conv_small[:10]), approximate=False))
    row_offset = 0
    for kernel in KERNELS:
        length = (length - kernel) // 2 + 1
        tap_rows = strided_taps(hidden, kernel, 2, length)
        hidden = jax.nn.gelu(
            matmul(tap_rows, conv_stack[row_offset : row_offset + kernel * CH]), approximate=False
        )
        row_offset = row_offset + kernel * CH
        if row_offset < conv_stack.shape[0]:
            hidden = low(hidden)
    normed = low(layer_norm(hidden, conv_small[10], conv_small[11]))
    return matmul(normed, side[:, :CH].T) + vectors[6]


def neighbours(segment):
    frames = segment.shape[0]
    reach = POS_K // 2
    padded = jnp.pad(segment, (reach, reach), constant_values=-1)
    return jnp.stack(
        [padded[offset : offset + frames] == segment for offset in range(POS_K)], 0
    ).astype(jnp.float32)[:, :, None]


def masked_of(starts):
    frames = starts.shape[0]
    padded = jnp.pad(starts, (SPAN - 1, 0))
    return (
        jnp.max(jnp.stack([padded[offset : offset + frames] for offset in range(SPAN)], 0), axis=0)
        > 0
    )


def position(values, side, pos_bias, nearby):
    frames = values.shape[0]
    group_width = D // GROUPS
    reach = POS_K // 2
    padded = jnp.pad(low(values), ((reach, reach), (0, 0)))
    tap_rows = jnp.stack([padded[offset : offset + frames] for offset in range(POS_K)], 0) * nearby
    tap_rows = (
        tap_rows.reshape(POS_K, frames, GROUPS, group_width)
        .transpose(2, 1, 0, 3)
        .reshape(GROUPS, frames, POS_K * group_width)
    )
    kernel = side[:, CH : CH + POS_K * group_width].reshape(GROUPS, group_width, POS_K, group_width)
    kernel = kernel.transpose(0, 2, 1, 3).reshape(GROUPS, POS_K * group_width, group_width)
    mixed = bprod(tap_rows, kernel).transpose(1, 0, 2).reshape(frames, D)
    return jax.nn.gelu(mixed + pos_bias, approximate=False)


def transform(values, side, block, vectors, nearby, attend):
    frames = values.shape[0]
    hidden = layer_norm(values + position(values, side, vectors[7], nearby), vectors[0], vectors[1])
    triple = low(matmul(low(hidden), block[0][:, : 3 * D]))
    heads = triple.reshape(frames, 3, HEADS, HEAD_DIM).transpose(1, 2, 0, 3)
    scores = bprod(heads[0], heads[1].transpose(0, 2, 1)) / math.sqrt(HEAD_DIM)
    scores = jnp.where(attend[None], scores, -1e30)
    weights = low(jax.nn.softmax(scores, axis=-1))
    mixed = bprod(weights, heads[2]).transpose(1, 0, 2).reshape(frames, D)
    hidden = layer_norm(hidden + matmul(low(mixed), block[0][:, 3 * D :]), vectors[2], vectors[3])
    inner = low(jax.nn.gelu(matmul(low(hidden), block[1]), approximate=False))
    return layer_norm(hidden + matmul(inner, block[2].T), vectors[4], vectors[5])


def target_of(feats, side, teacher_block, teacher_vectors, nearby, attend):
    output = transform(feats, side, teacher_block, teacher_vectors, nearby, attend)
    member = attend.astype(jnp.float32)
    clip_size = jnp.sum(member, axis=1, keepdims=True)
    average = jnp.dot(member, output, precision=HIGHEST) / clip_size
    center = output - average
    spread = jnp.dot(member, center * center, precision=HIGHEST) / clip_size
    return center * lax.rsqrt(jnp.maximum(spread, VAR_FLOOR))


def student_loss(feats, side, block, vectors, nearby, attend, masked, target, total):
    chosen = masked[:, None]
    values = jnp.where(chosen, vectors[9], feats)
    hidden = transform(values, side, block, vectors, nearby, attend)
    predict = matmul(low(hidden), side[:, CH + POS_K * (D // GROUPS) :]) + vectors[8]
    error = jnp.where(chosen, predict - target, 0.0)
    return jnp.sum(error * error) / (total * math.sqrt(D))


def local_step(
    wave,
    segment,
    starts,
    conv_small,
    conv_stack,
    side,
    vectors,
    block,
    teacher_block,
    teacher_vectors,
    total,
):
    nearby = neighbours(segment)
    attend = segment[:, None] == segment[None, :]
    masked = masked_of(starts)
    feats, encode_back = jax.vjp(
        lambda small_part, stack_part, side_part, vector_part: encode(
            low(small_part), low(stack_part), low(side_part), low(vector_part), wave
        ),
        conv_small,
        conv_stack,
        side,
        vectors,
    )
    target = target_of(feats, low(side), low(teacher_block), low(teacher_vectors), nearby, attend)
    loss_part, student_back = jax.vjp(
        lambda feat_part, side_part, block_part, vector_part: student_loss(
            feat_part,
            low(side_part),
            low(block_part),
            low(vector_part),
            nearby,
            attend,
            masked,
            target,
            total,
        ),
        feats,
        side,
        block,
        vectors,
    )
    feat_grad, side_two, block_grad, vector_two = student_back(jnp.ones_like(loss_part))
    small_grad, stack_grad, side_one, vector_one = encode_back(feat_grad)
    return (
        loss_part,
        small_grad,
        stack_grad,
        side_one + side_two,
        block_grad,
        vector_one + vector_two,
    )


def adamw(weight, grad, first, second, power):
    first = DECAY * first + (1.0 - DECAY) * grad
    second = DECAY * second + (1.0 - DECAY) * grad * grad
    unbias = 1.0 - power
    step_size = first / unbias / (jnp.sqrt(second / unbias) + 1e-08)
    return (weight - LR_ADAM * (step_size + WEIGHT_DECAY * weight), first, second)


def orthogonal(matrix, gram_total):
    blocks = matrix
    for iteration in range(5):
        gram_matrix = gram_total(jnp.einsum("brc,bsc->brs", blocks, blocks, precision=HIGHEST))
        if iteration == 0:
            scales = 1.0 / (jnp.sqrt(jnp.trace(gram_matrix, axis1=1, axis2=2)) + 1e-07)
            blocks = blocks * scales[:, None, None]
            gram_matrix = gram_matrix * (scales * scales)[:, None, None]
        polynom = COEFF_B * gram_matrix + COEFF_C * jnp.einsum(
            "brs,bst->brt", gram_matrix, gram_matrix, precision=HIGHEST
        )
        blocks = COEFF_A * blocks + jnp.einsum("brs,bsc->brc", polynom, blocks, precision=HIGHEST)
    return blocks.reshape(matrix.shape)


def apply_updates(factor, power, weights, grads, states, gram_total):
    (
        small_weight,
        stack_weight,
        side_weight,
        vector_weight,
        block_weight,
        teacher_weight,
        teacher_vector,
    ) = weights
    small_grad, stack_grad, side_grad, block_grad, vector_grad = grads
    small_next = adamw(small_weight, factor * small_grad, states[0], states[1], power)
    stack_next = adamw(stack_weight, factor * stack_grad, states[2], states[3], power)
    side_next = adamw(side_weight, factor * side_grad, states[4], states[5], power)
    vector_next = adamw(vector_weight, factor * vector_grad, states[6], states[7], power)
    momentum = DECAY * states[8] + factor * block_grad
    block_next = block_weight * (1.0 - LR_MUON * WEIGHT_DECAY) - LR_MUON * orthogonal(
        momentum, gram_total
    )
    teacher_next = EMA_RATE * teacher_weight + (1.0 - EMA_RATE) * block_next
    teacher_vec_next = EMA_RATE * teacher_vector + (1.0 - EMA_RATE) * vector_next[0]
    return (
        small_next
        + stack_next
        + side_next
        + vector_next
        + (block_next, momentum, teacher_next, teacher_vec_next, block_next.astype(jnp.bfloat16))
    )


def narrow_total(gram_matrix):
    return lax.psum(gram_matrix, "narrow")


def per_device(
    wave,
    clip_ids,
    span_starts,
    step_count,
    conv_small,
    conv_stack,
    side,
    vectors,
    block,
    teacher_block,
    teacher_vectors,
    small_mean,
    small_square,
    stack_mean,
    stack_square,
    side_mean,
    side_square,
    vector_mean,
    vector_square,
    block_momentum,
):
    parts = (
        block.astype(jnp.bfloat16),
        teacher_block.astype(jnp.bfloat16),
        side.astype(jnp.bfloat16),
    )
    parts = (
        lax.all_gather(parts[0], "narrow", axis=2, tiled=True),
        lax.all_gather(parts[1], "narrow", axis=2, tiled=True),
        lax.all_gather(parts[2], "narrow", axis=1, tiled=True),
    )
    parts = (
        lax.all_gather(parts[0], "dp", axis=1, tiled=True),
        lax.all_gather(parts[1], "dp", axis=1, tiled=True),
        lax.all_gather(parts[2], "dp", axis=0, tiled=True),
    )
    whole_block = parts[0].astype(jnp.float32)
    whole_teacher = parts[1].astype(jnp.float32)
    whole_side = parts[2].astype(jnp.float32)
    whole_stack = lax.all_gather(
        conv_stack.astype(jnp.bfloat16), ("dp", "narrow"), axis=0, tiled=True
    ).astype(jnp.float32)
    masked_here = jnp.sum(masked_of(span_starts).astype(jnp.float32))
    total = jnp.maximum(lax.psum(masked_here, ("dp", "narrow")), 1.0)
    loss_part, small_grad, stack_grad, side_grad, block_grad, vector_grad = local_step(
        wave,
        clip_ids,
        span_starts,
        conv_small,
        whole_stack,
        whole_side,
        vectors,
        whole_block,
        whole_teacher,
        teacher_vectors,
        total,
    )
    row_parts = [
        lax.psum_scatter(block_grad[matrix_index], "dp", scatter_dimension=0, tiled=True)
        for matrix_index in range(3)
    ]
    side_rows = lax.psum_scatter(side_grad, "dp", scatter_dimension=0, tiled=True)
    pieces = (
        lax.psum_scatter(jnp.stack(row_parts, 0), "narrow", scatter_dimension=2, tiled=True),
        lax.psum_scatter(side_rows, "narrow", scatter_dimension=1, tiled=True),
    )
    block_piece = pieces[0]
    side_piece = pieces[1]
    stack_piece = lax.psum_scatter(stack_grad, ("dp", "narrow"), scatter_dimension=0, tiled=True)
    small_total, vector_total, loss_value = lax.psum(
        (small_grad, vector_grad, loss_part), ("dp", "narrow")
    )
    shard_squares = (
        jnp.sum(block_piece * block_piece)
        + jnp.sum(side_piece * side_piece)
        + jnp.sum(stack_piece * stack_piece)
    )
    grad_norm = jnp.sqrt(
        lax.psum(shard_squares, ("dp", "narrow"))
        + jnp.sum(small_total * small_total)
        + jnp.sum(vector_total * vector_total)
    )
    factor = jnp.minimum(1.0, CLIP_LIMIT / (grad_norm + 1e-06))
    power = jnp.power(DECAY, step_count[0].astype(jnp.float32))
    updates = apply_updates(
        factor,
        power,
        (conv_small, conv_stack, side, vectors, block, teacher_block, teacher_vectors),
        (small_total, stack_piece, side_piece, block_piece, vector_total),
        (
            small_mean,
            small_square,
            stack_mean,
            stack_square,
            side_mean,
            side_square,
            vector_mean,
            vector_square,
            block_momentum,
        ),
        narrow_total,
    )
    return (
        loss_value,
        grad_norm,
        updates[0],
        updates[1],
        updates[2],
        updates[3],
        updates[4],
        updates[5],
        updates[6],
        updates[7],
        updates[8],
        updates[9],
        updates[10],
        updates[11],
        updates[12],
        updates[13],
        updates[14],
        updates[15],
        updates[16],
    )


def solution(mesh):
    in_specs = (
        P(("dp", "narrow")),
        P(("dp", "narrow")),
        P(("dp", "narrow")),
        P(),
        P(),
        P(("dp", "narrow"), None),
        P("dp", "narrow"),
        P(),
        P(None, "dp", "narrow"),
        P(None, "dp", "narrow"),
        P(),
        P(),
        P(),
        P(("dp", "narrow"), None),
        P(("dp", "narrow"), None),
        P("dp", "narrow"),
        P("dp", "narrow"),
        P(),
        P(),
        P(None, "dp", "narrow"),
    )
    out_specs = (
        P(),
        P(),
        P(),
        P(),
        P(),
        P(("dp", "narrow"), None),
        P(("dp", "narrow"), None),
        P(("dp", "narrow"), None),
        P("dp", "narrow"),
        P("dp", "narrow"),
        P("dp", "narrow"),
        P(),
        P(),
        P(),
        P(None, "dp", "narrow"),
        P(None, "dp", "narrow"),
        P(None, "dp", "narrow"),
        P(),
        P(None, "dp", "narrow"),
    )
    return jax.shard_map(
        per_device, mesh=mesh, in_specs=in_specs, out_specs=out_specs, check_vma=False
    )
```

profile of v0, /device:TPU:0, one launch (start us, length us, event | category | flops | bytes accessed | tf_op | source)
XLA Modules:
  0.0 2136.7 jit_solution(9828727559107884883)
XLA Ops:
  34.9 39.8 %psum.70 = f32[]{:T(128)} all-reduce(f32[]{:T(128)} %get-tuple-element.160), channel_id=1, replica_groups=mesh['dp'=8,'narrow'=4] {'dp','narrow'}, use_global_device_ids=true, to_apply=%region_21.22 | all-reduce | flops 1 | bytes 8 | tf_op jit(solution)/shard_map/psum | solution.py:311
  115.6 39.3 %fusion.62 = (bf16[8207,512]{1,0:T(8,128)(2,1)}, f32[8207,512]{1,0:T(8,128)}) fusion(f32[8207,512]{1,0:T(8,128)S(1)} %fusion.404, bf16[1,8207,512]{2,1,0:T(8,128)(2,1)S(1)} %convert_bitcast_fusion), kind=kLoop, calls=%fused_computation.104 | loop fusion | flops 285734912 | bytes 50423808 | tf_op jit(solution)/shard_map/jvp()/convert_element_type | solution.py:33
  172.4 41.3 %slice.450 = f32[4103,512]{1,0:T(8,128)} slice(f32[8207,512]{1,0:T(8,128)} %subtract_add_fusion.2), slice={[0:8205:2], [0:512:1]} | slice | bytes 16805888 | tf_op jit(solution)/shard_map/jvp()/slice | solution.py:61
  213.7 41.1 %slice.451 = f32[4103,512]{1,0:T(8,128)} slice(f32[8207,512]{1,0:T(8,128)} %subtract_add_fusion.2), slice={[1:8206:2], [0:512:1]} | slice | bytes 16805888 | tf_op jit(solution)/shard_map/jvp()/slice | solution.py:61
  254.9 41.7 %slice.452 = f32[4103,512]{1,0:T(8,128)} slice(f32[8207,512]{1,0:T(8,128)} %subtract_add_fusion.2), slice={[2:8207:2], [0:512:1]} | slice | bytes 16805888 | tf_op jit(solution)/shard_map/jvp()/slice | solution.py:61
  351.7 45.0 %fusion.4 = f32[4103,512]{1,0:T(8,128)S(1)} fusion(f32[4103,512]{1,0:T(8,128)} %slice.452, f32[4103,512]{1,0:T(8,128)} %slice.451, f32[4103,512]{1,0:T(8,128)} %slice.450, f32[8192,512]{1,0:T(8,128)} %subtract_add_fusion.4), kind=kOutput, calls=%fused_computation.11 | convolution fusion | flops 38733369344 | bytes 36763648 | tf_op jit(solution)/shard_map/jvp(bmk,bkn->bmn)/dot_general | solution.py:45
  490.9 24.5 %fusion.28 = f32[2051,512]{1,0:T(8,128)S(1)} fusion(f32[2051,512]{1,0:T(8,128)} %slice.456, f32[2051,512]{1,0:T(8,128)} %slice.455, f32[2051,512]{1,0:T(8,128)} %slice.454, f32[8192,512]{1,0:T(8,128)} %subtract_add_fusion.4), kind=kOutput, calls=%fused_computation.59 | convolution fusion | flops 19361964032 | bytes 19978240 | tf_op jit(solution)/shard_map/jvp(bmk,bkn->bmn)/dot_general | solution.py:45
  836.9 22.6 %subtract_add_fusion.1 = f32[3,768,3072]{2,1,0:T(8,128)} fusion(bf16[3,768,3072]{2,1,0:T(8,128)(2,1)} %all-gather.14.cloned.1.call-done), kind=kLoop, calls=%fused_computation.3 | loop fusion | flops 28311552 | bytes 42467328 | tf_op jit(solution)/shard_map/jvp()/add | solution.py:37
  1266.1 32.9 %pad.271 = f32[4103,512]{1,0:T(8,128)} pad(f32[2051,512]{1,0:T(8,128)} %get-tuple-element.204, f32[]{:T(128)} %constant.65.clone.1), padding=2_0_1x0_0_0 | pad | bytes 12603396 | tf_op jit(solution)/shard_map/transpose(jvp())/pad | solution.py:61
  1298.9 32.6 %pad.272 = f32[4103,512]{1,0:T(8,128)} pad(f32[2051,512]{1,0:T(8,128)} %get-tuple-element.202, f32[]{:T(128)} %constant.65.clone.1), padding=1_1_1x0_0_0 | pad | bytes 12603396 | tf_op jit(solution)/shard_map/transpose(jvp())/pad | solution.py:61
  1331.6 32.6 %pad.273 = f32[4103,512]{1,0:T(8,128)} pad(f32[2051,512]{1,0:T(8,128)} %get-tuple-element.203, f32[]{:T(128)} %constant.65.clone.1), padding=0_2_1x0_0_0 | pad | bytes 12603396 | tf_op jit(solution)/shard_map/transpose(jvp())/pad | solution.py:61
  1364.2 136.0 %reduce-scatter.15.cloned.1.call-done = f32[96,3072]{1,0:T(8,128)} async-done(((f32[768,3072]{1,0:T(8,128)}), f32[96,3072]{1,0:T(8,128)}) %reduce-scatter.15.cloned.1.call-update) | async-done | bytes 1179664 | tf_op jit(solution)/shard_map/reduce_scatter | solution.py:326
  1556.5 26.4 %fusion.91 = f32[1536,512]{1,0:T(8,128)} fusion(f32[4103,512]{1,0:T(8,128)} %slice.452, f32[4103,512]{1,0:T(8,128)S(1)} %bitcast.1359, f32[4103,512]{1,0:T(8,128)S(1)} %bitcast.1357, bf16[1,4103,512]{2,1,0:T(8,128)(2,1)S(1)} %bitcast.1368), kind=kOutput, calls=%fused_computation.150 | convolution fusion | flops 38733369344 | bytes 32556032 | tf_op jit(solution)/shard_map/transpose(jvp(bmk,bkn->bmn))/dot_general | solution.py:45
  1596.4 25.8 %fusion.85 = f32[4103,1536]{1,0:T(8,128)} fusion(bf16[1,4103,512]{2,1,0:T(8,128)(2,1)} %fusion.88, f32[8192,512]{1,0:T(8,128)} %subtract_add_fusion.4), kind=kOutput, calls=%fused_computation.141 | convolution fusion | flops 38720765952 | bytes 32557056 | tf_op jit(solution)/shard_map/transpose(jvp(bmk,bkn->bmn))/dot_general | solution.py:45
  1640.1 65.6 %pad.277 = f32[8207,512]{1,0:T(8,128)} pad(f32[4103,512]{1,0:T(8,128)} %get-tuple-element.201, f32[]{:T(128)} %constant.65.clone.1), padding=2_0_1x0_0_0 | pad | bytes 25210884 | tf_op jit(solution)/shard_map/transpose(jvp())/pad | solution.py:61
  1705.6 64.6 %pad.278 = f32[8207,512]{1,0:T(8,128)} pad(f32[4103,512]{1,0:T(8,128)} %get-tuple-element.199, f32[]{:T(128)} %constant.65.clone.1), padding=1_1_1x0_0_0 | pad | bytes 25210884 | tf_op jit(solution)/shard_map/transpose(jvp())/pad | solution.py:61
  1770.2 64.4 %pad.279 = f32[8207,512]{1,0:T(8,128)} pad(f32[4103,512]{1,0:T(8,128)} %get-tuple-element.200, f32[]{:T(128)} %constant.65.clone.1), padding=0_2_1x0_0_0 | pad | bytes 25210884 | tf_op jit(solution)/shard_map/transpose(jvp())/pad | solution.py:61
  1834.6 34.4 %fusion.55 = bf16[1,8207,512]{2,1,0:T(8,128)(2,1)} fusion(f32[8207,512]{1,0:T(8,128)} %get-tuple-element.195, f32[8207,512]{1,0:T(8,128)} %pad.279, f32[8207,512]{1,0:T(8,128)} %pad.277, f32[8207,512]{1,0:T(8,128)} %pad.278, f32[8207,512]{1,0:T(8,128)} %copy-done, bf16[1,8207,512]{2,1,0:T(8,128)(2,1)} %copy-done.2), kind=kLoop, calls=%fused_computation.94 | loop fusion | flops 79837696 | bytes 100847616 | tf_op jit(solution)/shard_map/transpose(jvp())/convert_element_type | solution.py:33
  1901.0 43.9 %all-reduce.72 = (f32[]{:T(128)}, f32[]{:T(128)}, f32[12,512]{1,0:T(8,128)S(1)}, f32[10,768]{1,0:T(8,128)S(1)}) all-reduce(f32[]{:T(128)S(6)} %div.229, f32[]{:T(128)S(6)} %add.761, f32[12,512]{1,0:T(8,128)S(1)} %pad_add_fusion.9, f32[10,768]{1,0:T(8,128)S(1)} %add_add_fusion.5), channel_id=1, replica_groups=mesh['dp'=8,'narrow'=4] {'dp','narrow'}, use_global_device_ids=true, to_apply=%region_22.23 | all-reduce | flops 13826 | bytes 110608 | tf_op jit(solution)/shard_map/psum | solution.py:337
  1955.9 26.1 %all-reduce.79.cloned.1.call-done = f32[3,96,96]{2,1,0:T(8,128)} async-done(((f32[3,96,96]{2,1,0:T(8,128)}), f32[3,96,96]{2,1,0:T(8,128)}) %all-reduce.79.cloned.1.call-update) | async-done | bytes 110608 | tf_op jit(solution)/shard_map/psum | solution.py:264
  1989.7 28.9 %all-reduce.81.cloned.1.call-done = f32[3,96,96]{2,1,0:T(8,128)} async-done(((f32[3,96,96]{2,1,0:T(8,128)}), f32[3,96,96]{2,1,0:T(8,128)}) %all-reduce.81.cloned.1.call-update) | async-done | bytes 110608 | tf_op jit(solution)/shard_map/psum | solution.py:264
  2023.6 30.6 %all-reduce.83.cloned.1.call-done = f32[3,96,96]{2,1,0:T(8,128)} async-done(((f32[3,96,96]{2,1,0:T(8,128)}), f32[3,96,96]{2,1,0:T(8,128)}) %all-reduce.83.cloned.1.call-update) | async-done | bytes 110608 | tf_op jit(solution)/shard_map/psum | solution.py:264
  2059.6 30.0 %all-reduce.85.cloned.1.call-done = f32[3,96,96]{2,1,0:T(8,128)} async-done(((f32[3,96,96]{2,1,0:T(8,128)}), f32[3,96,96]{2,1,0:T(8,128)}) %all-reduce.85.cloned.1.call-update) | async-done | bytes 110608 | tf_op jit(solution)/shard_map/psum | solution.py:264
  2100.3 24.8 %all-reduce.87.cloned.1.call-done = f32[3,96,96]{2,1,0:T(8,128)} async-done(((f32[3,96,96]{2,1,0:T(8,128)}), f32[3,96,96]{2,1,0:T(8,128)}) %all-reduce.87.cloned.1.call-update) | async-done | bytes 110608 | tf_op jit(solution)/shard_map/psum | solution.py:264
  (945 shorter events, 1114.8 us)
Async XLA Ops:
  7.2 26.5 %all-gather.16.cloned.1.call-start = ((), (), s32[]{:S(2)}) async-start(), calls=%async_computation.10 | async-start | bytes 2211840 | tf_op jit(solution)/shard_map/all_gather | solution.py:296
  9.3 292.0 %all-gather.12.cloned.1.call-start = ((), (), s32[]{:S(2)}) async-start(), calls=%async_computation.8 | async-start | bytes 2211840 | tf_op jit(solution)/shard_map/all_gather | solution.py:295
  11.4 86.8 %copy-start.140 = (f32[12,512]{1,0:T(8,128)S(1)}, f32[12,512]{1,0:T(8,128)}, u32[]{:S(2)}) copy-start(f32[12,512]{1,0:T(8,128)} %param.24) | copy-start | bytes 73732
  11.4 290.0 %all-gather.10.cloned.1.call-start = ((), (), s32[]{:S(2)}) async-start(), calls=%async_computation.7 | async-start | bytes 3981312 | tf_op jit(solution)/shard_map/all_gather | solution.py:302
  22.3 314.9 %all-gather.8.cloned.1.call-start = ((), (), s32[]{:S(2)}) async-start(), calls=%async_computation.6 | async-start | bytes 8650752 | tf_op jit(solution)/shard_map/all_gather | solution.py:307
  23.1 744.1 %all-gather.18.cloned.1.call-start = ((), (), s32[]{:S(2)}) async-start(), calls=%async_computation.11 | async-start | bytes 15925248 | tf_op jit(solution)/shard_map/all_gather | solution.py:301
  33.7 803.2 %all-gather.14.cloned.1.call-start = ((), (), s32[]{:S(2)}) async-start(), calls=%async_computation.9 | async-start | bytes 15925248 | tf_op jit(solution)/shard_map/all_gather | solution.py:300
  301.3 1062.8 %reduce-scatter.11.cloned.1.call-start = ((), (), s32[]{:S(2)}) async-start(), calls=%async_computation.12 | async-start | bytes 10616832 | tf_op jit(solution)/shard_map/reduce_scatter | solution.py:326
  766.8 97.0 %copy-start.179 = (f32[128]{0:T(128)}, f32[128]{0:T(128)S(1)}, u32[]{:S(2)}) copy-start(f32[128]{0:T(128)S(1)} %broadcast_multiply_fusion.6) | copy-start | bytes 1540
  767.0 96.8 %copy-start.190 = (f32[128]{0:T(128)}, f32[128]{0:T(128)S(1)}, u32[]{:S(2)}) copy-start(f32[128]{0:T(128)S(1)} %fusion.431) | copy-start | bytes 1540
  767.2 96.7 %copy-start.90 = (bf16[128,768]{1,0:T(8,128)(2,1)}, bf16[128,768]{1,0:T(8,128)(2,1)S(1)}, u32[]{:S(2)}) copy-start(bf16[128,768]{1,0:T(8,128)(2,1)S(1)} %fusion.441) | copy-start | bytes 589828
  1003.7 360.5 %reduce-scatter.13.cloned.1.call-start = ((), (), s32[]{:S(2)}) async-start(), calls=%async_computation.13 | async-start | bytes 10616832 | tf_op jit(solution)/shard_map/reduce_scatter | solution.py:326
  1004.4 495.8 %reduce-scatter.15.cloned.1.call-start = ((), (), s32[]{:S(2)}) async-start(), calls=%async_computation.14 | async-start | bytes 10616832 | tf_op jit(solution)/shard_map/reduce_scatter | solution.py:326
  1005.2 869.8 %reduce-scatter.21.cloned.1.call-start = ((), (), s32[]{:S(2)}) async-start(), calls=%async_computation.22 | async-start | bytes 7962624
  1084.5 810.8 %reduce-scatter.17.cloned.1.call-start = ((), (), s32[]{:S(2)}) async-start(), calls=%async_computation.15 | async-start | bytes 4423680 | tf_op jit(solution)/shard_map/reduce_scatter | solution.py:331
  1504.4 394.1 %reduce-scatter.19.cloned.1.call-start = ((), (), s32[]{:S(2)}) async-start(), calls=%async_computation.16 | async-start | bytes 17301504 | tf_op jit(solution)/shard_map/reduce_scatter | solution.py:336
  1593.7 388.3 %all-reduce.79.cloned.1.call-start = ((), (), s32[]{:S(2)}) async-start(), calls=%async_computation.17 | async-start | bytes 294912 | tf_op jit(solution)/shard_map/psum | solution.py:264
  1874.9 73.3 %copy-start.130 = (f32[3,96,768]{2,1,0:T(8,128)S(1)}, f32[3,96,768]{2,1,0:T(8,128)}, u32[]{:S(2)}) copy-start(f32[3,96,768]{2,1,0:T(8,128)} %param.39) | copy-start | bytes 2654212
  1876.6 74.8 %copy-start.129 = (f32[96,548]{1,0:T(8,128)S(1)}, f32[96,548]{1,0:T(8,128)}, u32[]{:S(2)}) copy-start(f32[96,548]{1,0:T(8,128)} %param.26) | copy-start | bytes 631300
  1891.7 2.2 collective-permute-start
  1951.2 67.5 %all-reduce.81.cloned.1.call-start = ((), (), s32[]{:S(2)}) async-start(), calls=%async_computation.18 | async-start | bytes 294912 | tf_op jit(solution)/shard_map/psum | solution.py:264
  1987.0 67.2 %all-reduce.83.cloned.1.call-start = ((), (), s32[]{:S(2)}) async-start(), calls=%async_computation.19 | async-start | bytes 294912 | tf_op jit(solution)/shard_map/psum | solution.py:264
  2022.5 67.2 %all-reduce.85.cloned.1.call-start = ((), (), s32[]{:S(2)}) async-start(), calls=%async_computation.20 | async-start | bytes 294912 | tf_op jit(solution)/shard_map/psum | solution.py:264
  2058.0 67.1 %all-reduce.87.cloned.1.call-start = ((), (), s32[]{:S(2)}) async-start(), calls=%async_computation.21 | async-start | bytes 294912 | tf_op jit(solution)/shard_map/psum | solution.py:264
  (245 other events, 2643.4 us)
Sparse Core Ops, SparseCore 0:
  10.2 23.4 all-gather.15
  35.8 20.9 all-gather.11
  59.5 65.1 all-gather.9
  128.0 76.0 all-gather.7
  206.2 194.1 all-gather.17
  402.4 193.7 all-gather.13
  1003.8 164.3 reduce-scatter.10
  1171.8 162.3 reduce-scatter.12
  1337.8 162.3 reduce-scatter.14
  1503.7 128.0 reduce-scatter.20
  1634.6 39.4 reduce-scatter.16
  1676.3 182.9 reduce-scatter.18
  1951.3 30.6 all-reduce.78
  1987.1 31.5 all-reduce.80
  2022.6 31.5 all-reduce.82
  2058.1 31.5 all-reduce.84
  2093.6 31.4 all-reduce.86
where the time goes:
time: 2160 us; the launch traced here: 2140 us
  local copies, waits for them, and re-layouts  972 us (45%)
  matrix products  398 us (18%)
  other arithmetic  342 us (16%)
  waiting for transfers between devices  289 us (13%)
  blocking collectives  107 us (5%)
  between operations  26.8 us (1%)
    pad x16, local copies, waits for them, and re-layouts, strided_taps(): lax.slice_in_dim(values, offset, offset + stride * (rows_out - 1) + 1, st...  404 us
    dot_general x54, matrix products, bprod(): jnp.einsum('bmk,bkn->bmn', left_side, right_side, precision=HIGHEST)  376 us
    slice x26, local copies, waits for them, and re-layouts, strided_taps(): lax.slice_in_dim(values, offset, offset + stride * (rows_out - 1) + 1, st...  293 us
    psum x5, waiting for transfers between devices, narrow_total(): return lax.psum(gram_matrix, 'narrow')  140 us
    reduce_scatter x3, waiting for transfers between devices, per_device(): lax.psum_scatter(block_grad[matrix_index], 'dp', scatter_dimension=0, til...  136 us
    add x18, other arithmetic, low(): return values + lax.stop_gradient(rounded(values) - values)  93.9 us
    convert_element_type x43, other arithmetic, rounded(): values.astype(jnp.bfloat16)  91.3 us
    convert_element_type x13, other arithmetic, rounded(): lax.optimization_barrier(values.astype(jnp.bfloat16)).astype(jnp.float32)  72.2 us
  transfers between devices with their start and end apart: 18, of which 8 were waited for; matrix products, arithmetic and copies ran while one was open for 71% of the time, Pallas kernels for 0%

commit v1 on v0

v1 whole, which is shorter than its diff:
```python
import math

import jax
import jax.numpy as jnp
import numpy as np
from jax import lax
from jax.sharding import Mesh
from jax.sharding import PartitionSpec as P

D = 768
HEADS = 12
HEAD_DIM = 64
CH = 512
GROUPS = 16
WIDTH = D // GROUPS
POS_K = 19
REACH = POS_K // 2
SPAN = 10
TAIL = 16

EPS = 1e-05
VAR_FLOOR = 0.1
CLIP_LIMIT = 0.01
LR_ADAM = 0.03
LR_MUON = 2.0
DECAY = 0.5
WEIGHT_DECAY = 0.01
EMA_RATE = 0.5
KERNELS = (3, 3, 3, 3, 2, 2)
COEFF_A = 3.4445
COEFF_B = -4.775
COEFF_C = 2.0315
HIGHEST = lax.Precision.HIGHEST
F32 = jnp.float32
BF16 = jnp.bfloat16
ROOT_HALF = math.sqrt(0.5)
ROOT_TAU = 1.0 / math.sqrt(2.0 * math.pi)


def bf(values):
    return values.astype(BF16)


def low(values):
    return lax.optimization_barrier(values.astype(BF16)).astype(F32)


def dot(left, right, contract, batch=((), ())):
    return lax.dot_general(left, right, (contract, batch), preferred_element_type=F32)


def mm(left, right):
    return dot(left, right, ((1,), (0,)))


def mm_t(left, right):
    return dot(left, right, ((1,), (1,)))


def t_mm(left, right):
    return dot(left, right, ((0,), (0,)))


def gelu(values):
    return 0.5 * values * (1.0 + lax.erf(values * ROOT_HALF))


def gelu_slope(values):
    return 0.5 * (1.0 + lax.erf(values * ROOT_HALF)) + values * (
        ROOT_TAU * jnp.exp(-0.5 * values * values)
    )


def norm_fwd(values, gain, shift):
    center = values - jnp.mean(values, axis=-1, keepdims=True)
    scale = lax.rsqrt(jnp.mean(center * center, axis=-1, keepdims=True) + EPS)
    unit = center * scale
    return unit * gain + shift, (unit, scale)


def norm_bwd(kept, gain, grad):
    unit, scale = kept
    inner = grad * gain
    back = scale * (
        inner
        - jnp.mean(inner, axis=-1, keepdims=True)
        - unit * jnp.mean(inner * unit, axis=-1, keepdims=True)
    )
    return back, jnp.sum(grad * unit, axis=0), jnp.sum(grad, axis=0)


def wave_taps(wave, frames):
    padded = jnp.pad(bf(wave), (0, 320 * (frames + 2) - wave.shape[0])).reshape(frames + 2, 320)
    rows = jnp.concatenate([padded[: frames + 1], padded[1:, :5]], axis=1)
    pick = np.zeros((325, 640), np.float32)
    for phase in range(64):
        for tap in range(10):
            pick[5 * phase + tap, 10 * phase + tap] = 1.0
    taps = bf(mm(rows, jnp.asarray(pick, BF16)))
    taps = taps.reshape(frames + 1, 64, 10).transpose(1, 0, 2)
    return jnp.concatenate(
        [taps[:, :frames].reshape(64 * frames, 10), taps[:TAIL, frames]], axis=0
    )


def tap_rows(hidden, kernel, frames):
    tail = hidden[-TAIL:]
    main = hidden[:-TAIL].reshape(-1, 2, frames, CH)
    half = main.shape[0]
    even, odd = main[:, 0], main[:, 1]
    pieces = [even.reshape(half * frames, CH), odd.reshape(half * frames, CH)]
    pad = jnp.zeros((TAIL // 2, CH), hidden.dtype)
    ends = [jnp.concatenate([tail[0::2], pad]), jnp.concatenate([tail[1::2], pad])]
    if kernel == 3:
        wrap = jnp.concatenate([even[0, 1:], tail[:1]], axis=0)
        pieces.append(jnp.concatenate([even[1:], wrap[None]], axis=0).reshape(half * frames, CH))
        ends.append(jnp.concatenate([tail[2::2], pad, pad[:1]]))
    return jnp.concatenate(
        [jnp.concatenate(pieces, axis=1), jnp.concatenate(ends, axis=1)], axis=0
    )


def tap_rows_back(grad, kernel, frames):
    main, tail = grad[:-TAIL], grad[-TAIL:]
    half = main.shape[0] // frames
    even = main[:, :CH].reshape(half, frames, CH)
    odd = main[:, CH : 2 * CH].reshape(half, frames, CH)
    tail_even = tail[: TAIL // 2, :CH]
    tail_odd = tail[: TAIL // 2, CH : 2 * CH]
    if kernel == 3:
        next_even = main[:, 2 * CH :].reshape(half, frames, CH)
        wrap = next_even[-1]
        first = jnp.concatenate([jnp.zeros((1, CH), F32), wrap[:-1]], axis=0)
        even = even + jnp.concatenate([first[None], next_even[:-1]], axis=0)
        tail_even = tail_even + jnp.concatenate(
            [wrap[-1:], tail[: TAIL // 2 - 1, 2 * CH :]], axis=0
        )
    main = jnp.stack([even, odd], axis=1).reshape(2 * half * frames, CH)
    tail = jnp.stack([tail_even, tail_odd], axis=1).reshape(TAIL, CH)
    return jnp.concatenate([main, tail], axis=0)


def encode_fwd(small, stack, taps, frames):
    first = mm(taps, bf(small[:10]))
    hidden = bf(gelu(first))
    kept = []
    offset = 0
    for kernel in KERNELS:
        rows = tap_rows(hidden, kernel, frames)
        values = mm(rows, stack[offset : offset + kernel * CH])
        kept.append((rows, values))
        offset += kernel * CH
        activated = gelu(values)
        hidden = bf(activated)
    encoded = activated[:frames]
    normed, norm_kept = norm_fwd(encoded, small[10], small[11])
    return bf(normed), (first, kept, norm_kept)


def encode_bwd(saved, small, stack, taps, frames, grad):
    first, kept, norm_kept = saved
    grad, gain_grad, shift_grad = norm_bwd(norm_kept, small[10], grad)
    grad = jnp.concatenate([grad, jnp.zeros((TAIL, CH), F32)], axis=0)
    offset = stack.shape[0]
    pieces = []
    for kernel, (rows, values) in zip(KERNELS[::-1], kept[::-1]):
        offset -= kernel * CH
        product_grad = bf(grad * gelu_slope(values))
        pieces.append(t_mm(rows, product_grad))
        grad = tap_rows_back(
            mm_t(product_grad, stack[offset : offset + kernel * CH]), kernel, frames
        )
    product_grad = bf(grad * gelu_slope(first))
    tap_grad = t_mm(taps, product_grad)
    small_grad = jnp.concatenate([tap_grad, gain_grad[None], shift_grad[None]], axis=0)
    return small_grad, jnp.concatenate(pieces[::-1], axis=0)


def neighbours(segment):
    frames = segment.shape[0]
    padded = jnp.pad(segment, (REACH, REACH), constant_values=-1)
    return jnp.stack([padded[offset : offset + frames] == segment for offset in range(POS_K)], 0)


def masked_of(starts):
    frames = starts.shape[0]
    padded = jnp.pad(starts, (SPAN - 1, 0))
    return (
        jnp.max(jnp.stack([padded[offset : offset + frames] for offset in range(SPAN)], 0), axis=0)
        > 0
    )


def group_taps(values, nearby):
    frames = values.shape[0]
    padded = jnp.pad(values, ((REACH, REACH), (0, 0)))
    rows = jnp.stack([padded[offset : offset + frames] for offset in range(POS_K)], 0)
    rows = jnp.where(nearby[:, :, None], rows, jnp.zeros((), BF16))
    return (
        rows.reshape(POS_K, frames, GROUPS, WIDTH)
        .transpose(2, 1, 0, 3)
        .reshape(GROUPS, frames, POS_K * WIDTH)
    )


def batch_mm(left, right):
    return dot(left, right, ((2,), (1,)), ((0,), (0,)))


def batch_mm_t(left, right):
    return dot(left, right, ((2,), (2,)), ((0,), (0,)))


def batch_t_mm(left, right):
    return dot(left, right, ((1,), (1,)), ((0,), (0,)))


def block_fwd(values, kernel, weights, vectors, nearby, attend):
    frames = values.shape[0]
    taps = group_taps(bf(values), nearby)
    mixed = batch_mm(taps, kernel).transpose(1, 0, 2).reshape(frames, D) + vectors[7]
    hidden, norm_one = norm_fwd(values + gelu(mixed), vectors[0], vectors[1])
    hidden_low = bf(hidden)
    triple = bf(mm(hidden_low, weights[0][:, : 3 * D]))
    heads = triple.reshape(frames, 3, HEADS, HEAD_DIM).transpose(1, 2, 0, 3)
    scores = batch_mm_t(heads[0], heads[1]) * (1.0 / math.sqrt(HEAD_DIM))
    scores = jnp.where(attend[None], scores, -1e30)
    chances = jax.nn.softmax(scores, axis=-1)
    chances_low = bf(chances)
    outs = bf(batch_mm(chances_low, heads[2]).transpose(1, 0, 2).reshape(frames, D))
    second, norm_two = norm_fwd(
        hidden + mm(outs, weights[0][:, 3 * D :]), vectors[2], vectors[3]
    )
    second_low = bf(second)
    wide = mm(second_low, weights[1])
    inner = bf(gelu(wide))
    result, norm_three = norm_fwd(second + mm_t(inner, weights[2]), vectors[4], vectors[5])
    return result, (
        taps,
        mixed,
        norm_one,
        hidden_low,
        heads,
        chances,
        chances_low,
        outs,
        norm_two,
        second_low,
        wide,
        inner,
        norm_three,
    )


def block_bwd(saved, kernel_back, weights, vectors, nearby, grad):
    (
        taps,
        mixed,
        norm_one,
        hidden_low,
        heads,
        chances,
        chances_low,
        outs,
        norm_two,
        second_low,
        wide,
        inner,
        norm_three,
    ) = saved
    frames = grad.shape[0]
    grad, gain_three, shift_three = norm_bwd(norm_three, vectors[4], grad)
    down = bf(grad)
    out_grad = t_mm(down, inner)
    wide_grad = bf(mm(down, weights[2]) * gelu_slope(wide))
    in_grad = t_mm(second_low, wide_grad)
    grad = grad + mm_t(wide_grad, weights[1])
    grad, gain_two, shift_two = norm_bwd(norm_two, vectors[2], grad)
    down = bf(grad)
    mix_grad = t_mm(outs, down)
    outs_grad = bf(mm_t(down, weights[0][:, 3 * D :]))
    outs_grad = outs_grad.reshape(frames, HEADS, HEAD_DIM).transpose(1, 0, 2)
    chance_grad = batch_mm_t(outs_grad, heads[2])
    value_grad = batch_t_mm(chances_low, outs_grad)
    score_grad = chances * (
        chance_grad - jnp.sum(chance_grad * chances, axis=-1, keepdims=True)
    )
    score_grad = bf(score_grad * (1.0 / math.sqrt(HEAD_DIM)))
    query_grad = batch_mm(score_grad, heads[1])
    key_grad = batch_t_mm(score_grad, heads[0])
    triple_grad = bf(
        jnp.stack([query_grad, key_grad, value_grad], 0)
        .transpose(2, 0, 1, 3)
        .reshape(frames, 3 * D)
    )
    triple_weight_grad = t_mm(hidden_low, triple_grad)
    grad = grad + mm_t(triple_grad, weights[0][:, : 3 * D])
    grad, gain_one, shift_one = norm_bwd(norm_one, vectors[0], grad)
    mixed_grad = grad * gelu_slope(mixed)
    bias_grad = jnp.sum(mixed_grad, axis=0)
    mixed_low = bf(mixed_grad)
    kernel_grad = batch_t_mm(
        taps, mixed_low.reshape(frames, GROUPS, WIDTH).transpose(1, 0, 2)
    )
    back_taps = group_taps(mixed_low, nearby)
    grad = grad + batch_mm(back_taps, kernel_back).transpose(1, 0, 2).reshape(frames, D)
    block_grad = jnp.stack(
        [jnp.concatenate([triple_weight_grad, mix_grad], axis=1), in_grad, out_grad], 0
    )
    kernel_grad = (
        kernel_grad.reshape(GROUPS, POS_K, WIDTH, WIDTH)
        .transpose(0, 2, 1, 3)
        .reshape(D, POS_K * WIDTH)
    )
    vector_grad = (gain_one, shift_one, gain_two, shift_two, gain_three, shift_three, bias_grad)
    return grad, block_grad, kernel_grad, vector_grad


def clip_normal(output, attend):
    member = attend.astype(F32)
    clip_size = jnp.sum(member, axis=1, keepdims=True)
    average = jnp.dot(member, output, precision=HIGHEST) / clip_size
    center = output - average
    spread = jnp.dot(member, center * center, precision=HIGHEST) / clip_size
    return center * lax.rsqrt(jnp.maximum(spread, VAR_FLOOR))


def adamw(weight, grad, first, second, power):
    first = DECAY * first + (1.0 - DECAY) * grad
    second = DECAY * second + (1.0 - DECAY) * grad * grad
    unbias = 1.0 - power
    step_size = first / unbias / (jnp.sqrt(second / unbias) + 1e-08)
    return (weight - LR_ADAM * (step_size + WEIGHT_DECAY * weight), first, second)


def exact(left, right):
    return jnp.einsum("brs,bst->brt", left, right, precision=HIGHEST)


def orthogonal(blocks, gram_total):
    gram = gram_total(jnp.einsum("brc,bsc->brs", blocks, blocks, precision=HIGHEST))
    scales = 1.0 / (jnp.sqrt(jnp.trace(gram, axis1=1, axis2=2)) + 1e-07)
    gram = gram * (scales * scales)[:, None, None]
    eye = jnp.eye(gram.shape[1], dtype=F32)[None]
    whole = None
    for iteration in range(5):
        square = exact(gram, gram)
        step = COEFF_A * eye + COEFF_B * gram + COEFF_C * square
        whole = step if whole is None else exact(step, whole)
        if iteration < 4:
            gram = exact(exact(step, gram), step)
            gram = 0.5 * (gram + gram.transpose(0, 2, 1))
    return exact(whole * scales[:, None, None], blocks)


def per_device(
    wave,
    clip_ids,
    span_starts,
    step_count,
    conv_small,
    conv_stack,
    side,
    vectors,
    block,
    teacher_block,
    teacher_vectors,
    small_mean,
    small_square,
    stack_mean,
    stack_square,
    side_mean,
    side_square,
    vector_mean,
    vector_square,
    block_momentum,
    n_dp,
    n_narrow,
):
    everyone = ("dp", "narrow")
    frames = clip_ids.shape[0]
    rows_here, cols_here = block.shape[1:]
    side_rows, side_cols = side.shape
    stack = lax.all_gather(bf(conv_stack), everyone, axis=0, tiled=True)
    masked = masked_of(span_starts)
    total = jnp.maximum(lax.psum(jnp.sum(masked.astype(F32)), everyone), 1.0)
    send = jnp.concatenate(
        [
            bf(block).reshape(3 * rows_here, cols_here),
            bf(teacher_block).reshape(3 * rows_here, cols_here),
            jnp.pad(bf(side), ((0, 0), (0, cols_here - side_cols))),
        ],
        axis=0,
    )
    whole = lax.all_gather(send, everyone, axis=0, tiled=False)
    whole = whole.reshape(n_dp, n_narrow, 7, rows_here, cols_here)
    weights = whole[:, :, :6].transpose(2, 0, 3, 1, 4).reshape(6, D, n_narrow * cols_here)
    whole_side = (
        whole[:, :, 6, :, :side_cols]
        .transpose(0, 2, 1, 3)
        .reshape(n_dp * side_rows, n_narrow * side_cols)
    )
    project = whole_side[:, :CH]
    kernel = whole_side[:, CH : CH + POS_K * WIDTH].reshape(GROUPS, WIDTH, POS_K, WIDTH)
    head = whole_side[:, CH + POS_K * WIDTH :]
    kernel_fwd = kernel.transpose(0, 2, 1, 3).reshape(GROUPS, POS_K * WIDTH, WIDTH)
    kernel_back = kernel[:, :, ::-1].transpose(0, 2, 3, 1).reshape(GROUPS, POS_K * WIDTH, WIDTH)

    nearby = neighbours(clip_ids)
    attend = clip_ids[:, None] == clip_ids[None, :]
    small_low = low(conv_small)
    vector_low = low(vectors)
    taps = wave_taps(wave, frames)
    normed, encode_saved = encode_fwd(small_low, stack, taps, frames)
    feats = mm_t(normed, project) + vector_low[6]
    teacher_out, unused = block_fwd(
        feats, kernel_fwd, weights[3:], low(teacher_vectors), nearby, attend
    )
    target = clip_normal(teacher_out, attend)
    chosen = masked[:, None]
    values = jnp.where(chosen, vector_low[9], feats)
    student_out, block_saved = block_fwd(
        values, kernel_fwd, weights[:3], vector_low, nearby, attend
    )
    student_low = bf(student_out)
    error = jnp.where(chosen, mm(student_low, head) + vector_low[8] - target, 0.0)
    weight = 1.0 / (total * math.sqrt(D))
    loss_part = jnp.sum(error * error) * weight

    predict_grad = error * (2.0 * weight)
    head_bias_grad = jnp.sum(predict_grad, axis=0)
    predict_low = bf(predict_grad)
    head_grad = t_mm(student_low, predict_low)
    grad, block_grad, kernel_grad, vector_parts = block_bwd(
        block_saved, kernel_back, weights[:3], vector_low, nearby, mm_t(predict_low, head)
    )
    mask_grad = jnp.sum(jnp.where(chosen, grad, 0.0), axis=0)
    feat_grad = jnp.where(chosen, 0.0, grad)
    project_bias_grad = jnp.sum(feat_grad, axis=0)
    feat_low = bf(feat_grad)
    project_grad = t_mm(feat_low, normed)
    vector_grad = jnp.stack(
        vector_parts[:6] + (project_bias_grad, vector_parts[6], head_bias_grad, mask_grad), 0
    )
    side_grad = jnp.concatenate([project_grad, kernel_grad, head_grad], axis=1)

    block_send = block_grad.reshape(3, n_dp, rows_here, n_narrow, cols_here).transpose(
        1, 3, 0, 2, 4
    )
    block_piece = lax.psum_scatter(
        block_send.reshape(n_dp * n_narrow * 3 * rows_here, cols_here),
        everyone,
        scatter_dimension=0,
        tiled=True,
    ).reshape(3, rows_here, cols_here)
    side_send = side_grad.reshape(n_dp, side_rows, n_narrow, side_cols).transpose(0, 2, 1, 3)
    side_piece = lax.psum_scatter(
        side_send.reshape(n_dp * n_narrow * side_rows, side_cols),
        everyone,
        scatter_dimension=0,
        tiled=True,
    )
    small_grad, stack_grad = encode_bwd(
        encode_saved, small_low, stack, taps, frames, mm(feat_low, project)
    )
    stack_piece = lax.psum_scatter(stack_grad, everyone, scatter_dimension=0, tiled=True)
    small_total, vector_total, loss_value = lax.psum(
        (small_grad, vector_grad, loss_part), everyone
    )
    shard_squares = (
        jnp.sum(block_piece * block_piece)
        + jnp.sum(side_piece * side_piece)
        + jnp.sum(stack_piece * stack_piece)
    )
    grad_norm = jnp.sqrt(
        lax.psum(shard_squares, everyone)
        + jnp.sum(small_total * small_total)
        + jnp.sum(vector_total * vector_total)
    )
    factor = jnp.minimum(1.0, CLIP_LIMIT / (grad_norm + 1e-06))
    power = jnp.power(DECAY, step_count[0].astype(F32))
    small_next = adamw(conv_small, factor * small_total, small_mean, small_square, power)
    stack_next = adamw(conv_stack, factor * stack_piece, stack_mean, stack_square, power)
    side_next = adamw(side, factor * side_piece, side_mean, side_square, power)
    vector_next = adamw(vectors, factor * vector_total, vector_mean, vector_square, power)
    momentum = DECAY * block_momentum + factor * block_piece
    ortho = orthogonal(momentum, lambda gram: lax.psum(gram, "narrow"))
    block_next = block * (1.0 - LR_MUON * WEIGHT_DECAY) - LR_MUON * ortho
    teacher_next = EMA_RATE * teacher_block + (1.0 - EMA_RATE) * block_next
    teacher_vec_next = EMA_RATE * teacher_vectors + (1.0 - EMA_RATE) * vector_next[0]
    return (
        (loss_value, grad_norm)
        + small_next
        + stack_next
        + side_next
        + vector_next
        + (block_next, momentum, teacher_next, teacher_vec_next, bf(block_next))
    )


def solution(mesh):
    n_dp, n_narrow = mesh.shape["dp"], mesh.shape["narrow"]

    def step(*arguments):
        return per_device(*arguments, n_dp, n_narrow)

    rows = P(("dp", "narrow"), None)
    flat = P(("dp", "narrow"))
    grid = P("dp", "narrow")
    cube = P(None, "dp", "narrow")
    one = P()
    in_specs = (
        (flat, flat, flat, one, one, rows, grid, one, cube, cube, one, one, one)
        + (rows, rows, grid, grid, one, one, cube)
    )
    out_specs = (
        (one, one, one, one, one, rows, rows, rows, grid, grid, grid, one, one, one)
        + (cube, cube, cube, one, cube)
    )
    return jax.shard_map(
        step, mesh=mesh, in_specs=in_specs, out_specs=out_specs, check_vma=False
    )
```

time: 2160 us -> 1350 us (0.62)
  local copies, waits for them, and re-layouts: 972 us -> 407 us
  other arithmetic: 342 us -> 142 us
  matrix products: 398 us -> 208 us
  waiting for transfers between devices: 289 us -> 473 us
  blocking collectives: 107 us -> 82.2 us
    pad x16 -> x1, local copies, waits for them, and re-layouts: 404 us -> 0.01 us  [wave_taps(): jnp.pad(bf(wave), (0, 320 * (frames + 2) - wave.shape[0]))]
    reduce_scatter x5 -> x3, waiting for transfers between devices: 136 us -> 335 us  [the longest x1 271 us: per_device(): lax.psum_scatter(block_send.reshape(n_dp * n_narrow * 3 * rows_here, cols...]
    slice x71 -> x128, local copies, waits for them, and re-layouts: 363 us -> 175 us  [the longest x57 70.8 us: group_taps(): padded[offset:offset + frames]]
    dot_general x66 -> x74, matrix products: 390 us -> 205 us  [the longest x54 195 us: dot(): lax.dot_general(left, right, (contract, batch), preferred_element_type=F32)]
    convert_element_type x60 -> x13, other arithmetic: 169 us -> 14.6 us  [the longest x8 14.6 us: bf(): return values.astype(BF16)]
    psum x5 -> x1, waiting for transfers between devices: 140 us -> 24.6 us  [per_device(): ortho = orthogonal(momentum, lambda gram: lax.psum(gram, 'narrow'))]
    all_gather x6 -> x2, waiting for transfers between devices: 10.6 us -> 112 us  [the longest x1 94.7 us: per_device(): whole = lax.all_gather(send, everyone, axis=0, tiled=False)]
    add x26 -> x6, other arithmetic: 101 us -> 14.6 us  [the longest x4 11.6 us: tap_rows_back(): even = even + jnp.concatenate([first[None], next_even[:-1]], axis=0)]
  transfers between devices with their start and end apart: 18 -> 6, of which waited for: 8 -> 5; matrix products, arithmetic and copies ran while one was open for 71% -> 27% of each run, Pallas kernels for 0% -> 0%
where the time goes in v1:
time: 1350 us; the launch traced here: 1340 us
  waiting for transfers between devices  473 us (35%)
  local copies, waits for them, and re-layouts  407 us (30%)
  matrix products  208 us (15%)
  other arithmetic  142 us (11%)
  blocking collectives  82.2 us (6%)
  between operations  26.2 us (2%)
    reduce_scatter x1, waiting for transfers between devices, per_device(): lax.psum_scatter(block_send.reshape(n_dp * n_narrow * 3 * rows_here, cols...  271 us
    dot_general x54, matrix products, dot(): lax.dot_general(left, right, (contract, batch), preferred_element_type=F32)  195 us
    all_gather x1, waiting for transfers between devices, per_device(): whole = lax.all_gather(send, everyone, axis=0, tiled=False)  94.7 us
    slice x57, local copies, waits for them, and re-layouts, group_taps(): padded[offset:offset + frames]  70.8 us
    reduce_scatter x1, waiting for transfers between devices, per_device(): lax.psum_scatter(stack_grad, everyone, scatter_dimension=0, tiled=True)  64.3 us
    another operation x6, local copies, waits for them, and re-layouts, block_bwd(): jnp.stack([jnp.concatenate([triple_weight_grad, mix_grad], axis=1), in_gr...  61.4 us
    unnamed x542, local copies, waits for them, and re-layouts  55.1 us
    concatenate x2, other arithmetic, tap_rows(): jnp.concatenate([jnp.concatenate(pieces, axis=1), jnp.concatenate(ends, a...  41.7 us
  transfers between devices with their start and end apart: 6, of which 5 were waited for; matrix products, arithmetic and copies ran while one was open for 27% of the time, Pallas kernels for 0%

profile of v1, /device:TPU:0, one launch (start us, length us, event | category | flops | bytes accessed | tf_op | source)
XLA Modules:
  0.0 1338.5 jit_solution(11029722890989353373)
XLA Ops:
  45.5 28.3 %fusion.25 = bf16[4112,1536]{1,0:T(8,128)(2,1)} fusion(bf16[8,512]{1,0:T(8,128)(2,1)S(1)} %slice.843, bf16[8,512]{1,0:T(8,128)(2,1)S(1)} %slice.842, bf16[1,512]{1,0:T(2,128)(2,1)S(1)} %broadcast.421, bf16[8,512]{1,0:T(8,128)(2,1)S(1)} %broadcast.420, bf16[7,512]{1,0:T(8,128)(2,1)S(1)} %slice.844, bf16[4096,512]{1,0:T(8,128)(2,1)S(1)} %bitcast.537, ...), kind=kLoop, calls=%fused_computation.39 | loop fusion | flops 170532864 | bytes 25247744 | tf_op jit(solution)/shard_map/concatenate | solution.py:118
  73.7 17.8 %all-gather.4.cloned.1.call-done = bf16[8192,512]{1,0:T(8,128)(2,1)} async-done(((bf16[256,512]{1,0:T(8,128)(2,1)}), bf16[8192,512]{1,0:T(8,128)(2,1)}) %all-gather.4.cloned.1.call-update) | async-done | bytes 8388624 | tf_op jit(solution)/shard_map/all_gather | solution.py:384
  91.5 12.9 multiply_convert_fusion.1
  111.7 13.4 %fusion.43 = bf16[2064,1536]{1,0:T(8,128)(2,1)S(1)} fusion(bf16[8,512]{1,0:T(8,128)(2,1)S(1)} %slice.855, bf16[8,512]{1,0:T(8,128)(2,1)S(1)} %slice.854, bf16[1,512]{1,0:T(2,128)(2,1)S(1)} %broadcast.421, bf16[8,512]{1,0:T(8,128)(2,1)S(1)} %broadcast.420, bf16[7,512]{1,0:T(8,128)(2,1)S(1)} %slice.856, bf16[2048,512]{1,0:T(8,128)(2,1)S(1)} %bitcast.554, ...), kind=kLoop, calls=%fused_computation.67 | loop fusion | flops 85598208 | bytes 12664832 | tf_op jit(solution)/shard_map/concatenate | solution.py:118
  151.0 40.6 %psum.42 = f32[]{:T(128)} all-reduce(f32[]{:T(128)} %get-tuple-element.78), channel_id=1, replica_groups=mesh['dp'=8,'narrow'=4] {'dp','narrow'}, use_global_device_ids=true, to_apply=%region_21.22 | all-reduce | flops 1 | bytes 8 | tf_op jit(solution)/shard_map/psum | solution.py:386
  192.3 94.7 %all-gather.6.cloned.1.call-done = bf16[21504,768]{1,0:T(8,128)(2,1)} async-done(((bf16[672,768]{1,0:T(8,128)(2,1)}), bf16[21504,768]{1,0:T(8,128)(2,1)}) %all-gather.6.cloned.1.call-update) | async-done | bytes 33030160 | tf_op jit(solution)/shard_map/all_gather | solution.py:395
  289.5 19.4 %slice_bitcast_fusion = bf16[6,8,96,4,768]{4,2,0,3,1:T(8,128)(2,1)} fusion(bf16[8,4,7,96,768]{4,3,2,1,0:T(8,128)(2,1)} %bitcast.510), kind=kLoop, calls=%fused_computation.5 | loop fusion | bytes 56623104 | tf_op jit(solution)/shard_map/transpose | solution.py:397
  331.7 21.1 %fusion.345 = (bf16[1,8,96,4,768]{4,2,0,3,1:T(8,128)(2,1)}, bf16[1,8,96,4,768]{4,2,0,3,1:T(8,128)(2,1)}, bf16[1,8,96,4,768]{4,2,0,3,1:T(8,128)(2,1)}, bf16[1,8,9...) fusion(bf16[6,8,96,4,768]{4,2,0,3,1:T(8,128)(2,1)} %slice_bitcast_fusion), kind=kLoop, calls=%fused_computation.735 | loop fusion | bytes 56623104 | tf_op jit(solution)/shard_map/slice | solution.py:235
  609.6 10.9 copy.289
  639.5 10.3 reshape.760
  693.4 10.8 convolution_dynamic-update-slice_fusion.2
  739.0 12.6 stack.452
  751.6 9.3 copy.263
  765.8 12.5 stack.454
  792.5 12.5 stack.453
  810.5 17.5 %pad_maximum_fusion = f32[3,8,96,4,768]{4,2,0,3,1:T(8,128)} fusion(f32[1,8,96,4,768]{4,2,0,3,1:T(8,128)} %copy.265, f32[1,8,96,4,768]{4,2,0,3,1:T(8,128)S(1)} %copy.264, f32[1,8,96,4,768]{4,2,0,3,1:T(8,128)} %copy.263), kind=kLoop, calls=%fused_computation.6 | loop fusion | flops 14155776 | bytes 56623104 | tf_op jit(solution)/shard_map/stack | solution.py:307
  829.3 14.9 %fusion.95 = f32[4112,1536]{1,0:T(8,128)} fusion(bf16[4112,512]{1,0:T(8,128)(2,1)} %fusion.31, bf16[8192,512]{1,0:T(8,128)(2,1)} %all-gather.4.cloned.1.call-done), kind=kOutput, calls=%fused_computation.156 | convolution fusion | flops 6467616768 | bytes 31047680 | tf_op jit(solution)/shard_map/dot_general | solution.py:49
  854.7 10.4 fusion.346
  869.7 10.1 pad_maximum_fusion.1
  879.8 16.8 %fusion.32 = f32[10,512]{1,0:T(8,128)S(1)} fusion(f32[8208,512]{1,0:T(8,128)} %get-tuple-element.213, f32[16,512]{1,0:T(8,128)S(1)} %reshape.777, f32[8192,512]{1,0:T(8,128)} %bitcast.533, bf16[16,10]{0,1:T(8,128)(2,1)S(1)} %bitcast.686, bf16[8192,10]{0,1:T(8,128)(2,1)S(1)} %bitcast.591), kind=kOutput, calls=%fused_computation.52 | convolution fusion | flops 130605696 | bytes 33804608 | tf_op jit(solution)/shard_map/dot_general | solution.py:49
  898.3 64.3 %reduce-scatter.8.cloned.1.call-done = f32[256,512]{1,0:T(8,128)} async-done(((f32[8192,512]{1,0:T(8,128)}), f32[256,512]{1,0:T(8,128)}) %reduce-scatter.8.cloned.1.call-update) | async-done | bytes 524304 | tf_op jit(solution)/shard_map/reduce_scatter | solution.py:466
  964.4 271.1 %reduce-scatter.4.cloned.1.call-done = f32[288,768]{1,0:T(8,128)} async-done(((f32[9216,768]{1,0:T(8,128)}), f32[288,768]{1,0:T(8,128)}) %reduce-scatter.4.cloned.1.call-update) | async-done | bytes 884752 | tf_op jit(solution)/shard_map/reduce_scatter | solution.py:450
  1239.5 41.6 %all-reduce.24 = (f32[]{:T(128)}, f32[]{:T(128)}, f32[12,512]{1,0:T(8,128)S(1)}, f32[10,768]{1,0:T(8,128)S(1)}) all-reduce(f32[]{:T(128)S(6)} %mul.951, f32[]{:T(128)S(6)} %add.618, f32[12,512]{1,0:T(8,128)S(1)} %pad_maximum_fusion.23, f32[10,768]{1,0:T(8,128)S(1)} %stack.510), channel_id=1, replica_groups=mesh['dp'=8,'narrow'=4] {'dp','narrow'}, use_global_device_ids=true, to_apply=%region_22.23 | all-reduce | flops 13826 | bytes 110608 | tf_op jit(solution)/shard_map/psum | solution.py:467
  1294.6 24.6 %all-reduce.27.cloned.1.call-done = f32[3,96,96]{2,1,0:T(8,128)} async-done(((f32[3,96,96]{2,1,0:T(8,128)}), f32[3,96,96]{2,1,0:T(8,128)}) %all-reduce.27.cloned.1.call-update) | async-done | bytes 110608 | tf_op jit(solution)/shard_map/psum | solution.py:487
  (940 shorter events, 513.8 us)
Async XLA Ops:
  7.2 84.3 %all-gather.4.cloned.1.call-start = ((), (), s32[]{:S(2)}) async-start(), calls=%async_computation.3 | async-start | bytes 8650752 | tf_op jit(solution)/shard_map/all_gather | solution.py:384
  9.1 277.9 %all-gather.6.cloned.1.call-start = ((), (), s32[]{:S(2)}) async-start(), calls=%async_computation.8 | async-start | bytes 34062336 | tf_op jit(solution)/shard_map/all_gather | solution.py:395
  13.7 882.9 %reduce-scatter.6.cloned.1.call-start = ((), (), s32[]{:S(2)}) async-start(), calls=%async_computation.5 | async-start | bytes 8110080 | tf_op jit(solution)/shard_map/reduce_scatter | solution.py:457
  41.8 277.2 %copy-start.166 = (f32[768]{0:T(1024)}, f32[768]{0:T(1024)S(1)}, u32[]{:S(2)}) copy-start(f32[768]{0:T(1024)S(1)} %get-tuple-element.245) | copy-start | bytes 9220
  44.7 274.2 %copy-start.192 = (f32[1,512]{1,0:T(1,128)}, f32[1,512]{1,0:T(1,128)S(1)}, u32[]{:S(2)}) copy-start(f32[1,512]{1,0:T(1,128)S(1)} %get-tuple-element.191) | copy-start | bytes 6148
  45.5 94.8 %copy-start.155 = (bf16[1,512]{1,0:T(2,128)(2,1)}, bf16[1,512]{1,0:T(2,128)(2,1)S(1)}, u32[]{:S(2)}) copy-start(bf16[1,512]{1,0:T(2,128)(2,1)S(1)} %broadcast.421) | copy-start | bytes 3076
  45.5 94.8 %copy-start.136 = (bf16[8,512]{1,0:T(8,128)(2,1)}, bf16[8,512]{1,0:T(8,128)(2,1)S(1)}, u32[]{:S(2)}) copy-start(bf16[8,512]{1,0:T(8,128)(2,1)S(1)} %broadcast.420) | copy-start | bytes 24580
  147.0 142.5 %copy-start.188 = (bf16[8,512]{1,0:T(8,128)(2,1)}, bf16[8,512]{1,0:T(8,128)(2,1)S(1)}, u32[]{:S(2)}) copy-start(bf16[8,512]{1,0:T(8,128)(2,1)S(1)} %slice.894) | copy-start | bytes 24580
  147.0 142.5 %copy-start.190 = (bf16[8,512]{1,0:T(8,128)(2,1)}, bf16[8,512]{1,0:T(8,128)(2,1)S(1)}, u32[]{:S(2)}) copy-start(bf16[8,512]{1,0:T(8,128)(2,1)S(1)} %slice.893) | copy-start | bytes 24580
  151.0 168.0 %copy-start.194 = (pred[128]{0:T(512)(128)(4,1)}, pred[128]{0:T(512)(128)(4,1)S(1)}, u32[]{:S(2)}) copy-start(pred[128]{0:T(512)(128)(4,1)S(1)} %get-tuple-element.79) | copy-start | bytes 388
  400.3 27.6 %copy-start.61 = (bf16[128,768]{1,0:T(8,128)(2,1)S(1)}, bf16[128,768]{1,0:T(8,128)(2,1)}, u32[]{:S(2)}) copy-start(bf16[128,768]{1,0:T(8,128)(2,1)} %get-tuple-element.183) | copy-start | bytes 589828
  401.1 27.6 %copy-start.60 = (bf16[128,768]{1,0:T(8,128)(2,1)S(1)}, bf16[128,768]{1,0:T(8,128)(2,1)}, u32[]{:S(2)}) copy-start(bf16[128,768]{1,0:T(8,128)(2,1)} %get-tuple-element.184) | copy-start | bytes 589828
  401.9 27.6 %copy-start.59 = (bf16[128,768]{1,0:T(8,128)(2,1)S(1)}, bf16[128,768]{1,0:T(8,128)(2,1)}, u32[]{:S(2)}) copy-start(bf16[128,768]{1,0:T(8,128)(2,1)} %get-tuple-element.185) | copy-start | bytes 589828
  402.7 27.6 %copy-start.58 = (bf16[128,768]{1,0:T(8,128)(2,1)S(1)}, bf16[128,768]{1,0:T(8,128)(2,1)}, u32[]{:S(2)}) copy-start(bf16[128,768]{1,0:T(8,128)(2,1)} %get-tuple-element.186) | copy-start | bytes 589828
  403.5 27.6 %copy-start.57 = (bf16[128,768]{1,0:T(8,128)(2,1)S(1)}, bf16[128,768]{1,0:T(8,128)(2,1)}, u32[]{:S(2)}) copy-start(bf16[128,768]{1,0:T(8,128)(2,1)} %get-tuple-element.187) | copy-start | bytes 589828
  457.5 119.0 %copy-start.5 = (f32[128,768]{1,0:T(8,128)}, f32[128,768]{1,0:T(8,128)S(1)}, u32[]{:S(2)}) copy-start(f32[128,768]{1,0:T(8,128)S(1)} %get-tuple-element.81) | copy-start | bytes 1179652
  497.9 78.6 %copy-start.151 = (f32[128]{0:T(128)}, f32[128]{0:T(128)S(1)}, u32[]{:S(2)}) copy-start(f32[128]{0:T(128)S(1)} %broadcast_multiply_fusion.12) | copy-start | bytes 1540
  498.1 78.4 %copy-start.169 = (f32[128]{0:T(128)}, f32[128]{0:T(128)S(1)}, u32[]{:S(2)}) copy-start(f32[128]{0:T(128)S(1)} %add_rsqrt_fusion.5) | copy-start | bytes 1540
  657.2 305.4 %reduce-scatter.8.cloned.1.call-start = ((), (), s32[]{:S(2)}) async-start(), calls=%async_computation.6 | async-start | bytes 17301504 | tf_op jit(solution)/shard_map/reduce_scatter | solution.py:466
  724.1 511.4 %reduce-scatter.4.cloned.1.call-start = ((), (), s32[]{:S(2)}) async-start(), calls=%async_computation.4 | async-start | bytes 29196288 | tf_op jit(solution)/shard_map/reduce_scatter | solution.py:450
  827.9 491.2 %all-reduce.27.cloned.1.call-start = ((), (), s32[]{:S(2)}) async-start(), calls=%async_computation.7 | async-start | bytes 294912 | tf_op jit(solution)/shard_map/psum | solution.py:487
  1237.5 52.9 %copy-start.55 = (f32[96,548]{1,0:T(8,128)S(1)}, f32[96,548]{1,0:T(8,128)}, u32[]{:S(2)}) copy-start(f32[96,548]{1,0:T(8,128)} %param.27) | copy-start | bytes 631300
  1237.5 52.9 %copy-start.56 = (f32[96,548]{1,0:T(8,128)S(1)}, f32[96,548]{1,0:T(8,128)}, u32[]{:S(2)}) copy-start(f32[96,548]{1,0:T(8,128)} %reduce-scatter.6.cloned.1.call-done) | copy-start | bytes 631300
  1287.1 40.7 %copy-start.9 = (f32[3,96,768]{2,1,0:T(8,128)}, f32[3,96,768]{2,1,0:T(8,128)S(1)}, u32[]{:S(2)}) copy-start(f32[3,96,768]{2,1,0:T(8,128)S(1)} %multiply_add_fusion) | copy-start | bytes 2654212
  (223 other events, 1407.0 us)
Sparse Core Ops, SparseCore 0:
  11.5 80.0 all-gather.3
  94.5 192.5 all-gather.5
  657.4 120.7 reduce-scatter.5
  780.4 182.1 reduce-scatter.7
  970.0 265.4 reduce-scatter.3
  1288.9 30.2 all-reduce.26

commit v2 on v1

v2 whole, which is shorter than its diff:
```python
import math

import jax
import jax.numpy as jnp
import numpy as np
from jax import lax
from jax.experimental import pallas as pl
from jax.experimental.pallas import tpu as pltpu
from jax.sharding import Mesh
from jax.sharding import PartitionSpec as P

D = 768
HEADS = 12
HEAD_DIM = 64
CH = 512
GROUPS = 16
WIDTH = D // GROUPS
POS_K = 19
REACH = POS_K // 2
SPAN = 10
TAIL = 16

EPS = 1e-05
VAR_FLOOR = 0.1
CLIP_LIMIT = 0.01
LR_ADAM = 0.03
LR_MUON = 2.0
DECAY = 0.5
WEIGHT_DECAY = 0.01
EMA_RATE = 0.5
KERNELS = (3, 3, 3, 3, 2, 2)
COEFF_A = 3.4445
COEFF_B = -4.775
COEFF_C = 2.0315
HIGHEST = lax.Precision.HIGHEST
F32 = jnp.float32
BF16 = jnp.bfloat16
LIMIT = 60 * 1024 * 1024
ROOT_HALF = math.sqrt(0.5)
ROOT_TAU = 1.0 / math.sqrt(2.0 * math.pi)


VMEM = pl.BlockSpec(memory_space=pltpu.VMEM)
ANY = pl.BlockSpec(memory_space=pl.ANY)
SMEM = pl.BlockSpec(memory_space=pltpu.SMEM)


def bf(values):
    return values.astype(BF16)


def low(values):
    return lax.optimization_barrier(values.astype(BF16)).astype(F32)


def dot(left, right, contract, batch=((), ())):
    return lax.dot_general(left, right, (contract, batch), preferred_element_type=F32)


def mm(left, right):
    return dot(left, right, ((1,), (0,)))


def mm_t(left, right):
    return dot(left, right, ((1,), (1,)))


def t_mm(left, right):
    return dot(left, right, ((0,), (0,)))


def gelu(values):
    return 0.5 * values * (1.0 + lax.erf(values * ROOT_HALF))


def gelu_slope(values):
    return 0.5 * (1.0 + lax.erf(values * ROOT_HALF)) + values * (
        ROOT_TAU * jnp.exp(-0.5 * values * values)
    )


def norm_fwd(values, gain, shift):
    center = values - jnp.mean(values, axis=-1, keepdims=True)
    scale = lax.rsqrt(jnp.mean(center * center, axis=-1, keepdims=True) + EPS)
    unit = center * scale
    return unit * gain + shift, (unit, scale)


def norm_bwd(kept, gain, grad):
    unit, scale = kept
    inner = grad * gain
    back = scale * (
        inner
        - jnp.mean(inner, axis=-1, keepdims=True)
        - unit * jnp.mean(inner * unit, axis=-1, keepdims=True)
    )
    return back, jnp.sum(grad * unit, axis=0), jnp.sum(grad, axis=0)


def first_taps(wave, frames):
    padded = jnp.pad(bf(wave), (0, 320 * (frames + 2) - wave.shape[0])).reshape(frames + 2, 320)
    rows = jnp.concatenate([padded[: frames + 1], padded[1:, :16]], axis=1)
    pick = np.zeros((336, 65 * 16), np.float32)
    for phase in range(64):
        for tap in range(10):
            pick[5 * phase + tap, 16 * phase + tap] = 1.0
    taps = bf(mm(rows, jnp.asarray(pick[:, : 64 * 16], BF16)))
    taps = taps.reshape(frames + 1, 64, 16).transpose(1, 0, 2)
    main = jnp.concatenate(
        [taps[:, :frames], taps[:1, 1:], jnp.zeros((1, frames, 16), BF16)], axis=0
    )
    return main, taps[:TAIL, frames]


def chooser(delta, rows_last=True):
    rows = lax.broadcasted_iota(jnp.int32, (TAIL, TAIL), 0)
    cols = lax.broadcasted_iota(jnp.int32, (TAIL, TAIL), 1)
    hit = cols == 2 * rows + delta if rows_last else rows == 2 * cols + delta
    return jnp.where(hit, 1.0, 0.0)


def stack_rows(ref, tap, taps=sum(KERNELS)):
    count = ref.shape[0] // taps
    rows = CH // count
    return ref[tap * count : (tap + 1) * count, :rows, :].reshape(CH, CH)


def first_kernel(taps_ref, weight_ref, out_ref):
    frames = taps_ref.shape[1]
    rows = taps_ref[...].reshape(2 * frames, taps_ref.shape[2])
    out_ref[...] = bf(gelu(mm(rows, weight_ref[...]))).reshape(out_ref.shape)


def encode_kernel(hidden_ref, tail_ref, stack_ref, small_ref, *refs):
    value_refs, hidden_refs = refs[:6], (hidden_ref,) + refs[6:11]
    value_tail_ref, hidden_tail_ref, normed_ref, unit_ref, scale_ref = refs[11:]
    frames = hidden_ref.shape[2]
    offset = 0
    tail = tail_ref[...]
    for layer, kernel in enumerate(KERNELS):
        source, values = hidden_refs[layer], value_refs[layer]
        count = values.shape[0]
        size = min(4, count)
        target = hidden_refs[layer + 1] if layer < 5 else None

        def product(index, offset=offset, kernel=kernel, source=source, size=size):
            total = None
            for tap in range(kernel):
                piece = source[pl.ds(index * size + tap // 2, size), tap % 2]
                part = mm(
                    piece.reshape(size * frames, CH),
                    stack_rows(stack_ref, offset // CH + tap),
                )
                total = part if total is None else total + part
            return total

        def step(index, carry, values=values, target=target, size=size, product=product):
            total = product(index)
            values[pl.ds(index * size, size)] = total.reshape(size, frames, CH)
            active = bf(gelu(total))
            target[pl.ds(index * (size // 2), size // 2)] = active.reshape(
                size // 2, 2, frames, CH
            )
            return carry

        if layer < 5:
            if count == size:
                step(0, 0)
            else:
                lax.fori_loop(0, count // size, step, 0)
        else:
            total = product(0)
            values[...] = total.reshape(values.shape)
            encoded = gelu(total)
            normed, kept = norm_fwd(encoded, small_ref[10:11, :], small_ref[11:12, :])
            normed_ref[...] = bf(normed)
            unit_ref[...] = kept[0]
            scale_ref[...] = jnp.broadcast_to(kept[1], scale_ref.shape)
        if layer < 3:
            total = None
            for tap in range(kernel):
                part = mm(
                    bf(mm(bf(chooser(tap)), tail)),
                    stack_rows(stack_ref, offset // CH + tap),
                )
                total = part if total is None else total + part
            value_tail_ref[layer] = total
            active = gelu(total)
            tail = bf(active)
            hidden_tail_ref[layer] = tail
            head = target[0, 0].astype(F32)
            rows = lax.broadcasted_iota(jnp.int32, (frames, CH), 0)
            moved = jnp.where(
                rows == frames - 1, active[0:1].astype(BF16).astype(F32),
                pltpu.roll(head, frames - 1, 0),
            )
            target[count // 2, 0] = bf(moved)
            target[count // 2, 1] = jnp.zeros((frames, CH), BF16)
        offset += kernel * CH


def layer_dw(grad_ref, source_ref, tail_grad, source_tail, kernel, out_ref):
    count, frames = grad_ref.shape[:2]
    size = min(8, count)
    for tap in range(kernel):
        rows = slice(tap * CH, (tap + 1) * CH)
        if tail_grad is None:
            out_ref[rows, :] = jnp.zeros((CH, CH), F32)
        else:
            out_ref[rows, :] = t_mm(bf(mm(bf(chooser(tap)), source_tail)), tail_grad)

        def step(index, carry, tap=tap, rows=rows):
            piece = source_ref[pl.ds(index * size + tap // 2, size), tap % 2]
            grad = grad_ref[pl.ds(index * size, size)]
            out_ref[rows, :] += t_mm(
                piece.reshape(size * frames, CH), grad.reshape(size * frames, CH)
            )
            return carry

        if count == size:
            step(0, 0)
        else:
            lax.fori_loop(0, count // size, step, 0)


def layer_dx(grad_ref, tail_grad, kernel, weight_of, slope, write, carry_ref, head_ref):
    count, frames = grad_ref.shape[:2]
    size = min(4, count)
    carry_ref[...] = jnp.zeros((frames, CH), F32)

    def step(index, unused):
        grad = grad_ref[pl.ds(index * size, size)].reshape(size * frames, CH)
        even = mm_t(grad, weight_of(0)).reshape(size, frames, CH)
        odd = mm_t(grad, weight_of(1)).reshape(size, frames, CH)
        if kernel == 3:
            late = mm_t(grad, weight_of(2)).reshape(size, frames, CH)
            before = carry_ref[...][None]
            if size > 1:
                before = jnp.concatenate([before, late[:-1]], axis=0)
            even = even + before
            carry_ref[...] = late[-1]
        write(index, size, even, odd)
        return unused

    if count == size:
        step(0, 0)
    else:
        lax.fori_loop(0, count // size, step, 0)
    if kernel != 3:
        return None
    wrap = carry_ref[...]
    rows = lax.broadcasted_iota(jnp.int32, (frames, CH), 0)
    head_ref[...] = jnp.where(rows == 0, 0.0, pltpu.roll(wrap, 1, 0))
    first = lax.broadcasted_iota(jnp.int32, (TAIL, CH), 0) == 0
    back = jnp.where(first, wrap[frames - 1 : frames, :], 0.0)
    if tail_grad is not None:
        for tap in range(3):
            back = back + jnp.dot(
                chooser(tap, False), mm_t(tail_grad, weight_of(tap)),
                precision=HIGHEST, preferred_element_type=F32,
            )
    return back


def copy_halves(core_ref, held, send_ref, keep_ref, first, taps, sem):
    half = CH // 2
    core = core_ref[0]
    copies = []
    for tap in range(taps):
        for target, index in ((send_ref, 1 - core), (keep_ref, core)):
            start = pl.multiple_of(tap * CH + index * half, half)
            copies.append(
                pltpu.make_async_copy(held.at[pl.ds(start, half)], target.at[first + tap], sem)
            )
            copies[-1].start()
    return copies


def encode_back_kernel(core_ref, grad_ref, unit_ref, scale_ref, small_ref, stack_ref, *refs):
    value_refs, hidden_refs = refs[:6], refs[6:11]
    value_tail_ref, hidden_tail_ref = refs[11:13]
    send_ref, keep_ref, second_ref, second_tail_ref, norm_ref = refs[13:18]
    grad_refs = (second_ref,) + refs[18:23]
    buffer_ref, carry_ref, head_ref, even_ref, sems = refs[23:]
    frames = grad_ref.shape[0]
    grad, gain, shift = norm_bwd(
        (unit_ref[...], scale_ref[:, :1]), small_ref[10:11, :], grad_ref[...]
    )
    norm_ref[0:1, :] = gain[None]
    norm_ref[1:2, :] = shift[None]
    grad_refs[5][0] = bf(grad * gelu_slope(value_refs[5][0]))
    tail_grad = None
    offset = sum(KERNELS) * CH
    copies = [[], []]
    for layer in range(5, 0, -1):
        kernel = KERNELS[layer]
        offset -= kernel * CH
        slot = layer % 2
        for copy in copies[slot]:
            copy.wait()
        held = buffer_ref.at[slot, 0 : kernel * CH]
        tail_source = None if tail_grad is None else hidden_tail_ref[layer - 1]
        layer_dw(grad_refs[layer], hidden_refs[layer - 1], tail_grad, tail_source, kernel, held)
        copies[slot] = copy_halves(
            core_ref, held, send_ref, keep_ref, offset // CH, kernel, sems.at[slot]
        )
        values, target = value_refs[layer - 1], grad_refs[layer - 1]

        def weight_of(tap, offset=offset):
            return stack_rows(stack_ref, offset // CH + tap)

        def write(index, size, even, odd, values=values, target=target, kernel=kernel):
            if kernel == 3:
                if not isinstance(index, int):
                    @pl.when(index == 0)
                    def _():
                        even_ref[...] = even[0]
                else:
                    even_ref[...] = even[0]
            for item in range(size):
                place = 2 * (index * size + item)
                target[place] = bf(even[item] * gelu_slope(values[place]))
                target[place + 1] = bf(odd[item] * gelu_slope(values[place + 1]))

        back = layer_dx(grad_refs[layer], tail_grad, kernel, weight_of, None, write,
                        carry_ref, head_ref)
        tail_grad = None
        if kernel == 3:
            target[0] = bf((even_ref[...] + head_ref[...]) * gelu_slope(values[0]))
            tail_grad = bf(back * gelu_slope(value_tail_ref[layer - 1]))
    second_tail_ref[...] = tail_grad
    for copy in copies[0] + copies[1]:
        copy.wait()


def second_dw_kernel(core_ref, grad_ref, tail_grad_ref, hidden_ref, tail_ref, old_send_ref,
                     old_keep_ref, send_ref, keep_ref, buffer_ref, sem):
    layer_dw(grad_ref, hidden_ref, tail_grad_ref[...], tail_ref[...], 3, buffer_ref)
    for copy in copy_halves(core_ref, buffer_ref, send_ref, keep_ref, 0, 3, sem):
        copy.wait()


def second_dx_kernel(grad_ref, tail_grad_ref, weight_ref, taps_ref, tail_taps_ref, first_ref,
                     out_ref, carry_ref, head_ref, even_ref):
    frames = grad_ref.shape[1]
    weights = first_ref[...]
    out_ref[...] = jnp.zeros(out_ref.shape, F32)

    def piece(place, grad):
        rows = taps_ref[place]
        low_grad = bf(grad * gelu_slope(mm(rows, weights)))
        return t_mm(rows, low_grad)

    def write(index, size, even, odd):
        @pl.when(index == 0)
        def _():
            even_ref[...] = even[0]

        for item in range(size):
            place = 2 * (index * size + item)
            grad = even[item]
            if item == 0:
                grad = jnp.where(index == 0, 0.0, grad)
            out_ref[...] += piece(place, grad) + piece(place + 1, odd[item])

    def weight_of(tap):
        return stack_rows(weight_ref, tap, 3)

    back = layer_dx(grad_ref, tail_grad_ref[...], 3, weight_of, None, write, carry_ref, head_ref)
    out_ref[...] += piece(0, even_ref[...] + head_ref[...])
    rows = tail_taps_ref[...]
    out_ref[...] += t_mm(rows, bf(back * gelu_slope(mm(rows, weights))))


COUNTS = (32, 16, 8, 4, 2, 1)


def kernel_params():
    return pltpu.CompilerParams(vmem_limit_bytes=LIMIT)


def first_layer(small, taps, frames):
    main, tail = taps
    weights = jnp.pad(bf(small[:10]), ((0, 6), (0, 0)))
    hidden = pl.pallas_call(
        first_kernel,
        grid=(33,),
        in_specs=[
            pl.BlockSpec((2, frames, 16), lambda i: (i, 0, 0)),
            pl.BlockSpec((16, CH), lambda i: (0, 0)),
        ],
        out_specs=pl.BlockSpec((1, 2, frames, CH), lambda i: (i, 0, 0, 0)),
        out_shape=jax.ShapeDtypeStruct((33, 2, frames, CH), BF16),
        name="first_layer",
    )(main, weights)
    return weights, hidden, bf(gelu(mm(tail, weights)))


def encode_fwd(small, stack, hidden, hidden_tail, frames):
    shape = jax.ShapeDtypeStruct
    return pl.pallas_call(
        encode_kernel,
        in_specs=[VMEM] * 4,
        out_specs=[VMEM] * 16,
        out_shape=[shape((count, frames, CH), F32) for count in COUNTS]
        + [shape((count // 2 + 1, 2, frames, CH), BF16) for count in COUNTS[:5]]
        + [
            shape((3, TAIL, CH), F32),
            shape((3, TAIL, CH), BF16),
            shape((frames, CH), BF16),
            shape((frames, CH), F32),
            shape((frames, 128), F32),
        ],
        name="encode",
        compiler_params=kernel_params(),
    )(hidden, hidden_tail, stack, small)


def encode_back(core, outs, small, stack, frames, grad):
    shape = jax.ShapeDtypeStruct
    plane = pltpu.VMEM((frames, CH), F32)
    part = shape((sum(KERNELS), CH // 2, CH), F32)
    return pl.pallas_call(
        encode_back_kernel,
        in_specs=[SMEM] + [VMEM] * 18,
        out_specs=[ANY, ANY, VMEM, VMEM, VMEM],
        out_shape=[
            part,
            part,
            shape((COUNTS[0], frames, CH), BF16),
            shape((TAIL, CH), BF16),
            shape((2, CH), F32),
        ],
        scratch_shapes=[pltpu.VMEM((count, frames, CH), BF16) for count in COUNTS[1:]]
        + [
            pltpu.VMEM((2, 3 * CH, CH), F32),
            plane,
            plane,
            plane,
            pltpu.SemaphoreType.DMA((2,)),
        ],
        name="encode_back",
        compiler_params=kernel_params(),
    )(core, grad, outs[14], outs[15], small, stack, *outs[:13])


def second_dw(core, second, second_tail, hidden, hidden_tail, parts):
    return pl.pallas_call(
        second_dw_kernel,
        in_specs=[SMEM] + [VMEM] * 4 + [ANY, ANY],
        out_specs=[ANY, ANY],
        out_shape=[jax.ShapeDtypeStruct(part.shape, F32) for part in parts],
        scratch_shapes=[pltpu.VMEM((3 * CH, CH), F32), pltpu.SemaphoreType.DMA],
        input_output_aliases={5: 0, 6: 1},
        name="second_dw",
        compiler_params=kernel_params(),
    )(core, second, second_tail, hidden, hidden_tail, *parts)


def second_dx(second, second_tail, stack, taps, weights, frames):
    main, tail = taps
    plane = pltpu.VMEM((frames, CH), F32)
    parts = 3 * stack.shape[0] // sum(KERNELS)
    return pl.pallas_call(
        second_dx_kernel,
        grid=(1,),
        in_specs=[
            VMEM,
            VMEM,
            pl.BlockSpec((parts,) + stack.shape[1:], lambda i: (0, 0, 0)),
            VMEM,
            VMEM,
            VMEM,
        ],
        out_specs=VMEM,
        out_shape=jax.ShapeDtypeStruct((16, CH), F32),
        scratch_shapes=[plane, plane, plane],
        name="second_dx",
        compiler_params=kernel_params(),
    )(second, second_tail, stack, main, tail, weights)


def neighbours(segment):
    frames = segment.shape[0]
    padded = jnp.pad(segment, (REACH, REACH), constant_values=-1)
    return jnp.stack([padded[offset : offset + frames] == segment for offset in range(POS_K)], 0)


def masked_of(starts):
    frames = starts.shape[0]
    padded = jnp.pad(starts, (SPAN - 1, 0))
    return (
        jnp.max(jnp.stack([padded[offset : offset + frames] for offset in range(SPAN)], 0), axis=0)
        > 0
    )


def taps_of(values, near, offset, flip):
    frames = values.shape[0]
    lane = 2 * REACH - offset if flip else offset
    shift = (REACH - lane) % frames
    rolled = values if shift == 0 else pltpu.roll(values, shift, 0)
    return bf(jnp.where(near[:, lane : lane + 1] > 0.0, rolled, 0.0))


def position_sum(values, near, spread_ref, back):
    half = D // 2
    sums = [None, None]
    for offset in range(POS_K):
        taps = taps_of(values, near, offset, back)
        for side in range(2):
            weight = spread_ref[offset, side * half : (side + 1) * half, :]
            piece = taps[:, side * half : (side + 1) * half]
            part = mm_t(piece, weight) if back else mm(piece, weight)
            sums[side] = part if sums[side] is None else sums[side] + part
    return jnp.concatenate(sums, axis=1)


def lane_half(values, upper):
    lanes = lax.broadcasted_iota(jnp.int32, values.shape, 1)
    keep = lanes >= HEAD_DIM if upper else lanes < HEAD_DIM
    return jnp.where(keep, values, 0.0)


def start_copies(place_ref, piece_refs, weight_ref, sems):
    if len(piece_refs) == 1 and len(piece_refs[0].shape) == 5:
        n_dp, n_narrow, unused, rows, cols = piece_refs[0].shape
        copies = []
        for matrix in range(3):
            for d in range(n_dp):
                for n in range(n_narrow):
                    copy = pltpu.make_async_copy(
                        piece_refs[0].at[d, n, matrix],
                        weight_ref.at[
                            matrix, pl.ds(d * rows, rows), pl.ds(n * cols, cols)
                        ],
                        sems.at[matrix],
                    )
                    copy.start()
                    copies.append(copy)
        return copies
    if len(piece_refs) == 1:
        copies = [
            pltpu.make_async_copy(piece_refs[0].at[m], weight_ref.at[m], sems.at[m])
            for m in range(3)
        ]
        for copy in copies:
            copy.start()
        return copies
    line, unused, rows, lanes = piece_refs[0].shape
    x, y, c = place_ref[0], place_ref[1], place_ref[2]
    copies = []
    for matrix in range(3):
        for number, ref in enumerate(piece_refs):
            half, dx, dy, dc = number // 8, number // 4 % 2, number // 2 % 2, number % 2
            narrow = (y ^ dy) * 2 + (c ^ dc)
            col = pl.multiple_of((narrow * 2 + half) * lanes, 128)
            for z in range(line):
                row = pl.multiple_of((2 * z + (x ^ dx)) * rows, 16)
                copy = pltpu.make_async_copy(
                    ref.at[z, matrix],
                    weight_ref.at[matrix, pl.ds(row, rows), pl.ds(col, lanes)],
                    sems.at[matrix],
                )
                copy.start()
                copies.append(copy)
    return copies


def await_copies(copies, matrix):
    count = len(copies) // 3
    for copy in copies[matrix * count : (matrix + 1) * count]:
        copy.wait()


def run_block(values, near, attend, spread_ref, weight_ref, vec_ref, copies, keep):
    vec = lambda row: vec_ref[row : row + 1, :]
    frames = values.shape[0]
    mixed = position_sum(bf(values).astype(F32), near, spread_ref, False) + vec(7)
    hidden, norm_one = norm_fwd(values + gelu(mixed), vec(0), vec(1))
    hidden_low = bf(hidden)
    await_copies(copies, 0)
    triple = bf(mm(hidden_low, weight_ref[0, :, : 3 * D]))
    outs = []
    for pair in range(HEADS // 2):
        lo = pair * 2 * HEAD_DIM
        hi = lo + 2 * HEAD_DIM
        query = triple[:, lo:hi].astype(F32)
        key = triple[:, D + lo : D + hi]
        value = triple[:, 2 * D + lo : 2 * D + hi]
        both = []
        for upper in range(2):
            scores = mm_t(bf(lane_half(query, upper)), key) * (1.0 / math.sqrt(HEAD_DIM))
            scores = jnp.where(attend, scores, -1e30)
            raised = jnp.exp(scores - jnp.max(scores, axis=-1, keepdims=True))
            chances = raised / jnp.sum(raised, axis=-1, keepdims=True)
            if keep is not None:
                keep["chances"][2 * pair + upper] = chances
            both.append(lane_half(mm(bf(chances), value), upper))
        outs.append(bf(both[0] + both[1]))
    outs = jnp.concatenate(outs, axis=1)
    second, norm_two = norm_fwd(hidden + mm(outs, weight_ref[0, :, 3 * D :]), vec(2), vec(3))
    second_low = bf(second)
    await_copies(copies, 1)
    await_copies(copies, 2)
    total = second
    step = D
    for start in range(0, weight_ref.shape[2], step):
        wide = mm(second_low, weight_ref[1, :, start : start + step])
        inner = bf(gelu(wide))
        if keep is not None:
            keep["wide"][:, start : start + step] = wide
            keep["right"][2, :, start : start + step] = inner
        total = total + mm_t(inner, weight_ref[2, :, start : start + step])
    result, norm_three = norm_fwd(total, vec(4), vec(5))
    if keep is not None:
        keep["triple"][...] = triple
        keep["mixed"][...] = mixed
        keep["left"][0] = hidden_low
        keep["left"][1] = outs
        keep["left"][2] = second_low
        for index, kept in enumerate((norm_one, norm_two, norm_three)):
            keep["units"][index] = kept[0]
            keep["scales"][index] = jnp.broadcast_to(kept[1], (frames, 128))
    return result


def teacher_kernel(place_ref, feat_ref, near_ref, col_ref, row_ref, spread_ref, vec_ref, *refs):
    piece_refs, (target_ref, weight_ref, sems) = refs[:-3], refs[-3:]
    copies = start_copies(place_ref, piece_refs, weight_ref, sems)
    attend = col_ref[...] == row_ref[...]
    output = run_block(feat_ref[...], near_ref[...], attend, spread_ref, weight_ref, vec_ref,
                       copies, None)
    member = attend.astype(F32)
    clip_size = jnp.sum(member, axis=1, keepdims=True)
    average = jnp.dot(member, output, precision=HIGHEST, preferred_element_type=F32) / clip_size
    center = output - average
    spread = jnp.dot(
        member, center * center, precision=HIGHEST, preferred_element_type=F32
    ) / clip_size
    target_ref[...] = center * lax.rsqrt(jnp.maximum(spread, VAR_FLOOR))


def student_kernel(place_ref, feat_ref, near_ref, col_ref, row_ref, mask_ref, weight_one_ref,
                   spread_ref, vec_ref, target_ref, normed_ref, project_ref, head_ref, *refs):
    piece_refs, refs = refs[:-14], refs[-14:]
    (left_ref, right_ref, side_ref, vector_ref, normed_grad_ref, loss_ref,
     weight_ref, chance_ref, wide_ref, triple_ref, mixed_ref, unit_ref, scale_ref,
     sems) = refs
    copies = start_copies(place_ref, piece_refs, weight_ref, sems)
    vec = lambda row: vec_ref[row : row + 1, :]
    total_sum = lambda values: jnp.sum(values, axis=0, keepdims=True)
    attend = col_ref[...] == row_ref[...]
    near = near_ref[...]
    chosen = mask_ref[...] > 0.0
    values = jnp.where(chosen, vec(9), feat_ref[...])
    keep = {
        "chances": chance_ref, "wide": wide_ref, "right": right_ref, "triple": triple_ref,
        "mixed": mixed_ref, "left": left_ref, "units": unit_ref, "scales": scale_ref,
    }
    result = run_block(values, near, attend, spread_ref, weight_ref, vec_ref, copies, keep)
    kept = lambda index: (unit_ref[index], scale_ref[index, :, :1])
    student_low = bf(result)
    scale = weight_one_ref[0:1, 0:1]
    error = jnp.where(chosen, mm(student_low, head_ref[...]) + vec(8) - target_ref[...], 0.0)
    loss_ref[...] = jnp.broadcast_to(
        jnp.sum(total_sum(error * error), axis=1, keepdims=True) * scale, loss_ref.shape
    )
    predict_grad = error * (2.0 * scale)
    vector_ref[8:9, :] = total_sum(predict_grad)
    predict_low = bf(predict_grad)
    reach_end = CH + POS_K * WIDTH

    def put_side(first, values, group=slice(0, D)):
        if len(side_ref.shape) == 2:
            side_ref[group, first : first + values.shape[1]] = values
            return
        rows, width = side_ref.shape[2:]
        owners = slice(group.start // rows, group.stop // rows)
        for n in range(side_ref.shape[1]):
            low_end = max(first, n * width)
            high_end = min(first + values.shape[1], (n + 1) * width)
            if low_end < high_end:
                part = values[:, low_end - first : high_end - first]
                side_ref[owners, n, :, low_end - n * width : high_end - n * width] = part.reshape(
                    owners.stop - owners.start, rows, high_end - low_end
                )

    put_side(reach_end, t_mm(student_low, predict_low))
    grad = mm_t(predict_low, head_ref[...])

    def norm_step(grad, index):
        back, gain, shift = norm_bwd(kept(index), vec(2 * index), grad)
        vector_ref[2 * index : 2 * index + 1, :] = gain[None]
        vector_ref[2 * index + 1 : 2 * index + 2, :] = shift[None]
        return back

    grad = norm_step(grad, 2)
    down = bf(grad)
    left_ref[3] = down
    for start in range(0, weight_ref.shape[2], D):
        cols = slice(start, start + D)
        wide_grad = bf(mm(down, weight_ref[2, :, cols]) * gelu_slope(wide_ref[:, cols]))
        right_ref[1, :, cols] = wide_grad
        grad = grad + mm_t(wide_grad, weight_ref[1, :, cols])
    grad = norm_step(grad, 1)
    down = bf(grad)
    right_ref[0, :, 3 * D :] = down
    outs_grad = mm_t(down, weight_ref[0, :, 3 * D :])
    for pair in range(HEADS // 2):
        lo = pair * 2 * HEAD_DIM
        hi = lo + 2 * HEAD_DIM
        query = triple_ref[:, lo:hi]
        key = triple_ref[:, D + lo : D + hi]
        value = triple_ref[:, 2 * D + lo : 2 * D + hi]
        sums = [None, None, None]
        for upper in range(2):
            out_low = bf(lane_half(outs_grad[:, lo:hi], upper))
            chances = chance_ref[2 * pair + upper]
            chance_grad = mm_t(out_low, value)
            score_grad = chances * (
                chance_grad - jnp.sum(chance_grad * chances, axis=-1, keepdims=True)
            )
            score_grad = bf(score_grad * (1.0 / math.sqrt(HEAD_DIM)))
            parts = (
                lane_half(mm(score_grad, key), upper),
                lane_half(t_mm(score_grad, query), upper),
                t_mm(bf(chances), out_low),
            )
            for index in range(3):
                sums[index] = parts[index] if upper == 0 else sums[index] + parts[index]
        for index in range(3):
            right_ref[0, :, index * D + lo : index * D + hi] = bf(sums[index])
    grad = grad + mm_t(right_ref[0, :, : 3 * D], weight_ref[0, :, : 3 * D])
    grad = norm_step(grad, 0)
    mixed_grad = grad * gelu_slope(mixed_ref[...])
    vector_ref[7:8, :] = total_sum(mixed_grad)
    mixed_low = bf(mixed_grad)
    grad = grad + position_sum(mixed_low.astype(F32), near, spread_ref, True)
    shifted = bf(values).astype(F32)
    half = D // 2
    for offset in range(POS_K):
        taps = taps_of(shifted, near, offset, False)
        for part in range(2):
            cols = slice(part * half, (part + 1) * half)
            full = t_mm(taps[:, cols], mixed_low[:, cols])
            pieces = [
                full[g * WIDTH : (g + 1) * WIDTH, g * WIDTH : (g + 1) * WIDTH]
                for g in range(half // WIDTH)
            ]
            put_side(CH + offset * WIDTH, jnp.concatenate(pieces, axis=0), cols)
    vector_ref[9:10, :] = total_sum(jnp.where(chosen, grad, 0.0))
    grad = jnp.where(chosen, 0.0, grad)
    vector_ref[6:7, :] = total_sum(grad)
    feat_low = bf(grad)
    put_side(0, t_mm(feat_low, normed_ref[...]))
    normed_grad_ref[...] = mm(feat_low, project_ref[...])


def spread_kernel(side_ref, tile_ref, spread_ref):
    half = D // 2
    rows = lax.broadcasted_iota(jnp.int32, (half, half), 0) // WIDTH
    cols = lax.broadcasted_iota(jnp.int32, (half, half), 1) // WIDTH
    same = rows == cols
    for offset in range(POS_K):
        piece = side_ref[:, offset * WIDTH : (offset + 1) * WIDTH]
        for part in range(2):
            wide = mm(piece[part * half : (part + 1) * half], tile_ref[...])
            spread_ref[offset, part * half : (part + 1) * half, :] = bf(
                jnp.where(same, wide, 0.0)
            )


def block_grad_kernel(place_ref, left_ref, left_two_ref, right_ref, right_two_ref,
                      send_top_ref, keep_top_ref, send_low_ref, keep_low_ref, full_ref):
    line, unused, unused_two, half, cols = keep_top_ref.shape
    x = place_ref[0]
    far = pl.program_id(1)
    full_ref[...] = t_mm(left_ref[0], right_ref[0]) + t_mm(left_two_ref[0], right_two_ref[0])
    for z in range(line):
        start = lambda index: pl.multiple_of((2 * z + index) * 2 * half, 8)
        keep_top_ref[z, 0, 0] = full_ref[pl.ds(start(x), half), :]
        send_top_ref[z, 0, 0] = bf(full_ref[pl.ds(start(1 - x), half), :])

    @pl.when(far == 0)
    def _():
        for z in range(line):
            for index in range(2):
                row = (2 * z + index) * 2 * half + half
                keep_low_ref[z, index, 0] = full_ref[row : row + half, :]

    @pl.when(far == 1)
    def _():
        for z in range(line):
            for index in range(2):
                row = (2 * z + index) * 2 * half + half
                send_low_ref[z, index, 0] = bf(full_ref[row : row + half, :])


def block_grads(left, left_two, right, right_two, place, n_dp, n_narrow):
    frames = left.shape[1]
    cols = right.shape[2] // n_narrow
    half = D // n_dp // 2
    line = n_dp // 2
    shape = jax.ShapeDtypeStruct

    def narrow(far, place):
        return 2 * (place[1] ^ far) + place[2]

    def left_index(matrix, far, place):
        is_out = (narrow(far, place) + 1) * cols > 3 * D
        return (jnp.where(matrix == 0, jnp.where(is_out, 1, 0), matrix + 1), 0, 0)

    left_spec = pl.BlockSpec((1, frames, D), left_index)
    right_spec = pl.BlockSpec(
        (1, frames, cols), lambda matrix, far, place: (matrix, 0, narrow(far, place))
    )
    top_spec = pl.BlockSpec(
        (line, 1, 1, half, cols), lambda matrix, far, place: (0, place[1] ^ far, matrix, 0, 0)
    )
    low_spec = pl.BlockSpec(
        (line, 2, 1, half, cols), lambda matrix, far, place: (0, 0, matrix, 0, 0)
    )
    whole = (line, 2, 3, half, cols)
    return pl.pallas_call(
        block_grad_kernel,
        grid_spec=pltpu.PrefetchScalarGridSpec(
            num_scalar_prefetch=1,
            grid=(3, 2),
            in_specs=[left_spec, left_spec, right_spec, right_spec],
            out_specs=[top_spec, top_spec, low_spec, low_spec],
            scratch_shapes=[pltpu.VMEM((D, cols), F32)],
        ),
        out_shape=[shape(whole, BF16), shape(whole, F32), shape(whole, BF16), shape(whole, F32)],
        name="block_grads",
    )(place, left, left_two, right, right_two)


def plain_weight_grads(left, right, n_dp, n_narrow):
    full = [
        jnp.concatenate(
            [t_mm(left[0], right[0, :, : 3 * D]), t_mm(left[1], right[0, :, 3 * D :])], axis=1
        ),
        t_mm(left[2], right[1]),
        t_mm(left[3], right[2]),
    ]
    full = jnp.stack(full, 0)
    full = full.reshape(3, n_dp, D // n_dp, n_narrow, full.shape[2] // n_narrow)
    return full.transpose(1, 3, 0, 2, 4)


def spread_kernels(side_conv):
    tile = np.zeros((WIDTH, D // 2), np.float32)
    for column in range(D // 2):
        tile[column % WIDTH, column] = 1.0
    return pl.pallas_call(
        spread_kernel,
        in_specs=[VMEM, VMEM],
        out_specs=VMEM,
        out_shape=jax.ShapeDtypeStruct((POS_K, D, D // 2), BF16),
        name="spread",
        compiler_params=pltpu.CompilerParams(vmem_limit_bytes=LIMIT),
    )(side_conv, jnp.asarray(tile, BF16))


def flat_pieces(pieces):
    if not isinstance(pieces, list):
        return [pieces], pieces.shape[-1] * (pieces.shape[1] if pieces.ndim == 5 else 1)
    flat = [piece for half in pieces for row in half for column in row for piece in column]
    return flat, flat[0].shape[-1] * 8


def teacher_target(feats, near, col, row, spread, vec, pieces, place):
    pieces, width = flat_pieces(pieces)
    return pl.pallas_call(
        teacher_kernel,
        in_specs=[SMEM] + [VMEM] * 6 + [ANY] * len(pieces),
        out_specs=VMEM,
        out_shape=jax.ShapeDtypeStruct(feats.shape, F32),
        scratch_shapes=[pltpu.VMEM((3, D, width), BF16), pltpu.SemaphoreType.DMA((3,))],
        name="teacher",
        compiler_params=pltpu.CompilerParams(vmem_limit_bytes=LIMIT),
    )(place, feats, near, col, row, spread, vec, *pieces)


def student_step(feats, near, col, row, mask, weight, spread, vec, target, normed, project, head,
                 pieces, place, side_shape):
    pieces, width = flat_pieces(pieces)
    frames = feats.shape[0]
    shape = jax.ShapeDtypeStruct
    return pl.pallas_call(
        student_kernel,
        in_specs=[SMEM] + [VMEM] * 12 + [ANY] * len(pieces),
        out_specs=[VMEM] * 6,
        out_shape=[
            shape((4, frames, D), BF16),
            shape((3, frames, width), BF16),
            shape(side_shape, F32),
            shape((10, D), F32),
            shape((frames, CH), F32),
            shape((8, 128), F32),
        ],
        scratch_shapes=[
            pltpu.VMEM((3, D, width), BF16),
            pltpu.VMEM((HEADS, frames, frames), F32),
            pltpu.VMEM((frames, width), F32),
            pltpu.VMEM((frames, 3 * D), BF16),
            pltpu.VMEM((frames, D), F32),
            pltpu.VMEM((3, frames, D), F32),
            pltpu.VMEM((3, frames, 128), F32),
            pltpu.SemaphoreType.DMA((3,)),
        ],
        name="student",
        compiler_params=pltpu.CompilerParams(vmem_limit_bytes=LIMIT),
    )(
        place, feats, near, col, row, mask, weight, spread, vec, target, normed, project, head,
        *pieces,
    )


class Links:
    def __init__(self, n_dp, n_narrow):
        self.n_dp, self.n_narrow = n_dp, n_narrow
        self.line = n_dp // 2
        self.direct = n_narrow == 4 and n_dp % 2 == 0 and self.line <= 4 and D % (16 * n_dp) == 0
        dp, narrow = lax.axis_index("dp"), lax.axis_index("narrow")
        self.z, self.x, self.y, self.c = dp // 2, dp % 2, narrow // 2, narrow % 2

    def swap_c(self, values):
        return self.flip(values, "narrow", 1)

    def swap_y(self, values):
        return self.flip(values, "narrow", 2)

    def swap_x(self, values):
        return self.flip(values, "dp", 1)

    def flip(self, values, axis, bit):
        size = self.n_dp if axis == "dp" else self.n_narrow
        return lax.ppermute(values, axis, [(i, i ^ bit) for i in range(size)])

    def step_z(self, values, up, senders):
        move = 1 if up else -1
        pairs = [(2 * z + x, 2 * (z + move) + x) for z in senders for x in range(2)]
        return lax.ppermute(values, "dp", pairs)

    def total(self, values, axes=("narrow", "dp")):
        for axis in axes:
            size = self.n_dp if axis == "dp" else self.n_narrow
            if size & (size - 1):
                values = lax.psum(values, axis)
                continue
            bit = 1
            while bit < size:
                values = values + self.flip(values, axis, bit)
                bit *= 2
        return values

    def go(self, requests):
        results = []
        for request in requests:
            kind, values = request[0], request[1]
            if kind == "c":
                results.append(self.flip(values, "narrow", 1))
            elif kind == "y":
                results.append(self.flip(values, "narrow", 2))
            elif kind == "x":
                results.append(self.flip(values, "dp", 1))
            else:
                results.append(self.step_z(values, kind == "up", request[2]))
        return results

    def gather_steps(self, values):
        last = self.line - 1
        ups, downs = [], []
        up = down = values
        for hop in range(1, self.line):
            up, down = yield [
                ("up", up, range(hop - 1, last)),
                ("down", down, range(1, self.line - hop + 1)),
            ]
            ups.append(up)
            downs.append(down)
        stacked = jnp.stack(ups[::-1] + [values] + downs, 0)
        column = lax.dynamic_slice_in_dim(stacked, last - self.z, self.line, 0)
        lanes = values.shape[-1] // 2
        one, two = column[..., :lanes], column[..., lanes:]
        one_y, two_x, one_x, two_y, one_c, two_c = yield [
            ("y", one), ("x", two), ("x", one), ("y", two), ("c", one), ("c", two)
        ]
        one_xy, two_xy, one_yc, two_xc, one_xc, two_yc = yield [
            ("x", one_y), ("y", two_x), ("c", one_y), ("c", two_x), ("c", one_x), ("c", two_y)
        ]
        one_xyc, two_xyc = yield [("c", one_xy), ("c", two_xy)]
        return [
            [[[one, one_c], [one_y, one_yc]], [[one_x, one_xc], [one_xy, one_xyc]]],
            [[[two, two_c], [two_y, two_yc]], [[two_x, two_xc], [two_xy, two_xyc]]],
        ]

    def gather_whole(self, values):
        if not self.direct:
            whole = lax.all_gather(values, "narrow", axis=2, tiled=True)
            return lax.all_gather(whole, "dp", axis=1, tiled=True)
        whole = lax.all_gather(values, ("dp", "narrow"), axis=0)
        return whole.reshape((self.n_dp, self.n_narrow) + values.shape)

    def split(self, values):
        values = values.reshape((self.line, 2, 2, 2) + values.shape[1:])
        pick = lambda index: lax.dynamic_index_in_dim(values, index, 3, False)
        return pick(1 - self.c), pick(self.c)

    def scatter_steps(self, parts, coarse):
        send, keep = parts
        half = send.shape[-2] // 2
        pick = lambda array, axis, index: lax.dynamic_index_in_dim(array, index, axis, False)
        short = bf if coarse else lambda array: array
        (got,) = yield [("c", send)]

        def both(rows, axis, index):
            return pick(keep[..., rows, :], axis, index) + pick(got[..., rows, :], axis, index)

        top, low_rows = slice(0, half), slice(half, None)
        ends = yield [
            ("x", short(both(top, 1, 1 - self.x))), ("y", short(both(low_rows, 2, 1 - self.y)))
        ]

        def all_three(rows, first, at_first, second, at_second, end):
            mine = [
                pick(pick(array[..., rows, :], first, at_first), second, at_second)
                for array in (keep, got)
            ]
            return mine[0] + mine[1] + pick(end, second, at_second).astype(F32)

        top_of = lambda index: all_three(top, 1, self.x, 1, index, ends[0])
        low_of = lambda index: all_three(low_rows, 2, self.y, 1, index, ends[1])
        more = yield [("y", top_of(1 - self.y)), ("x", low_of(1 - self.x))]
        one = top_of(self.y) + more[0]
        two = low_of(self.x) + more[1]
        return (yield from self.line_steps(jnp.concatenate([one, two], axis=-2)))

    def half_steps(self, send_top, keep_top, send_low, keep_low):
        pick = lambda array, index: lax.dynamic_index_in_dim(array, index, 1, False)
        top, lower = yield [("x", send_top), ("y", send_low)]
        top_of = lambda index: pick(keep_top, index) + pick(top, index).astype(F32)
        low_of = lambda index: pick(keep_low, index) + pick(lower, index).astype(F32)
        more = yield [("y", top_of(1 - self.y)), ("x", low_of(1 - self.x))]
        one, two = top_of(self.y) + more[0], low_of(self.x) + more[1]
        return (yield from self.line_steps(jnp.concatenate([one, two], axis=-2)))

    def line_steps(self, column):
        pick = lambda array, axis, index: lax.dynamic_index_in_dim(array, index, axis, False)
        last = self.line - 1
        at = lambda offset: pick(column, 0, (self.z + offset) % self.line)
        up = down = None
        for hop in range(last, 0, -1):
            send_up = at(hop) if up is None else at(hop) + up
            send_down = at(-hop) if down is None else at(-hop) + down
            up, down = yield [
                ("up", send_up, range(0, last - hop + 1)),
                ("down", send_down, range(hop, self.line)),
            ]
        own = at(0)
        return own if up is None else own + up + down


class Stages:
    def __init__(self, links, steps):
        self.links, self.steps = links, list(steps)
        self.requests = [next(one) for one in self.steps]
        self.results = [None] * len(self.steps)

    def tie(self, *others):
        arrays = [[request[1] for request in one] for one in self.requests]
        arrays, others = lax.optimization_barrier((arrays, others))
        self.requests = [
            [(request[0], array) + tuple(request[2:]) for request, array in zip(one, part)]
            for one, part in zip(self.requests, arrays)
        ]
        return others if len(others) != 1 else others[0]

    def add(self, one):
        self.steps.append(one)
        self.requests.append(next(one))
        self.results.append(None)

    def advance(self, after=()):
        got = [self.links.go(one) for one in self.requests]
        if after:
            got, after = lax.optimization_barrier((got, tuple(after)))
        for index, one in enumerate(self.steps):
            if not self.requests[index]:
                continue
            try:
                self.requests[index] = one.send(got[index])
            except StopIteration as stop:
                self.requests[index] = []
                self.results[index] = stop.value
        return after if len(after) != 1 else after[0]

    def finish(self):
        while any(self.requests):
            self.advance()
        return self.results


def adamw(weight, grad, first, second, power):
    first = DECAY * first + (1.0 - DECAY) * grad
    second = DECAY * second + (1.0 - DECAY) * grad * grad
    unbias = 1.0 - power
    step_size = first / unbias / (jnp.sqrt(second / unbias) + 1e-08)
    return (weight - LR_ADAM * (step_size + WEIGHT_DECAY * weight), first, second)


def exact(left, right):
    return jnp.einsum("brs,bst->brt", left, right, precision=HIGHEST)


def orthogonal(blocks, gram_total):
    gram = gram_total(jnp.einsum("brc,bsc->brs", blocks, blocks, precision=HIGHEST))
    scales = 1.0 / (jnp.sqrt(jnp.trace(gram, axis1=1, axis2=2)) + 1e-07)
    gram = gram * (scales * scales)[:, None, None]
    eye = jnp.eye(gram.shape[1], dtype=F32)[None]
    whole = None
    for iteration in range(5):
        square = exact(gram, gram)
        step = COEFF_A * eye + COEFF_B * gram + COEFF_C * square
        whole = step if whole is None else exact(step, whole)
        if iteration < 4:
            gram = exact(exact(step, gram), step)
            gram = 0.5 * (gram + gram.transpose(0, 2, 1))
    return exact(whole * scales[:, None, None], blocks)


def per_device(
    wave,
    clip_ids,
    span_starts,
    step_count,
    conv_small,
    conv_stack,
    side,
    vectors,
    block,
    teacher_block,
    teacher_vectors,
    small_mean,
    small_square,
    stack_mean,
    stack_square,
    side_mean,
    side_square,
    vector_mean,
    vector_square,
    block_momentum,
    n_dp,
    n_narrow,
):
    everyone = ("dp", "narrow")
    frames = clip_ids.shape[0]
    rows_here, cols_here = block.shape[1:]
    side_rows, side_cols = side.shape
    links = Links(n_dp, n_narrow)
    place = jnp.stack([links.x, links.y, links.c]).astype(jnp.int32)
    stack_rows_here = conv_stack.shape[0]
    side_size = side_rows * side_cols
    side_lines = -(-side_size // CH)
    lines = -(-(stack_rows_here + side_lines) // 16) * 16
    side_flat = jnp.pad(bf(side).reshape(-1), (0, side_lines * CH - side_size))
    send = jnp.concatenate(
        [
            bf(conv_stack),
            side_flat.reshape(side_lines, CH),
            jnp.zeros((lines - stack_rows_here - side_lines, CH), BF16),
        ],
        axis=0,
    )
    stack = lax.all_gather(send, everyone, axis=0)
    teacher_pieces = links.gather_whole(bf(teacher_block))
    masked = masked_of(span_starts)
    masked_here = jnp.full((1, 128), jnp.sum(masked.astype(F32)), F32)
    total = jnp.maximum(links.total(masked_here)[0, 0], 1.0)
    small_low = low(conv_small)
    vector_low = low(vectors)
    taps = first_taps(wave, frames)
    first_weights, hidden, hidden_tail = first_layer(small_low, taps, frames)
    whole_side = stack[:, stack_rows_here : stack_rows_here + side_lines].reshape(
        n_dp * n_narrow, side_lines * CH
    )[:, :side_size]
    whole_side = (
        whole_side.reshape(n_dp, n_narrow, side_rows, side_cols)
        .transpose(0, 2, 1, 3)
        .reshape(n_dp * side_rows, n_narrow * side_cols)
    )
    spread_of = lambda: spread_kernels(whole_side[:, CH : CH + POS_K * WIDTH])
    if links.direct:
        exchange = Stages(links, [links.gather_steps(bf(block))])
        hidden = exchange.advance((hidden,))
        for unused in range(links.line - 2):
            exchange.advance()
        hidden = exchange.tie(hidden)
        outs = encode_fwd(small_low, stack, hidden, hidden_tail, frames)
        outs = list(outs)
        outs[13] = exchange.advance((outs[13],))
        whole_side = exchange.tie(whole_side)
        spread = spread_of()
    else:
        student_pieces = links.gather_whole(bf(block))
        outs = encode_fwd(small_low, stack, hidden, hidden_tail, frames)
        spread = spread_of()
    normed = outs[13]
    project = whole_side[:, :CH]
    head = whole_side[:, CH + POS_K * WIDTH :]
    near = jnp.pad(neighbours(clip_ids).astype(F32).T, ((0, 0), (0, 32 - POS_K)))
    col, row = clip_ids[:, None], clip_ids[None, :]
    feats = mm_t(normed, project) + vector_low[6]
    target = teacher_target(
        feats, near, col, row, spread, low(teacher_vectors), teacher_pieces, place
    )
    if links.direct:
        target = exchange.advance((target,))
        (student_pieces,) = exchange.finish()
    weight = jnp.full((8, 128), 1.0 / (total * math.sqrt(D)), F32)
    left, right, side_grad, vector_grad, normed_grad, loss_tile = student_step(
        feats,
        near,
        col,
        row,
        masked.astype(F32)[:, None],
        weight,
        spread,
        vector_low,
        target,
        normed,
        project,
        head,
        student_pieces,
        place,
        (n_dp, n_narrow, side_rows, side_cols)
        if links.direct
        else (n_dp * side_rows, n_narrow * side_cols),
    )
    loss_part = loss_tile[0, 0]
    devices = n_dp * n_narrow
    if links.direct:
        core = links.c.astype(jnp.int32).reshape(1)
        others = [links.swap_c(left), links.swap_c(right)]
        parts = links.split(side_grad.reshape(devices, side_rows, side_cols))
        others, parts = lax.optimization_barrier((others, parts))
        grads = block_grads(left, others[0], right, others[1], place, n_dp, n_narrow)
        feed = Stages(links, [links.half_steps(*grads)])
        normed_grad = feed.tie(normed_grad)
        *parts_two, second, second_tail, norm_grad = encode_back(
            core, outs, small_low, stack, frames, normed_grad
        )
        second = feed.advance((second,))
        second = feed.tie(second)
        parts_two = second_dw(core, second, second_tail, hidden, hidden_tail, parts_two)
        shape = (links.line, 2, 2) + conv_stack.shape
        last = Stages(
            links, [links.scatter_steps([part.reshape(shape) for part in parts_two], False)]
        )
        second = last.tie(second)
        parts, second = lax.optimization_barrier((parts, second))
        rest = Stages(links, [links.scatter_steps(parts, False)])
        tap_grad = second_dx(second, second_tail, stack, taps, first_weights, frames)
        tap_grad = last.advance((tap_grad,))
        tap_grad = last.tie(tap_grad)
        tap_grad = feed.advance((tap_grad,))
        tap_grad = rest.advance((tap_grad,))
        (stack_piece,) = last.finish()
        (block_piece,) = feed.finish()
        (side_piece,) = rest.finish()
    else:
        sums = lambda values: lax.psum_scatter(
            values.reshape((-1,) + values.shape[-1:]), everyone, scatter_dimension=0, tiled=True
        )
        block_piece = sums(plain_weight_grads(left, right, n_dp, n_narrow))
        block_piece = block_piece.reshape(3, rows_here, cols_here)
        side_grad = side_grad.reshape(n_dp, side_rows, n_narrow, side_cols)
        side_piece = sums(side_grad.transpose(0, 2, 1, 3))
        core = jnp.zeros((1,), jnp.int32)
        *parts, second, second_tail, norm_grad = encode_back(
            core, outs, small_low, stack, frames, normed_grad
        )
        parts = second_dw(core, second, second_tail, hidden, hidden_tail, parts)
        tap_grad = second_dx(second, second_tail, stack, taps, first_weights, frames)
        stack_piece = sums(jnp.stack([parts[1], parts[0]], 1).reshape(sum(KERNELS) * CH, CH))
    small_grad = jnp.concatenate([tap_grad[:10], norm_grad], axis=0)
    packed = jnp.concatenate(
        [
            vector_grad,
            small_grad.reshape(-1, D),
            jnp.full((1, D), loss_part, F32),
        ],
        axis=0,
    )
    packed = links.total(packed)
    vector_total = packed[:10]
    small_total = packed[10:-1].reshape(small_grad.shape)
    loss_value = packed[-1, 0]
    shard_squares = (
        jnp.sum(block_piece * block_piece)
        + jnp.sum(side_piece * side_piece)
        + jnp.sum(stack_piece * stack_piece)
    )
    grad_norm = jnp.sqrt(
        links.total(jnp.full((1, 128), shard_squares, F32))[0, 0]
        + jnp.sum(small_total * small_total)
        + jnp.sum(vector_total * vector_total)
    )
    factor = jnp.minimum(1.0, CLIP_LIMIT / (grad_norm + 1e-06))
    power = jnp.power(DECAY, step_count[0].astype(F32))
    small_next = adamw(conv_small, factor * small_total, small_mean, small_square, power)
    stack_next = adamw(conv_stack, factor * stack_piece, stack_mean, stack_square, power)
    side_next = adamw(side, factor * side_piece, side_mean, side_square, power)
    vector_next = adamw(vectors, factor * vector_total, vector_mean, vector_square, power)
    momentum = DECAY * block_momentum + factor * block_piece
    ortho = orthogonal(momentum, lambda gram: links.total(gram, ("narrow",)))
    block_next = block * (1.0 - LR_MUON * WEIGHT_DECAY) - LR_MUON * ortho
    teacher_next = EMA_RATE * teacher_block + (1.0 - EMA_RATE) * block_next
    teacher_vec_next = EMA_RATE * teacher_vectors + (1.0 - EMA_RATE) * vector_next[0]
    return (
        (loss_value, grad_norm)
        + small_next
        + stack_next
        + side_next
        + vector_next
        + (block_next, momentum, teacher_next, teacher_vec_next, bf(block_next))
    )


def solution(mesh):
    n_dp, n_narrow = mesh.shape["dp"], mesh.shape["narrow"]

    def step(*arguments):
        return per_device(*arguments, n_dp, n_narrow)

    rows = P(("dp", "narrow"), None)
    flat = P(("dp", "narrow"))
    grid = P("dp", "narrow")
    cube = P(None, "dp", "narrow")
    one = P()
    in_specs = (
        (flat, flat, flat, one, one, rows, grid, one, cube, cube, one, one, one)
        + (rows, rows, grid, grid, one, one, cube)
    )
    out_specs = (
        (one, one, one, one, one, rows, rows, rows, grid, grid, grid, one, one, one)
        + (cube, cube, cube, one, cube)
    )
    return jax.shard_map(
        step, mesh=mesh, in_specs=in_specs, out_specs=out_specs, check_vma=False
    )
```

time: 1350 us -> 750 us (0.56)
  local copies, waits for them, and re-layouts: 407 us -> 97.6 us
  waiting for transfers between devices: 473 us -> 214 us
  Pallas kernels: 0 us -> 207 us
  matrix products: 208 us -> 10.6 us
  starting transfers between devices: 0.46 us -> 112 us
  blocking collectives: 82.2 us -> 0 us
  other arithmetic: 142 us -> 79 us
    reduce_scatter x3 -> x0, waiting for transfers between devices: 335 us -> none  [the longest x1 271 us: per_device(): lax.psum_scatter(block_send.reshape(n_dp * n_narrow * 3 * rows_here, cols...]
    pallas_call x0 -> x9, Pallas kernels: none -> 207 us  [the longest x1 40.7 us: encode_back(): pl.pallas_call(encode_back_kernel, in_specs=[SMEM] + [VMEM] * 18, out_spe...]
    ppermute x0 -> x71, waiting for transfers between devices: none -> 202 us  [the longest x47 128 us: flip(): return lax.ppermute(values, axis, [(i, i ^ bit) for i in range(size)])]
    dot_general x54 -> x4, matrix products: 195 us -> 2.39 us  [dot(): lax.dot_general(left, right, (contract, batch), preferred_element_type=F32)]
    slice x128 -> x18, local copies, waits for them, and re-layouts: 175 us -> 26 us  [the longest x1 7.34 us: both(): got[..., rows, :]]
    ppermute x0 -> x71, starting transfers between devices: none -> 112 us  [the longest x24 74.8 us: step_z(): return lax.ppermute(values, 'dp', pairs)]
    all_gather x2, waiting for transfers between devices: 112 us -> 11.7 us  [the longest x1 11.3 us: gather_whole(): whole = lax.all_gather(values, ('dp', 'narrow'), axis=0)]
    psum x2 -> x0, blocking collectives: 82.2 us -> none  [the longest x1 41.6 us: per_device(): lax.psum((small_grad, vector_grad, loss_part), everyone)]
  transfers between devices with their start and end apart: 6 -> 73, of which waited for: 5 -> 24; matrix products, arithmetic and copies ran while one was open for 27% -> 21% of each run, Pallas kernels for 0% -> 19%
where the time goes in v2:
time: 750 us; the launch traced here: 742 us
  waiting for transfers between devices  214 us (29%)
  Pallas kernels  207 us (28%)
  starting transfers between devices  112 us (15%)
  local copies, waits for them, and re-layouts  97.6 us (13%)
  other arithmetic  79 us (11%)
  between operations  21.1 us (3%)
  matrix products  10.6 us (1%)
    ppermute x47, waiting for transfers between devices, flip(): return lax.ppermute(values, axis, [(i, i ^ bit) for i in range(size)])  128 us
    ppermute x24, starting transfers between devices, step_z(): return lax.ppermute(values, 'dp', pairs)  74.8 us
    ppermute x24, waiting for transfers between devices, step_z(): return lax.ppermute(values, 'dp', pairs)  73.6 us
    pallas_call x1, Pallas kernels, encode_back(): pl.pallas_call(encode_back_kernel, in_specs=[SMEM] + [VMEM] * 18, out_spe...  40.7 us
    ppermute x47, starting transfers between devices, flip(): return lax.ppermute(values, axis, [(i, i ^ bit) for i in range(size)])  37.6 us
    pallas_call x1, Pallas kernels, student_step(): pl.pallas_call(student_kernel, in_specs=[SMEM] + [VMEM] * 12 + [ANY] * le...  37 us
    pallas_call x1, Pallas kernels, encode_fwd(): pl.pallas_call(encode_kernel, in_specs=[VMEM] * 4, out_specs=[VMEM] * 16,...  30.2 us
    pallas_call x1, Pallas kernels, second_dx(): pl.pallas_call(second_dx_kernel, grid=(1,), in_specs=[VMEM, VMEM, pl.Bloc...  25.8 us
  transfers between devices with their start and end apart: 73, of which 24 were waited for; matrix products, arithmetic and copies ran while one was open for 21% of the time, Pallas kernels for 19%

profile of v2, /device:TPU:0, one launch (start us, length us, event | category | flops | bytes accessed | tf_op | source)
XLA Modules:
  0.0 741.6 jit_solution(14642300767264551681)
XLA Ops:
  27.8 20.8 %first_layer.1.hidden_ref = bf16[33,2,128,512]{3,2,1,0:T(8,128)(2,1)} custom-call(bf16[66,128,16]{2,1,0:T(8,128)(2,1)} %copy.167.taps_ref, bf16[16,512]{1,0:T(8,128)(2,1)} %pad.27.weight_ref.first_ref), custom_call_target="tpu_custom_call" | custom-call | tf_op jit(solution)/shard_map/first_layer/pallas_call | solution.py:385
  52.9 21.1 %collective-permute-done.4 = bf16[3,96,768]{2,1,0:T(8,128)(2,1)S(1)} collective-permute-done((bf16[3,96,768]{2,1,0:T(8,128)(2,1)}, bf16[3,96,768]{2,1,0:T(8,128)(2,1)S(1)}, u32[]{:S(2)}, u32[]{:S(2)}) %collective-permute-start.4) | collective-permute-done | bytes 442400 | tf_op jit(solution)/shard_map/ppermute | solution.py:945
  80.0 33.1 %collective-permute-done.5 = bf16[3,96,768]{2,1,0:T(8,128)(2,1)S(1)} collective-permute-done((bf16[3,96,768]{2,1,0:T(8,128)(2,1)S(1)}, bf16[3,96,768]{2,1,0:T(8,128)(2,1)S(1)}, u32[]{:S(2)}, u32[]{:S(2)}) %collective-permute-start.5) | collective-permute-done | bytes 442400 | tf_op jit(solution)/shard_map/ppermute | solution.py:945
  124.1 30.2 %encode.1 = (f32[32,128,512]{2,1,0:T(8,128)}, f32[16,128,512]{2,1,0:T(8,128)}, f32[8,128,512]{2,1,0:T(8,128)}, f32[4,128,512]{2,1,0:T(8,128)}, f32[2,128,512]{2,...) custom-call(bf16[33,2,128,512]{3,2,1,0:T(8,128)(2,1)} %first_layer.1, ...), custom_call_target="tpu_custom_call" | custom-call | tf_op jit(solution)/shard_map/encode/pallas_call | solution.py:401
  154.3 9.1 %collective-permute-done.8.refs_4_ = bf16[4,3,96,384]{3,2,1,0:T(8,128)(2,1)} collective-permute-done((bf16[4,3,96,384]{3,2,1,0:T(8,128)(2,1)}, bf16[4,3,96,384]{3,2,1,0:T(8,128)(2,1)}, u32[]{:S(2)}, u32[]{:S(2)}) %collective-permute-start.8) | collective-permute-done | bytes 884768 | tf_op jit(solution)/shard_map/ppermute | solution.py:940
  164.9 9.5 %reshape.200 = bf16[8,4,96,548]{3,2,1,0:T(8,128)(2,1)} reshape(bf16[32,52608]{1,0:T(8,128)(2,1)S(1)} %slice.263) | data formatting | bytes 6733824 | tf_op jit(solution)/shard_map/reshape | solution.py:1190
  174.3 6.1 copy.226
  180.4 6.3 reshape.201
  189.2 33.4 %collective-permute-done.17.refs_6_ = bf16[4,3,96,384]{3,2,1,0:T(8,128)(2,1)} collective-permute-done((bf16[4,3,96,384]{3,2,1,0:T(8,128)(2,1)}, bf16[4,3,96,384]{3,2,1,0:T(8,128)(2,1)}, u32[]{:S(2)}, u32[]{:S(2)}) %collective-permute-start.17) | collective-permute-done | bytes 884768 | tf_op jit(solution)/shard_map/ppermute | solution.py:940
  235.0 8.7 %spread.1.spread_ref = bf16[19,768,384]{2,1,0:T(8,128)(2,1)} custom-call(bf16[768,912]{1,0:T(8,128)(2,1)} %slice.239.side_ref, bf16[48,384]{1,0:T(8,128)(2,1)} %constant.769.clone.tile_ref), custom_call_target="tpu_custom_call" | custom-call | tf_op jit(solution)/shard_map/spread/pallas_call | solution.py:856
  244.8 11.3 %all-gather.7.cloned.1.call-done = bf16[96,96,768]{2,1,0:T(8,128)(2,1)} async-done(((bf16[3,96,768]{2,1,0:T(8,128)(2,1)}), bf16[96,96,768]{2,1,0:T(8,128)(2,1)}) %all-gather.7.cloned.1.call-update) | async-done | bytes 14155792 | tf_op jit(solution)/shard_map/all_gather | solution.py:1004
  256.1 16.8 %teacher.1.target_ref = f32[128,768]{1,0:T(8,128)} custom-call(s32[3]{0:T(128)} %pad_add_fusion.place_ref, f32[128,768]{1,0:T(8,128)} %convolution_add_fusion.1.feat_ref, f32[128,32]{1,0:T(8,128)} %pad_convert_fusion.near_ref, s32[128,1]{1,0:T(8,128)} %copy.171.col_ref, s32[1,128]{1,0:T(1,128)} %bitcast.372, bf16[19,768,384]{2,1,0:T(8,128)(2,1)} %spread.1.spread_ref, ...), custom_call_target="tpu_custom_call" | custom-call | tf_op jit(solution)/shard_map/teacher/pallas_call | solution.py:875
  296.9 37.0 %student.1 = (bf16[4,128,768]{2,1,0:T(8,128)(2,1)}, bf16[3,128,3072]{2,1,0:T(8,128)(2,1)}, f32[8,4,96,548]{3,2,1,0:T(8,128)}, f32[10,768]{1,0:T(8,128)}, f32[128,512]{1,0:T(8,128)}, /*index=5*/f32[8,128]{1,0:T(8,128)}) custom-call(s32[3]{0:T(128)} %pad_add_fusion.place_ref, f32[128,768]{1,0:T(8,128)} %convolution_add_fusion.1.feat_ref, ...), custom_call_target="tpu_custom_call" | custom-call | tf_op jit(solution)/shard_map/student/pallas_call | solution.py:891
  334.4 7.1 dynamic-slice_bitcast_fusion
  343.2 10.7 %block_grads.1 = (bf16[4,2,3,48,768]{4,3,2,1,0:T(8,128)(2,1)}, f32[4,2,3,48,768]{4,3,2,1,0:T(8,128)}, bf16[4,2,3,48,768]{4,3,2,1,0:T(8,128)(2,1)}, f32[4,2,3,48,768]{4,3,2,1,0:T(8,128)}) custom-call(s32[3]{0:T(128)} %pad_add_fusion.place_ref, bf16[4,128,768]{2,1,0:T(8,128)(2,1)} %get-tuple-element.144.left_ref, bf16[4,128,768]{2,1,0:T(8,128)(2,1)} %copy-done.33, ...), custom_call_target="tpu_custom_call" | custom-call | tf_op jit(solution)/shard_map/block_grads/pallas_call | solution.py:825
  360.4 40.7 %encode_back.1 = (f32[16,256,512]{2,1,0:T(8,128)}, f32[16,256,512]{2,1,0:T(8,128)}, bf16[32,128,512]{2,1,0:T(8,128)(2,1)}, bf16[16,512]{1,0:T(8,128)(2,1)}, f32[2,512]{1,0:T(2,128)}) custom-call(s32[1]{0:T(128)} %bitcast.2.core_ref, f32[128,512]{1,0:T(8,128)} %get-tuple-element.157.grad_ref, f32[128,512]{1,0:T(8,128)} %get-tuple-element.158.unit_ref, ...), custom_call_target="tpu_custom_call" | custom-call | tf_op jit(solution)/shard_map/encode_back/pallas_call | solution.py:423
  405.4 16.6 %second_dw.1 = (f32[16,256,512]{2,1,0:T(8,128)}, f32[16,256,512]{2,1,0:T(8,128)}) custom-call(s32[1]{0:T(128)} %bitcast.2.core_ref, bf16[32,128,512]{2,1,0:T(8,128)(2,1)} %get-tuple-element.189.grad_ref, bf16[16,512]{1,0:T(8,128)(2,1)} %get-tuple-element.179.tail_grad_ref, ...), custom_call_target="tpu_custom_call", output_to_operand_aliasing={{0}: (5, {}), {1}: (6, {})} | custom-call | tf_op jit(solution)/shard_map/second_dw/pallas_call | solution.py:448
  422.0 8.1 %copy.180 = f32[4,2,2,256,512]{4,3,0,2,1:T(8,128)} copy(f32[4,2,2,256,512]{4,3,2,1,0:T(8,128)} %bitcast.355) | data formatting | bytes 16777216 | tf_op jit(solution)/shard_map/optimization_barrier | solution.py:1074
  433.9 25.8 %second_dx.1 = f32[16,512]{1,0:T(8,128)} custom-call(bf16[32,128,512]{2,1,0:T(8,128)(2,1)} %get-tuple-element.189.grad_ref, bf16[16,512]{1,0:T(8,128)(2,1)} %get-tuple-element.179.tail_grad_ref, bf16[32,368,512]{2,1,0:T(8,128)(2,1)} %bitcast.354, bf16[66,128,16]{2,1,0:T(8,128)(2,1)} %copy.167.taps_ref, bf16[16,16]{1,0:T(8,128)(2,1)} %slice_bitcast_fusion.tail_taps_ref, ...), custom_call_target="tpu_custom_call" | custom-call | tf_op jit(solution)/shard_map/second_dx/pallas_call | solution.py:464
  464.2 7.3 fusion.139
  499.8 44.9 %collective-permute-done.46 = f32[4,2,48,548]{3,2,0,1:T(8,128)} collective-permute-done((f32[4,2,48,548]{3,2,0,1:T(8,128)S(1)}, f32[4,2,48,548]{3,2,0,1:T(8,128)}, u32[]{:S(2)}, u32[]{:S(2)}) %collective-permute-start.46) | collective-permute-done | bytes 841760 | tf_op jit(solution)/shard_map/ppermute | solution.py:940
  579.5 11.6 %collective-permute-done.57 = f32[4,128,512]{2,1,0:T(8,128)S(1)} collective-permute-done((f32[4,128,512]{2,1,0:T(8,128)S(1)}, f32[4,128,512]{2,1,0:T(8,128)S(1)}, u32[]{:S(2)}, u32[]{:S(2)}) %collective-permute-start.57) | collective-permute-done | bytes 1048608 | tf_op jit(solution)/shard_map/ppermute | solution.py:940
  623.9 13.0 %collective-permute-start.59 = (f32[256,512]{1,0:T(8,128)}, f32[256,512]{1,0:T(8,128)}, u32[]{:S(2)}, u32[]{:S(2)}) collective-permute-start(f32[256,512]{1,0:T(8,128)} %get-tuple-element.246), channel_id=1, source_target_pairs={{0,8},{4,12},{8,16},{12,20},{1,9},{5,13},{9,17},{13,21},{2,10},{6,... | collective-permute-start | bytes 1572872 | tf_op jit(solution)/shard_map/ppermute | solution.py:945
  660.3 9.2 %collective-permute-done.50 = f32[96,548]{1,0:T(8,128)S(1)} collective-permute-done((f32[96,548]{1,0:T(8,128)S(1)}, f32[96,548]{1,0:T(8,128)S(1)}, u32[]{:S(2)}, u32[]{:S(2)}) %collective-permute-start.50) | collective-permute-done | bytes 210464 | tf_op jit(solution)/shard_map/ppermute | solution.py:945
  (398 shorter events, 282.2 us)
Async XLA Ops:
  7.2 114.7 %all-gather.5.cloned.1.call-start = ((), (), s32[]{:S(2)}) async-start(), calls=%async_computation | async-start | bytes 12435456 | tf_op jit(solution)/shard_map/all_gather | solution.py:1177
  10.8 245.3 %all-gather.7.cloned.1.call-start = ((), (), s32[]{:S(2)}) async-start(), calls=%async_computation.1 | async-start | bytes 14598144 | tf_op jit(solution)/shard_map/all_gather | solution.py:1004
  114.5 39.8 %collective-permute-start.11 = (bf16[4,3,96,384]{3,2,1,0:T(8,128)(2,1)}, bf16[4,3,96,384]{3,2,1,0:T(8,128)(2,1)}, u32[]{:S(2)}, u32[]{:S(2)}) collective-permute-start(bf16[4,3,96,384]{3,2,1,0:T(8,128)(2,1)} %get-tuple-element.119.refs_8_), channel_id=1, source_target_pairs={{0,1},{1,0},{2,3},{3,2},{4,5},{5,4},{6,7},{7,6},{8,9},{9,8},{10,11... | collective-permute-start | bytes 2654216 | tf_op jit(solution)/shard_map/ppermute | solution.py:940
  117.7 45.7 %collective-permute-start.8 = (bf16[4,3,96,384]{3,2,1,0:T(8,128)(2,1)}, bf16[4,3,96,384]{3,2,1,0:T(8,128)(2,1)}, u32[]{:S(2)}, u32[]{:S(2)}) collective-permute-start(bf16[4,3,96,384]{3,2,1,0:T(8,128)(2,1)} %get-tuple-element.118.refs_0_), channel_id=1, source_target_pairs={{0,4},{4,0},{8,12},{12,8},{16,20},{20,16},{24,28},{28,24},{1,5},{5... | collective-permute-start | bytes 2654216 | tf_op jit(solution)/shard_map/ppermute | solution.py:940
  118.6 44.8 %collective-permute-start.9 = (bf16[4,3,96,384]{3,2,1,0:T(8,128)(2,1)}, bf16[4,3,96,384]{3,2,1,0:T(8,128)(2,1)}, u32[]{:S(2)}, u32[]{:S(2)}) collective-permute-start(bf16[4,3,96,384]{3,2,1,0:T(8,128)(2,1)} %get-tuple-element.119.refs_8_), channel_id=1, source_target_pairs={{0,2},{1,3},{2,0},{3,1},{4,6},{5,7},{6,4},{7,5},{8,10},{9,11},{10,... | collective-permute-start | bytes 2654216 | tf_op jit(solution)/shard_map/ppermute | solution.py:940
  188.7 84.3 %collective-permute-start.18 = (bf16[4,3,96,384]{3,2,1,0:T(8,128)(2,1)}, bf16[4,3,96,384]{3,2,1,0:T(8,128)(2,1)}, u32[]{:S(2)}, u32[]{:S(2)}) collective-permute-start(bf16[4,3,96,384]{3,2,1,0:T(8,128)(2,1)} %collective-permute-done.7.refs_12_), channel_id=1, source_target_pairs={{0,2},{1,3},{2,0},{3,1},{4,6},{5,7},{6,4},{7,5},{8,10},{9,11},{10,... | collective-permute-start | bytes 2654216 | tf_op jit(solution)/shard_map/ppermute | solution.py:940
  188.7 84.3 %collective-permute-start.19 = (bf16[4,3,96,384]{3,2,1,0:T(8,128)(2,1)}, bf16[4,3,96,384]{3,2,1,0:T(8,128)(2,1)}, u32[]{:S(2)}, u32[]{:S(2)}) collective-permute-start(bf16[4,3,96,384]{3,2,1,0:T(8,128)(2,1)} %collective-permute-done.6.refs_2_), channel_id=1, source_target_pairs={{0,1},{1,0},{2,3},{3,2},{4,5},{5,4},{6,7},{7,6},{8,9},{9,8},{10,11... | collective-permute-start | bytes 2654216 | tf_op jit(solution)/shard_map/ppermute | solution.py:940
  188.7 84.3 %collective-permute-start.20 = (bf16[4,3,96,384]{3,2,1,0:T(8,128)(2,1)}, bf16[4,3,96,384]{3,2,1,0:T(8,128)(2,1)}, u32[]{:S(2)}, u32[]{:S(2)}) collective-permute-start(bf16[4,3,96,384]{3,2,1,0:T(8,128)(2,1)} %collective-permute-done.7.refs_12_), channel_id=1, source_target_pairs={{0,1},{1,0},{2,3},{3,2},{4,5},{5,4},{6,7},{7,6},{8,9},{9,8},{10,11... | collective-permute-start | bytes 2654216 | tf_op jit(solution)/shard_map/ppermute | solution.py:940
  189.2 83.8 %collective-permute-start.21 = (bf16[4,3,96,384]{3,2,1,0:T(8,128)(2,1)}, bf16[4,3,96,384]{3,2,1,0:T(8,128)(2,1)}, u32[]{:S(2)}, u32[]{:S(2)}) collective-permute-start(bf16[4,3,96,384]{3,2,1,0:T(8,128)(2,1)} %collective-permute-done.8.refs_4_), channel_id=1, source_target_pairs={{0,1},{1,0},{2,3},{3,2},{4,5},{5,4},{6,7},{7,6},{8,9},{9,8},{10,11... | collective-permute-start | bytes 2654216 | tf_op jit(solution)/shard_map/ppermute | solution.py:940
  222.7 50.3 %collective-permute-start.22 = (bf16[4,3,96,384]{3,2,1,0:T(8,128)(2,1)}, bf16[4,3,96,384]{3,2,1,0:T(8,128)(2,1)}, u32[]{:S(2)}, u32[]{:S(2)}) collective-permute-start(bf16[4,3,96,384]{3,2,1,0:T(8,128)(2,1)} %collective-permute-done.9.refs_10_), channel_id=1, source_target_pairs={{0,1},{1,0},{2,3},{3,2},{4,5},{5,4},{6,7},{7,6},{8,9},{9,8},{10,11... | collective-permute-start | bytes 2654216 | tf_op jit(solution)/shard_map/ppermute | solution.py:940
  356.9 44.2 %collective-permute-start.27 = (bf16[4,2,3,48,768]{4,3,2,0,1:T(8,128)(2,1)}, bf16[4,2,3,48,768]{4,3,2,0,1:T(8,128)(2,1)}, u32[]{:S(2)}, u32[]{:S(2)}) collective-permute-start(bf16[4,2,3,48,768]{4,3,2,0,1:T(8,128)(2,1)} %copy.176), channel_id=1, source_target_pairs={{0,4},{4,0},{8,12},{12,8},{16,20},{20,16},{24,28},{28,24},{1,5},{5... | collective-permute-start | bytes 5308424 | tf_op jit(solution)/shard_map/ppermute | solution.py:940
  360.3 40.8 %collective-permute-start.28 = (bf16[4,2,3,48,768]{4,3,2,0,1:T(8,128)(2,1)}, bf16[4,2,3,48,768]{4,3,2,0,1:T(8,128)(2,1)}, u32[]{:S(2)}, u32[]{:S(2)}) collective-permute-start(bf16[4,2,3,48,768]{4,3,2,0,1:T(8,128)(2,1)} %copy.177), channel_id=1, source_target_pairs={{0,2},{1,3},{2,0},{3,1},{4,6},{5,7},{6,4},{7,5},{8,10},{9,11},{10,... | collective-permute-start | bytes 5308424 | tf_op jit(solution)/shard_map/ppermute | solution.py:940
  430.1 48.4 %collective-permute-start.29 = (f32[4,2,2,96,548]{4,3,2,1,0:T(8,128)}, f32[4,2,2,96,548]{4,3,2,1,0:T(8,128)}, u32[]{:S(2)}, u32[]{:S(2)}) collective-permute-start(f32[4,2,2,96,548]{4,3,2,1,0:T(8,128)} %get-tuple-element.184), channel_id=1, source_target_pairs={{0,1},{1,0},{2,3},{3,2},{4,5},{5,4},{6,7},{7,6},{8,9},{9,8},{10,11... | collective-permute-start | bytes 10100744 | tf_op jit(solution)/shard_map/ppermute | solution.py:940
  431.9 46.6 %collective-permute-start.30 = (f32[4,3,48,768]{3,2,1,0:T(8,128)S(1)}, f32[4,3,48,768]{3,2,1,0:T(8,128)}, u32[]{:S(2)}, u32[]{:S(2)}) collective-permute-start(f32[4,3,48,768]{3,2,1,0:T(8,128)S(1)} %copy-done.29), channel_id=1, source_target_pairs={{0,2},{1,3},{2,0},{3,1},{4,6},{5,7},{6,4},{7,5},{8,10},{9,11},{10,... | collective-permute-start | bytes 5308424 | tf_op jit(solution)/shard_map/ppermute | solution.py:940
  433.9 44.6 %collective-permute-start.31 = (f32[4,3,48,768]{3,2,1,0:T(8,128)S(1)}, f32[4,3,48,768]{3,2,1,0:T(8,128)}, u32[]{:S(2)}, u32[]{:S(2)}) collective-permute-start(f32[4,3,48,768]{3,2,1,0:T(8,128)S(1)} %copy-done.28), channel_id=1, source_target_pairs={{0,4},{4,0},{8,12},{12,8},{16,20},{20,16},{24,28},{28,24},{1,5},{5... | collective-permute-start | bytes 5308424 | tf_op jit(solution)/shard_map/ppermute | solution.py:940
  476.1 79.0 %collective-permute-start.56 = (f32[4,2,128,512]{3,2,0,1:T(8,128)}, f32[4,2,128,512]{3,2,0,1:T(8,128)}, u32[]{:S(2)}, u32[]{:S(2)}) collective-permute-start(f32[4,2,128,512]{3,2,0,1:T(8,128)} %fusion), channel_id=1, source_target_pairs={{0,2},{1,3},{2,0},{3,1},{4,6},{5,7},{6,4},{7,5},{8,10},{9,11},{10,... | collective-permute-start | bytes 6291464 | tf_op jit(solution)/shard_map/ppermute | solution.py:940
  476.2 82.9 %collective-permute-start.54 = (f32[4,2,128,512]{3,2,0,1:T(8,128)}, f32[4,2,128,512]{3,2,0,1:T(8,128)}, u32[]{:S(2)}, u32[]{:S(2)}) collective-permute-start(f32[4,2,128,512]{3,2,0,1:T(8,128)} %fusion.1), channel_id=1, source_target_pairs={{0,4},{4,0},{8,12},{12,8},{16,20},{20,16},{24,28},{28,24},{1,5},{5... | collective-permute-start | bytes 6291464 | tf_op jit(solution)/shard_map/ppermute | solution.py:940
  484.9 59.8 %collective-permute-start.46 = (f32[4,2,48,548]{3,2,0,1:T(8,128)S(1)}, f32[4,2,48,548]{3,2,0,1:T(8,128)}, u32[]{:S(2)}, u32[]{:S(2)}) collective-permute-start(f32[4,2,48,548]{3,2,0,1:T(8,128)S(1)} %fusion.18), channel_id=1, source_target_pairs={{0,2},{1,3},{2,0},{3,1},{4,6},{5,7},{6,4},{7,5},{8,10},{9,11},{10,... | collective-permute-start | bytes 2525192 | tf_op jit(solution)/shard_map/ppermute | solution.py:940
  488.7 64.7 %collective-permute-start.44 = (f32[4,2,48,548]{3,2,0,1:T(8,128)}, f32[4,2,48,548]{3,2,0,1:T(8,128)}, u32[]{:S(2)}, u32[]{:S(2)}) collective-permute-start(f32[4,2,48,548]{3,2,0,1:T(8,128)} %add_bitcast_fusion.2), channel_id=1, source_target_pairs={{0,4},{4,0},{8,12},{12,8},{16,20},{20,16},{24,28},{28,24},{1,5},{5... | collective-permute-start | bytes 2525192 | tf_op jit(solution)/shard_map/ppermute | solution.py:940
  494.9 66.4 %collective-permute-start.38 = (f32[3,96,768]{2,1,0:T(8,128)}, f32[3,96,768]{2,1,0:T(8,128)}, u32[]{:S(2)}, u32[]{:S(2)}) collective-permute-start(f32[3,96,768]{2,1,0:T(8,128)} %get-tuple-element.240), channel_id=1, source_target_pairs={{0,8},{4,12},{1,9},{5,13},{2,10},{6,14},{3,11},{7,15}} | collective-permute-start | bytes 2654216 | tf_op jit(solution)/shard_map/ppermute | solution.py:945
  553.4 51.5 %collective-permute-start.33 = (f32[19,768]{1,0:T(8,128)S(1)}, f32[19,768]{1,0:T(8,128)}, u32[]{:S(2)}, u32[]{:S(2)}) collective-permute-start(f32[19,768]{1,0:T(8,128)S(1)} %maximum_maximum_fusion.2), channel_id=1, source_target_pairs={{0,1},{1,0},{2,3},{3,2},{4,5},{5,4},{6,7},{7,6},{8,9},{9,8},{10,11... | collective-permute-start | bytes 175112 | tf_op jit(solution)/shard_map/ppermute | solution.py:940
  569.2 54.7 %collective-permute-start.39 = (f32[3,96,768]{2,1,0:T(8,128)}, f32[3,96,768]{2,1,0:T(8,128)}, u32[]{:S(2)}, u32[]{:S(2)}) collective-permute-start(f32[3,96,768]{2,1,0:T(8,128)} %get-tuple-element.238), channel_id=1, source_target_pairs={{0,8},{4,12},{8,16},{12,20},{1,9},{5,13},{9,17},{13,21},{2,10},{6,... | collective-permute-start | bytes 2654216 | tf_op jit(solution)/shard_map/ppermute | solution.py:945
  575.5 61.3 %collective-permute-start.42 = (f32[3,96,768]{2,1,0:T(8,128)}, f32[3,96,768]{2,1,0:T(8,128)}, u32[]{:S(2)}, u32[]{:S(2)}) collective-permute-start(f32[3,96,768]{2,1,0:T(8,128)} %get-tuple-element.239), channel_id=1, source_target_pairs={{16,8},{20,12},{24,16},{28,20},{17,9},{21,13},{25,17},{29,21},{18,... | collective-permute-start | bytes 2654216 | tf_op jit(solution)/shard_map/ppermute | solution.py:945
  648.6 42.1 %collective-permute-start.35 = (f32[19,768]{1,0:T(8,128)}, f32[19,768]{1,0:T(8,128)}, u32[]{:S(2)}, u32[]{:S(2)}) collective-permute-start(f32[19,768]{1,0:T(8,128)} %add.736), channel_id=1, source_target_pairs={{0,4},{4,0},{8,12},{12,8},{16,20},{20,16},{24,28},{28,24},{1,5},{5... | collective-permute-start | bytes 175112 | tf_op jit(solution)/shard_map/ppermute | solution.py:940
  (102 other events, 1627.6 us)
Sparse Core Ops, SparseCore 0:
  11.5 110.3 all-gather.4
  125.4 130.6 all-gather.6

commit v3 on v2

--- a/solution.py
+++ b/solution.py
@@ -79,6 +79,11 @@
     )
 
 
+def gelu_both(values):
+    chance = 0.5 * (1.0 + lax.erf(values * ROOT_HALF))
+    return values * chance, chance + values * (ROOT_TAU * jnp.exp(-0.5 * values * values))
+
+
 def norm_fwd(values, gain, shift):
     center = values - jnp.mean(values, axis=-1, keepdims=True)
     scale = lax.rsqrt(jnp.mean(center * center, axis=-1, keepdims=True) + EPS)
@@ -156,9 +161,9 @@
 
         def step(index, carry, values=values, target=target, size=size, product=product):
             total = product(index)
-            values[pl.ds(index * size, size)] = total.reshape(size, frames, CH)
-            active = bf(gelu(total))
-            target[pl.ds(index * (size // 2), size // 2)] = active.reshape(
+            active, slope = gelu_both(total)
+            values[pl.ds(index * size, size)] = slope.reshape(size, frames, CH)
+            target[pl.ds(index * (size // 2), size // 2)] = bf(active).reshape(
                 size // 2, 2, frames, CH
             )
             return carry
@@ -170,8 +175,8 @@
                 lax.fori_loop(0, count // size, step, 0)
         else:
             total = product(0)
-            values[...] = total.reshape(values.shape)
-            encoded = gelu(total)
+            encoded, slope = gelu_both(total)
+            values[...] = slope.reshape(values.shape)
             normed, kept = norm_fwd(encoded, small_ref[10:11, :], small_ref[11:12, :])
             normed_ref[...] = bf(normed)
             unit_ref[...] = kept[0]
@@ -184,8 +189,8 @@
                     stack_rows(stack_ref, offset // CH + tap),
                 )
                 total = part if total is None else total + part
-            value_tail_ref[layer] = total
-            active = gelu(total)
+            active, slope = gelu_both(total)
+            value_tail_ref[layer] = slope
             tail = bf(active)
             hidden_tail_ref[layer] = tail
             head = target[0, 0].astype(F32)
@@ -262,21 +267,22 @@
     return back
 
 
-def copy_halves(core_ref, held, send_ref, keep_ref, first, taps, sem):
+def copy_halves(order, core_ref, held, send_ref, keep_ref, first, taps, sem):
     half = CH // 2
     core = core_ref[0]
     copies = []
     for tap in range(taps):
         for target, index in ((send_ref, 1 - core), (keep_ref, core)):
             start = pl.multiple_of(tap * CH + index * half, half)
+            place = order[first + tap]
             copies.append(
-                pltpu.make_async_copy(held.at[pl.ds(start, half)], target.at[first + tap], sem)
+                pltpu.make_async_copy(held.at[pl.ds(start, half)], target.at[place], sem)
             )
             copies[-1].start()
     return copies
 
 
-def encode_back_kernel(core_ref, grad_ref, unit_ref, scale_ref, small_ref, stack_ref, *refs):
+def encode_back_kernel(order, core_ref, grad_ref, unit_ref, scale_ref, small_ref, stack_ref, *refs):
     value_refs, hidden_refs = refs[:6], refs[6:11]
     value_tail_ref, hidden_tail_ref = refs[11:13]
     send_ref, keep_ref, second_ref, second_tail_ref, norm_ref = refs[13:18]
@@ -288,7 +294,7 @@
     )
     norm_ref[0:1, :] = gain[None]
     norm_ref[1:2, :] = shift[None]
-    grad_refs[5][0] = bf(grad * gelu_slope(value_refs[5][0]))
+    grad_refs[5][0] = bf(grad * value_refs[5][0])
     tail_grad = None
     offset = sum(KERNELS) * CH
     copies = [[], []]
@@ -302,7 +308,7 @@
         tail_source = None if tail_grad is None else hidden_tail_ref[layer - 1]
         layer_dw(grad_refs[layer], hidden_refs[layer - 1], tail_grad, tail_source, kernel, held)
         copies[slot] = copy_halves(
-            core_ref, held, send_ref, keep_ref, offset // CH, kernel, sems.at[slot]
+            order, core_ref, held, send_ref, keep_ref, offset // CH, kernel, sems.at[slot]
         )
         values, target = value_refs[layer - 1], grad_refs[layer - 1]
 
@@ -319,24 +325,26 @@
                     even_ref[...] = even[0]
             for item in range(size):
                 place = 2 * (index * size + item)
-                target[place] = bf(even[item] * gelu_slope(values[place]))
-                target[place + 1] = bf(odd[item] * gelu_slope(values[place + 1]))
+                target[place] = bf(even[item] * values[place])
+                target[place + 1] = bf(odd[item] * values[place + 1])
 
         back = layer_dx(grad_refs[layer], tail_grad, kernel, weight_of, None, write,
                         carry_ref, head_ref)
         tail_grad = None
         if kernel == 3:
-            target[0] = bf((even_ref[...] + head_ref[...]) * gelu_slope(values[0]))
-            tail_grad = bf(back * gelu_slope(value_tail_ref[layer - 1]))
+            target[0] = bf((even_ref[...] + head_ref[...]) * values[0])
+            tail_grad = bf(back * value_tail_ref[layer - 1])
     second_tail_ref[...] = tail_grad
     for copy in copies[0] + copies[1]:
         copy.wait()
 
 
-def second_dw_kernel(core_ref, grad_ref, tail_grad_ref, hidden_ref, tail_ref, old_send_ref,
+def second_dw_kernel(order, core_ref, grad_ref, tail_grad_ref, hidden_ref, tail_ref, old_send_ref,
                      old_keep_ref, send_ref, keep_ref, buffer_ref, sem):
     layer_dw(grad_ref, hidden_ref, tail_grad_ref[...], tail_ref[...], 3, buffer_ref)
-    for copy in copy_halves(core_ref, buffer_ref, send_ref, keep_ref, 0, 3, sem):
+    for copy in copy_halves(
+        order, core_ref, buffer_ref, send_ref, keep_ref, 0, 3, sem
+    ):
         copy.wait()
 
 
@@ -416,12 +424,12 @@
     )(hidden, hidden_tail, stack, small)
 
 
-def encode_back(core, outs, small, stack, frames, grad):
+def encode_back(order, core, outs, small, stack, frames, grad):
     shape = jax.ShapeDtypeStruct
     plane = pltpu.VMEM((frames, CH), F32)
     part = shape((sum(KERNELS), CH // 2, CH), F32)
     return pl.pallas_call(
-        encode_back_kernel,
+        lambda *refs: encode_back_kernel(order, *refs),
         in_specs=[SMEM] + [VMEM] * 18,
         out_specs=[ANY, ANY, VMEM, VMEM, VMEM],
         out_shape=[
@@ -444,9 +452,9 @@
     )(core, grad, outs[14], outs[15], small, stack, *outs[:13])
 
 
-def second_dw(core, second, second_tail, hidden, hidden_tail, parts):
+def second_dw(order, core, second, second_tail, hidden, hidden_tail, parts):
     return pl.pallas_call(
-        second_dw_kernel,
+        lambda *refs: second_dw_kernel(order, *refs),
         in_specs=[SMEM] + [VMEM] * 4 + [ANY, ANY],
         out_specs=[ANY, ANY],
         out_shape=[jax.ShapeDtypeStruct(part.shape, F32) for part in parts],
@@ -547,19 +555,31 @@
         for copy in copies:
             copy.start()
         return copies
-    line, unused, rows, lanes = piece_refs[0].shape
+    line, unused, rows, cols = piece_refs[0].shape
+    lanes = cols // 2
     x, y, c = place_ref[0], place_ref[1], place_ref[2]
+    column, one_y, two_x, one_x, two_y, one_xy, two_xy, column_c, next_c, far_c = piece_refs
+    pieces = [
+        (column, None, None, 0, 0, 0), (column_c, None, None, 0, 0, 1),
+        (one_y, None, 0, 0, 1, 0), (two_x, None, 1, 1, 0, 0),
+        (one_x, None, 0, 1, 0, 0), (two_y, None, 1, 0, 1, 0),
+        (next_c, 0, 0, 0, 1, 1), (next_c, 1, 1, 1, 0, 1),
+        (next_c, 2, 0, 1, 0, 1), (next_c, 3, 1, 0, 1, 1),
+        (one_xy, None, 0, 1, 1, 0), (two_xy, None, 1, 1, 1, 0),
+        (far_c, 0, 0, 1, 1, 1), (far_c, 1, 1, 1, 1, 1),
+    ]
     copies = []
     for matrix in range(3):
-        for number, ref in enumerate(piece_refs):
-            half, dx, dy, dc = number // 8, number // 4 % 2, number // 2 % 2, number % 2
+        for ref, index, half, dx, dy, dc in pieces:
+            width = cols if half is None else lanes
             narrow = (y ^ dy) * 2 + (c ^ dc)
-            col = pl.multiple_of((narrow * 2 + half) * lanes, 128)
+            col = pl.multiple_of(narrow * cols + (half or 0) * lanes, 128)
             for z in range(line):
                 row = pl.multiple_of((2 * z + (x ^ dx)) * rows, 16)
+                source = ref.at[z, matrix] if index is None else ref.at[index, z, matrix]
                 copy = pltpu.make_async_copy(
-                    ref.at[z, matrix],
-                    weight_ref.at[matrix, pl.ds(row, rows), pl.ds(col, lanes)],
+                    source,
+                    weight_ref.at[matrix, pl.ds(row, rows), pl.ds(col, width)],
                     sems.at[matrix],
                 )
                 copy.start()
@@ -773,28 +793,28 @@
 
 def block_grad_kernel(place_ref, left_ref, left_two_ref, right_ref, right_two_ref,
                       send_top_ref, keep_top_ref, send_low_ref, keep_low_ref, full_ref):
-    line, unused, unused_two, half, cols = keep_top_ref.shape
+    unused, line, unused_two, half, cols = keep_top_ref.shape
     x = place_ref[0]
     far = pl.program_id(1)
     full_ref[...] = t_mm(left_ref[0], right_ref[0]) + t_mm(left_two_ref[0], right_two_ref[0])
     for z in range(line):
         start = lambda index: pl.multiple_of((2 * z + index) * 2 * half, 8)
-        keep_top_ref[z, 0, 0] = full_ref[pl.ds(start(x), half), :]
-        send_top_ref[z, 0, 0] = bf(full_ref[pl.ds(start(1 - x), half), :])
+        keep_top_ref[0, z, 0] = full_ref[pl.ds(start(x), half), :]
+        send_top_ref[0, z, 0] = bf(full_ref[pl.ds(start(1 - x), half), :])
 
     @pl.when(far == 0)
     def _():
         for z in range(line):
             for index in range(2):
                 row = (2 * z + index) * 2 * half + half
-                keep_low_ref[z, index, 0] = full_ref[row : row + half, :]
+                keep_low_ref[index, z, 0] = full_ref[row : row + half, :]
 
     @pl.when(far == 1)
     def _():
         for z in range(line):
             for index in range(2):
                 row = (2 * z + index) * 2 * half + half
-                send_low_ref[z, index, 0] = bf(full_ref[row : row + half, :])
+                send_low_ref[index, z, 0] = bf(full_ref[row : row + half, :])
 
 
 def block_grads(left, left_two, right, right_two, place, n_dp, n_narrow):
@@ -816,12 +836,12 @@
         (1, frames, cols), lambda matrix, far, place: (matrix, 0, narrow(far, place))
     )
     top_spec = pl.BlockSpec(
-        (line, 1, 1, half, cols), lambda matrix, far, place: (0, place[1] ^ far, matrix, 0, 0)
+        (1, line, 1, half, cols), lambda matrix, far, place: (place[1] ^ far, 0, matrix, 0, 0)
     )
     low_spec = pl.BlockSpec(
-        (line, 2, 1, half, cols), lambda matrix, far, place: (0, 0, matrix, 0, 0)
-    )
-    whole = (line, 2, 3, half, cols)
+        (2, line, 1, half, cols), lambda matrix, far, place: (0, 0, matrix, 0, 0)
+    )
+    whole = (2, line, 3, half, cols)
     return pl.pallas_call(
         block_grad_kernel,
         grid_spec=pltpu.PrefetchScalarGridSpec(
@@ -864,10 +884,9 @@
 
 
 def flat_pieces(pieces):
-    if not isinstance(pieces, list):
-        return [pieces], pieces.shape[-1] * (pieces.shape[1] if pieces.ndim == 5 else 1)
-    flat = [piece for half in pieces for row in half for column in row for piece in column]
-    return flat, flat[0].shape[-1] * 8
+    if isinstance(pieces, list):
+        return pieces, pieces[0].shape[-1] * 4
+    return [pieces], pieces.shape[-1] * (pieces.shape[1] if pieces.ndim == 5 else 1)
 
 
 def teacher_target(feats, near, col, row, spread, vec, pieces, place):
@@ -922,7 +941,7 @@
     def __init__(self, n_dp, n_narrow):
         self.n_dp, self.n_narrow = n_dp, n_narrow
         self.line = n_dp // 2
-        self.direct = n_narrow == 4 and n_dp % 2 == 0 and self.line <= 4 and D % (16 * n_dp) == 0
+        self.direct = n_narrow == 4 and n_dp % 2 == 0 and 4 * self.line == sum(KERNELS)
         dp, narrow = lax.axis_index("dp"), lax.axis_index("narrow")
         self.z, self.x, self.y, self.c = dp // 2, dp % 2, narrow // 2, narrow % 2
 
@@ -985,17 +1004,13 @@
         column = lax.dynamic_slice_in_dim(stacked, last - self.z, self.line, 0)
         lanes = values.shape[-1] // 2
         one, two = column[..., :lanes], column[..., lanes:]
-        one_y, two_x, one_x, two_y, one_c, two_c = yield [
-            ("y", one), ("x", two), ("x", one), ("y", two), ("c", one), ("c", two)
+        one_y, two_x, one_x, two_y, column_c = yield [
+            ("y", one), ("x", two), ("x", one), ("y", two), ("c", column)
         ]
-        one_xy, two_xy, one_yc, two_xc, one_xc, two_yc = yield [
-            ("x", one_y), ("y", two_x), ("c", one_y), ("c", two_x), ("c", one_x), ("c", two_y)
-        ]
-        one_xyc, two_xyc = yield [("c", one_xy), ("c", two_xy)]
-        return [
-            [[[one, one_c], [one_y, one_yc]], [[one_x, one_xc], [one_xy, one_xyc]]],
-            [[[two, two_c], [two_y, two_yc]], [[two_x, two_xc], [two_xy, two_xyc]]],
-        ]
+        next_c = jnp.stack([one_y, two_x, one_x, two_y], 0)
+        one_xy, two_xy, next_c = yield [("x", one_y), ("y", two_x), ("c", next_c)]
+        (far_c,) = yield [("c", jnp.stack([one_xy, two_xy], 0))]
+        return [column, one_y, two_x, one_x, two_y, one_xy, two_xy, column_c, next_c, far_c]
 
     def gather_whole(self, values):
         if not self.direct:
@@ -1004,16 +1019,10 @@
         whole = lax.all_gather(values, ("dp", "narrow"), axis=0)
         return whole.reshape((self.n_dp, self.n_narrow) + values.shape)
 
-    def split(self, values):
-        values = values.reshape((self.line, 2, 2, 2) + values.shape[1:])
-        pick = lambda index: lax.dynamic_index_in_dim(values, index, 3, False)
-        return pick(1 - self.c), pick(self.c)
-
-    def scatter_steps(self, parts, coarse):
+    def scatter_steps(self, parts):
         send, keep = parts
         half = send.shape[-2] // 2
         pick = lambda array, axis, index: lax.dynamic_index_in_dim(array, index, axis, False)
-        short = bf if coarse else lambda array: array
         (got,) = yield [("c", send)]
 
         def both(rows, axis, index):
@@ -1021,7 +1030,7 @@
 
         top, low_rows = slice(0, half), slice(half, None)
         ends = yield [
-            ("x", short(both(top, 1, 1 - self.x))), ("y", short(both(low_rows, 2, 1 - self.y)))
+            ("x", both(top, 0, 1 - self.x)), ("y", both(low_rows, 1, 1 - self.y))
         ]
 
         def all_three(rows, first, at_first, second, at_second, end):
@@ -1029,17 +1038,17 @@
                 pick(pick(array[..., rows, :], first, at_first), second, at_second)
                 for array in (keep, got)
             ]
-            return mine[0] + mine[1] + pick(end, second, at_second).astype(F32)
-
-        top_of = lambda index: all_three(top, 1, self.x, 1, index, ends[0])
-        low_of = lambda index: all_three(low_rows, 2, self.y, 1, index, ends[1])
+            return mine[0] + mine[1] + pick(end, second, at_second)
+
+        top_of = lambda index: all_three(top, 0, self.x, 0, index, ends[0])
+        low_of = lambda index: all_three(low_rows, 1, self.y, 0, index, ends[1])
         more = yield [("y", top_of(1 - self.y)), ("x", low_of(1 - self.x))]
         one = top_of(self.y) + more[0]
         two = low_of(self.x) + more[1]
         return (yield from self.line_steps(jnp.concatenate([one, two], axis=-2)))
 
     def half_steps(self, send_top, keep_top, send_low, keep_low):
-        pick = lambda array, index: lax.dynamic_index_in_dim(array, index, 1, False)
+        pick = lambda array, index: lax.dynamic_index_in_dim(array, index, 0, False)
         top, lower = yield [("x", send_top), ("y", send_low)]
         top_of = lambda index: pick(keep_top, index) + pick(top, index).astype(F32)
         low_of = lambda index: pick(keep_low, index) + pick(lower, index).astype(F32)
@@ -1178,7 +1187,7 @@
     teacher_pieces = links.gather_whole(bf(teacher_block))
     masked = masked_of(span_starts)
     masked_here = jnp.full((1, 128), jnp.sum(masked.astype(F32)), F32)
-    total = jnp.maximum(links.total(masked_here)[0, 0], 1.0)
+    masked_all = links.total(masked_here)
     small_low = low(conv_small)
     vector_low = low(vectors)
     taps = first_taps(wave, frames)
@@ -1198,6 +1207,7 @@
         for unused in range(links.line - 2):
             exchange.advance()
         hidden = exchange.tie(hidden)
+        hidden, masked_all = lax.optimization_barrier((hidden, masked_all))
         outs = encode_fwd(small_low, stack, hidden, hidden_tail, frames)
         outs = list(outs)
         outs[13] = exchange.advance((outs[13],))
@@ -1219,6 +1229,7 @@
     if links.direct:
         target = exchange.advance((target,))
         (student_pieces,) = exchange.finish()
+    total = jnp.maximum(masked_all[0, 0], 1.0)
     weight = jnp.full((8, 128), 1.0 / (total * math.sqrt(D)), F32)
     left, right, side_grad, vector_grad, normed_grad, loss_tile = student_step(
         feats,
@@ -1243,33 +1254,36 @@
     devices = n_dp * n_narrow
     if links.direct:
         core = links.c.astype(jnp.int32).reshape(1)
+        order = [tap // 2 % 2 * 8 + tap % 2 * 4 + tap // 4 for tap in range(sum(KERNELS))]
         others = [links.swap_c(left), links.swap_c(right)]
-        parts = links.split(side_grad.reshape(devices, side_rows, side_cols))
-        others, parts = lax.optimization_barrier((others, parts))
+        side_piece = lax.psum_scatter(
+            side_grad.reshape(devices * side_rows, side_cols),
+            everyone,
+            scatter_dimension=0,
+            tiled=True,
+        )
         grads = block_grads(left, others[0], right, others[1], place, n_dp, n_narrow)
         feed = Stages(links, [links.half_steps(*grads)])
         normed_grad = feed.tie(normed_grad)
-        *parts_two, second, second_tail, norm_grad = encode_back(
-            core, outs, small_low, stack, frames, normed_grad
+        *parts, second, second_tail, norm_grad = encode_back(
+            order, core, outs, small_low, stack, frames, normed_grad
         )
+        parts = second_dw(order, core, second, second_tail, hidden, hidden_tail, parts)
+        parts = feed.advance(tuple(parts))
+        second = feed.tie(second)
+        shape = (2, 2, links.line) + conv_stack.shape
+        last = Stages(links, [links.scatter_steps([part.reshape(shape) for part in parts])])
+        second = last.tie(second)
+        second = last.advance((second,))
+        second = last.tie(second)
         second = feed.advance((second,))
         second = feed.tie(second)
-        parts_two = second_dw(core, second, second_tail, hidden, hidden_tail, parts_two)
-        shape = (links.line, 2, 2) + conv_stack.shape
-        last = Stages(
-            links, [links.scatter_steps([part.reshape(shape) for part in parts_two], False)]
-        )
-        second = last.tie(second)
-        parts, second = lax.optimization_barrier((parts, second))
-        rest = Stages(links, [links.scatter_steps(parts, False)])
         tap_grad = second_dx(second, second_tail, stack, taps, first_weights, frames)
-        tap_grad = last.advance((tap_grad,))
-        tap_grad = last.tie(tap_grad)
-        tap_grad = feed.advance((tap_grad,))
-        tap_grad = rest.advance((tap_grad,))
+        for one in (feed, last, feed, last):
+            tap_grad = one.advance((tap_grad,))
+            tap_grad = one.tie(tap_grad)
+        (block_piece,) = feed.finish()
         (stack_piece,) = last.finish()
-        (block_piece,) = feed.finish()
-        (side_piece,) = rest.finish()
     else:
         sums = lambda values: lax.psum_scatter(
             values.reshape((-1,) + values.shape[-1:]), everyone, scatter_dimension=0, tiled=True
@@ -1279,10 +1293,11 @@
         side_grad = side_grad.reshape(n_dp, side_rows, n_narrow, side_cols)
         side_piece = sums(side_grad.transpose(0, 2, 1, 3))
         core = jnp.zeros((1,), jnp.int32)
+        order = list(range(sum(KERNELS)))
         *parts, second, second_tail, norm_grad = encode_back(
-            core, outs, small_low, stack, frames, normed_grad
+            order, core, outs, small_low, stack, frames, normed_grad
         )
-        parts = second_dw(core, second, second_tail, hidden, hidden_tail, parts)
+        parts = second_dw(order, core, second, second_tail, hidden, hidden_tail, parts)
         tap_grad = second_dx(second, second_tail, stack, taps, first_weights, frames)
         stack_piece = sums(jnp.stack([parts[1], parts[0]], 1).reshape(sum(KERNELS) * CH, CH))
     small_grad = jnp.concatenate([tap_grad[:10], norm_grad], axis=0)

time: 750 us -> 670 us (0.89)
  waiting for transfers between devices: 214 us -> 181 us
  local copies, waits for them, and re-layouts: 97.6 us -> 71.6 us
  starting transfers between devices: 112 us -> 89.3 us
    ppermute x47 -> x37, waiting for transfers between devices: 128 us -> 85.1 us  [flip(): return lax.ppermute(values, axis, [(i, i ^ bit) for i in range(size)])]
    ppermute x24 -> x18, starting transfers between devices: 74.8 us -> 47.3 us  [step_z(): return lax.ppermute(values, 'dp', pairs)]
    optimization_barrier x4 -> x0, local copies, waits for them, and re-layouts: 15.6 us -> none  [the longest x3 12.5 us: tie(): arrays, others = lax.optimization_barrier((arrays, others))]
    all_gather x1, waiting for transfers between devices: 11.3 us -> 21.8 us  [gather_whole(): whole = lax.all_gather(values, ('dp', 'narrow'), axis=0)]
    add x6 -> x2, other arithmetic: 14.4 us -> 3.87 us  [line_steps(): send_up = at(hop) if up is None else at(hop) + up]
    add x4 -> x5, other arithmetic: 7.04 us -> 14.9 us  [the longest x2 6.49 us: all_three(): return mine[0] + mine[1] + pick(end, second, at_second)]
    ppermute x47 -> x37, starting transfers between devices: 37.6 us -> 41.9 us  [flip(): return lax.ppermute(values, axis, [(i, i ^ bit) for i in range(size)])]
    ppermute x24 -> x18, waiting for transfers between devices: 73.6 us -> 73.7 us  [step_z(): return lax.ppermute(values, 'dp', pairs)]
  transfers between devices with their start and end apart: 73 -> 58, of which waited for: 24 -> 25; matrix products, arithmetic and copies ran while one was open for 21% -> 21% of each run, Pallas kernels for 19% -> 24%
where the time goes in v3:
time: 670 us; the launch traced here: 660 us
  Pallas kernels  207 us (31%)
  waiting for transfers between devices  181 us (27%)
  starting transfers between devices  89.3 us (13%)
  other arithmetic  79.7 us (12%)
  local copies, waits for them, and re-layouts  71.6 us (11%)
  between operations  20.8 us (3%)
  matrix products  10.6 us (2%)
    ppermute x37, waiting for transfers between devices, flip(): return lax.ppermute(values, axis, [(i, i ^ bit) for i in range(size)])  85.1 us
    ppermute x18, waiting for transfers between devices, step_z(): return lax.ppermute(values, 'dp', pairs)  73.7 us
    ppermute x18, starting transfers between devices, step_z(): return lax.ppermute(values, 'dp', pairs)  47.3 us
    ppermute x37, starting transfers between devices, flip(): return lax.ppermute(values, axis, [(i, i ^ bit) for i in range(size)])  41.9 us
    pallas_call x1, Pallas kernels, student_step(): pl.pallas_call(student_kernel, in_specs=[SMEM] + [VMEM] * 12 + [ANY] * le...  36.9 us
    pallas_call x1, Pallas kernels, encode_back(): pl.pallas_call(lambda *refs: encode_back_kernel(order, *refs), in_specs=[...  35.4 us
    pallas_call x1, Pallas kernels, encode_fwd(): pl.pallas_call(encode_kernel, in_specs=[VMEM] * 4, out_specs=[VMEM] * 16,...  34.7 us
    pallas_call x1, Pallas kernels, second_dx(): pl.pallas_call(second_dx_kernel, grid=(1,), in_specs=[VMEM, VMEM, pl.Bloc...  26.6 us
  transfers between devices with their start and end apart: 58, of which 25 were waited for; matrix products, arithmetic and copies ran while one was open for 21% of the time, Pallas kernels for 24%

profile of v3, /device:TPU:0, one launch (start us, length us, event | category | flops | bytes accessed | tf_op | source)
XLA Modules:
  0.0 659.8 jit_solution(13245023133170960143)
XLA Ops:
  13.9 6.3 collective-permute-start
  28.7 20.9 %first_layer.1.hidden_ref.refs_3_ = bf16[33,2,128,512]{3,2,1,0:T(8,128)(2,1)} custom-call(bf16[66,128,16]{2,1,0:T(8,128)(2,1)} %copy.118.taps_ref, bf16[16,512]{1,0:T(8,128)(2,1)} %pad.27.weight_ref.first_ref), custom_call_target="tpu_custom_call" | custom-call | tf_op jit(solution)/shard_map/first_layer/pallas_call | solution.py:393
  53.8 20.1 %collective-permute-done.4 = bf16[3,96,768]{2,1,0:T(8,128)(2,1)S(1)} collective-permute-done((bf16[3,96,768]{2,1,0:T(8,128)(2,1)}, bf16[3,96,768]{2,1,0:T(8,128)(2,1)S(1)}, u32[]{:S(2)}, u32[]{:S(2)}) %collective-permute-start.4) | collective-permute-done | bytes 442400 | tf_op jit(solution)/shard_map/ppermute | solution.py:964
  79.4 33.3 %collective-permute-done.5 = bf16[3,96,768]{2,1,0:T(8,128)(2,1)S(1)} collective-permute-done((bf16[3,96,768]{2,1,0:T(8,128)(2,1)S(1)}, bf16[3,96,768]{2,1,0:T(8,128)(2,1)S(1)}, u32[]{:S(2)}, u32[]{:S(2)}) %collective-permute-start.5) | collective-permute-done | bytes 442400 | tf_op jit(solution)/shard_map/ppermute | solution.py:964
  145.7 9.9 %reshape.181 = bf16[8,4,96,548]{3,2,1,0:T(8,128)(2,1)} reshape(bf16[32,52608]{1,0:T(8,128)(2,1)S(1)} %slice.239) | data formatting | bytes 6733824 | tf_op jit(solution)/shard_map/reshape | solution.py:1199
  155.6 6.1 copy.131
  161.8 6.1 reshape.182
  167.9 34.7 %encode.1 = (f32[32,128,512]{2,1,0:T(8,128)}, f32[16,128,512]{2,1,0:T(8,128)}, f32[8,128,512]{2,1,0:T(8,128)}, f32[4,128,512]{2,1,0:T(8,128)}, f32[2,128,512]{2,...) custom-call(bf16[33,2,128,512]{3,2,1,0:T(8,128)(2,1)} %first_layer.1, ...), custom_call_target="tpu_custom_call" | custom-call | tf_op jit(solution)/shard_map/encode/pallas_call | solution.py:409
  222.0 8.6 %spread.1.spread_ref = bf16[19,768,384]{2,1,0:T(8,128)(2,1)} custom-call(bf16[768,912]{1,0:T(8,128)(2,1)} %slice.219.side_ref, bf16[48,384]{1,0:T(8,128)(2,1)} %constant.486.clone.tile_ref), custom_call_target="tpu_custom_call" | custom-call | tf_op jit(solution)/shard_map/spread/pallas_call | solution.py:876
  231.7 21.8 %all-gather.7.cloned.1.call-done = bf16[96,96,768]{2,1,0:T(8,128)(2,1)} async-done(((bf16[3,96,768]{2,1,0:T(8,128)(2,1)}), bf16[96,96,768]{2,1,0:T(8,128)(2,1)}) %all-gather.7.cloned.1.call-update) | async-done | bytes 14155792 | tf_op jit(solution)/shard_map/all_gather | solution.py:1019
  253.6 16.6 %teacher.1.target_ref = f32[128,768]{1,0:T(8,128)} custom-call(s32[3]{0:T(128)} %pad_add_fusion.place_ref, f32[128,768]{1,0:T(8,128)} %convolution_add_fusion.1.feat_ref, f32[128,32]{1,0:T(8,128)} %pad_convert_fusion.near_ref, s32[128,1]{1,0:T(8,128)} %copy.122.col_ref, s32[1,128]{1,0:T(1,128)} %bitcast.267, bf16[19,768,384]{2,1,0:T(8,128)(2,1)} %spread.1.spread_ref, ...), custom_call_target="tpu_custom_call" | custom-call | tf_op jit(solution)/shard_map/teacher/pallas_call | solution.py:894
  278.0 36.9 %student.1 = (bf16[4,128,768]{2,1,0:T(8,128)(2,1)}, bf16[3,128,3072]{2,1,0:T(8,128)(2,1)}, f32[8,4,96,548]{3,2,1,0:T(8,128)}, f32[10,768]{1,0:T(8,128)}, f32[128,512]{1,0:T(8,128)}, /*index=5*/f32[8,128]{1,0:T(8,128)}) custom-call(s32[3]{0:T(128)} %pad_add_fusion.place_ref, f32[128,768]{1,0:T(8,128)} %convolution_add_fusion.1.feat_ref, ...), custom_call_target="tpu_custom_call" | custom-call | tf_op jit(solution)/shard_map/student/pallas_call | solution.py:910
  315.5 5.4 collective-permute-done.20.left_two_ref
  323.2 10.6 %block_grads.1 = (bf16[2,4,3,48,768]{4,3,2,1,0:T(8,128)(2,1)}, f32[2,4,3,48,768]{4,3,2,1,0:T(8,128)}, bf16[2,4,3,48,768]{4,3,2,1,0:T(8,128)(2,1)}, f32[2,4,3,48,768]{4,3,2,1,0:T(8,128)}) custom-call(s32[3]{0:T(128)} %pad_add_fusion.place_ref, bf16[4,128,768]{2,1,0:T(8,128)(2,1)} %get-tuple-element.151.left_ref, bf16[4,128,768]{2,1,0:T(8,128)(2,1)} %copy-done.20, ...), custom_call_target="tpu_custom_call" | custom-call | tf_op jit(solution)/shard_map/block_grads/pallas_call | solution.py:845
  336.3 35.4 %encode_back.1 = (f32[16,256,512]{2,1,0:T(8,128)}, f32[16,256,512]{2,1,0:T(8,128)}, bf16[32,128,512]{2,1,0:T(8,128)(2,1)}, bf16[16,512]{1,0:T(8,128)(2,1)}, f32[2,512]{1,0:T(2,128)}) custom-call(s32[1]{0:T(128)} %bitcast.2.refs_0_, f32[128,512]{1,0:T(8,128)} %get-tuple-element.158.refs_1_, f32[128,512]{1,0:T(8,128)} %get-tuple-element.159.refs_2_, ...), custom_call_target="tpu_custom_call" | custom-call | tf_op jit(solution)/shard_map/encode_back/pallas_call | solution.py:431
  371.7 16.9 %second_dw.1 = (f32[16,256,512]{2,1,0:T(8,128)}, f32[16,256,512]{2,1,0:T(8,128)}) custom-call(s32[1]{0:T(128)} %bitcast.2.refs_0_, bf16[32,128,512]{2,1,0:T(8,128)(2,1)} %get-tuple-element.201.refs_1_.grad_ref, bf16[16,512]{1,0:T(8,128)(2,1)} %get-tuple-element.175.refs_2_.tail_grad_ref, ...), custom_call_target="tpu_custom_call", output_to_operand_aliasing={{0}: (5, {}), {1}: (6, {})} | custom-call | tf_op jit(solution)/shard_map/second_dw/pallas_call | solution.py:456
  400.8 5.5 collective-permute-done.24
  417.6 18.1 %collective-permute-done.27 = f32[4,3,48,768]{3,2,1,0:T(8,128)} collective-permute-done((f32[4,3,48,768]{3,2,1,0:T(8,128)S(1)}, f32[4,3,48,768]{3,2,1,0:T(8,128)}, u32[]{:S(2)}, u32[]{:S(2)}) %collective-permute-start.27) | collective-permute-done | bytes 1769504 | tf_op jit(solution)/shard_map/ppermute | solution.py:959
  448.5 26.6 %second_dx.1 = f32[16,512]{1,0:T(8,128)} custom-call(bf16[32,128,512]{2,1,0:T(8,128)(2,1)} %get-tuple-element.201.refs_1_.grad_ref, bf16[16,512]{1,0:T(8,128)(2,1)} %get-tuple-element.175.refs_2_.tail_grad_ref, bf16[32,368,512]{2,1,0:T(8,128)(2,1)} %bitcast.250, bf16[66,128,16]{2,1,0:T(8,128)(2,1)} %copy.118.taps_ref, ...), custom_call_target="tpu_custom_call" | custom-call | tf_op jit(solution)/shard_map/second_dx/pallas_call | solution.py:472
  483.0 11.8 %collective-permute-done.25 = f32[2,4,128,512]{3,2,1,0:T(8,128)} collective-permute-done((f32[2,4,128,512]{3,2,1,0:T(8,128)}, f32[2,4,128,512]{3,2,1,0:T(8,128)}, u32[]{:S(2)}, u32[]{:S(2)}) %collective-permute-start.25) | collective-permute-done | bytes 2097184 | tf_op jit(solution)/shard_map/ppermute | solution.py:959
  512.1 21.0 %collective-permute-done.31 = f32[4,128,512]{2,1,0:T(8,128)} collective-permute-done((f32[4,128,512]{2,1,0:T(8,128)}, f32[4,128,512]{2,1,0:T(8,128)}, u32[]{:S(2)}, u32[]{:S(2)}) %collective-permute-start.31) | collective-permute-done | bytes 1048608 | tf_op jit(solution)/shard_map/ppermute | solution.py:959
  542.0 12.1 %collective-permute-done.42 = f32[256,512]{1,0:T(8,128)S(1)} collective-permute-done((f32[256,512]{1,0:T(8,128)S(1)}, f32[256,512]{1,0:T(8,128)S(1)}, u32[]{:S(2)}, u32[]{:S(2)}) %collective-permute-start.42) | collective-permute-done | bytes 524320 | tf_op jit(solution)/shard_map/ppermute | solution.py:964
  575.9 8.2 %collective-permute-start.44 = (f32[256,512]{1,0:T(8,128)}, f32[256,512]{1,0:T(8,128)}, u32[]{:S(2)}, u32[]{:S(2)}) collective-permute-start(f32[256,512]{1,0:T(8,128)} %get-tuple-element.264), channel_id=1, source_target_pairs={{0,8},{4,12},{8,16},{12,20},{16,24},{20,28},{1,9},{5,13},{9,17},{1... | collective-permute-start | bytes 1572872 | tf_op jit(solution)/shard_map/ppermute | solution.py:964
  604.2 5.6 collective-permute-start.38
  (325 shorter events, 240.5 us)
Async XLA Ops:
  7.2 134.8 %all-gather.5.cloned.1.call-start = ((), (), s32[]{:S(2)}) async-start(), calls=%async_computation.2 | async-start | bytes 12435456 | tf_op jit(solution)/shard_map/all_gather | solution.py:1186
  10.8 242.7 %all-gather.7.cloned.1.call-start = ((), (), s32[]{:S(2)}) async-start(), calls=%async_computation.3 | async-start | bytes 14598144 | tf_op jit(solution)/shard_map/all_gather | solution.py:1019
  11.7 573.9 %reduce-scatter.2.cloned.1.call-start = ((), (), s32[]{:S(2)}) async-start(), calls=%async_computation.1 | async-start | bytes 8110080 | tf_op jit(solution)/shard_map/reduce_scatter | solution.py:1259
  12.6 37.0 %collective-permute-start.1 = (bf16[3,96,768]{2,1,0:T(8,128)(2,1)}, bf16[3,96,768]{2,1,0:T(8,128)(2,1)}, u32[]{:S(2)}, u32[]{:S(2)}) collective-permute-start(bf16[3,96,768]{2,1,0:T(8,128)(2,1)} %convert_element_type.82), channel_id=1, source_target_pairs={{8,0},{12,4},{16,8},{20,12},{24,16},{28,20},{9,1},{13,5},{17,9},{2... | collective-permute-start | bytes 1327112 | tf_op jit(solution)/shard_map/ppermute | solution.py:964
  13.9 35.7 %collective-permute-start = (bf16[3,96,768]{2,1,0:T(8,128)(2,1)}, bf16[3,96,768]{2,1,0:T(8,128)(2,1)}, u32[]{:S(2)}, u32[]{:S(2)}) collective-permute-start(bf16[3,96,768]{2,1,0:T(8,128)(2,1)} %convert_element_type.82), channel_id=1, source_target_pairs={{0,8},{4,12},{8,16},{12,20},{16,24},{20,28},{1,9},{5,13},{9,17},{1... | collective-permute-start | bytes 1327112 | tf_op jit(solution)/shard_map/ppermute | solution.py:964
  73.9 38.9 %collective-permute-start.5 = (bf16[3,96,768]{2,1,0:T(8,128)(2,1)S(1)}, bf16[3,96,768]{2,1,0:T(8,128)(2,1)S(1)}, u32[]{:S(2)}, u32[]{:S(2)}) collective-permute-start(bf16[3,96,768]{2,1,0:T(8,128)(2,1)S(1)} %collective-permute-done.4), channel_id=1, source_target_pairs={{8,0},{12,4},{9,1},{13,5},{10,2},{14,6},{11,3},{15,7}} | collective-permute-start | bytes 1327112 | tf_op jit(solution)/shard_map/ppermute | solution.py:964
  115.5 87.1 %collective-permute-start.10 = (bf16[4,3,96,768]{3,2,1,0:T(8,128)(2,1)}, bf16[4,3,96,768]{3,2,1,0:T(8,128)(2,1)}, u32[]{:S(2)}, u32[]{:S(2)}) collective-permute-start(bf16[4,3,96,768]{3,2,1,0:T(8,128)(2,1)} %constant_dynamic-slice_fusion.2.refs_0_), channel_id=1, source_target_pairs={{0,1},{1,0},{2,3},{3,2},{4,5},{5,4},{6,7},{7,6},{8,9},{9,8},{10,11... | collective-permute-start | bytes 5308424 | tf_op jit(solution)/shard_map/ppermute | solution.py:959
  136.0 66.6 %collective-permute-start.6 = (bf16[4,3,96,384]{3,2,1,0:T(8,128)(2,1)}, bf16[4,3,96,384]{3,2,1,0:T(8,128)(2,1)}, u32[]{:S(2)}, u32[]{:S(2)}) collective-permute-start(bf16[4,3,96,384]{3,2,1,0:T(8,128)(2,1)} %get-tuple-element.129), channel_id=1, source_target_pairs={{0,2},{1,3},{2,0},{3,1},{4,6},{5,7},{6,4},{7,5},{8,10},{9,11},{10,... | collective-permute-start | bytes 2654216 | tf_op jit(solution)/shard_map/ppermute | solution.py:959
  137.6 65.0 %collective-permute-start.7 = (bf16[4,3,96,384]{3,2,1,0:T(8,128)(2,1)}, bf16[4,3,96,384]{3,2,1,0:T(8,128)(2,1)}, u32[]{:S(2)}, u32[]{:S(2)}) collective-permute-start(bf16[4,3,96,384]{3,2,1,0:T(8,128)(2,1)} %get-tuple-element.130), channel_id=1, source_target_pairs={{0,4},{4,0},{8,12},{12,8},{16,20},{20,16},{24,28},{28,24},{1,5},{5... | collective-permute-start | bytes 2654216 | tf_op jit(solution)/shard_map/ppermute | solution.py:959
  139.1 63.5 %collective-permute-start.8 = (bf16[4,3,96,384]{3,2,1,0:T(8,128)(2,1)}, bf16[4,3,96,384]{3,2,1,0:T(8,128)(2,1)}, u32[]{:S(2)}, u32[]{:S(2)}) collective-permute-start(bf16[4,3,96,384]{3,2,1,0:T(8,128)(2,1)} %get-tuple-element.129), channel_id=1, source_target_pairs={{0,4},{4,0},{8,12},{12,8},{16,20},{20,16},{24,28},{28,24},{1,5},{5... | collective-permute-start | bytes 2654216 | tf_op jit(solution)/shard_map/ppermute | solution.py:959
  139.7 63.0 %collective-permute-start.9 = (bf16[4,3,96,384]{3,2,1,0:T(8,128)(2,1)}, bf16[4,3,96,384]{3,2,1,0:T(8,128)(2,1)}, u32[]{:S(2)}, u32[]{:S(2)}) collective-permute-start(bf16[4,3,96,384]{3,2,1,0:T(8,128)(2,1)} %get-tuple-element.130), channel_id=1, source_target_pairs={{0,2},{1,3},{2,0},{3,1},{4,6},{5,7},{6,4},{7,5},{8,10},{9,11},{10,... | collective-permute-start | bytes 2654216 | tf_op jit(solution)/shard_map/ppermute | solution.py:959
  206.3 63.9 %collective-permute-start.18 = (bf16[4,4,3,96,384]{4,3,2,1,0:T(8,128)(2,1)}, bf16[4,4,3,96,384]{4,3,2,1,0:T(8,128)(2,1)}, u32[]{:S(2)}, u32[]{:S(2)}) collective-permute-start(bf16[4,4,3,96,384]{4,3,2,1,0:T(8,128)(2,1)} %pad_maximum_fusion), channel_id=1, source_target_pairs={{0,1},{1,0},{2,3},{3,2},{4,5},{5,4},{6,7},{7,6},{8,9},{9,8},{10,11... | collective-permute-start | bytes 10616840 | tf_op jit(solution)/shard_map/ppermute | solution.py:959
  206.4 63.8 %collective-permute-start.16 = (bf16[4,3,96,384]{3,2,1,0:T(8,128)(2,1)}, bf16[4,3,96,384]{3,2,1,0:T(8,128)(2,1)}, u32[]{:S(2)}, u32[]{:S(2)}) collective-permute-start(bf16[4,3,96,384]{3,2,1,0:T(8,128)(2,1)} %collective-permute-done.6.refs_1_), channel_id=1, source_target_pairs={{0,4},{4,0},{8,12},{12,8},{16,20},{20,16},{24,28},{28,24},{1,5},{5... | collective-permute-start | bytes 2654216 | tf_op jit(solution)/shard_map/ppermute | solution.py:959
  208.1 62.1 %collective-permute-start.17 = (bf16[4,3,96,384]{3,2,1,0:T(8,128)(2,1)}, bf16[4,3,96,384]{3,2,1,0:T(8,128)(2,1)}, u32[]{:S(2)}, u32[]{:S(2)}) collective-permute-start(bf16[4,3,96,384]{3,2,1,0:T(8,128)(2,1)} %collective-permute-done.7.refs_2_), channel_id=1, source_target_pairs={{0,2},{1,3},{2,0},{3,1},{4,6},{5,7},{6,4},{7,5},{8,10},{9,11},{10,... | collective-permute-start | bytes 2654216 | tf_op jit(solution)/shard_map/ppermute | solution.py:959
  333.8 54.8 %collective-permute-start.22 = (bf16[2,4,3,48,768]{4,3,2,1,0:T(8,128)(2,1)}, bf16[2,4,3,48,768]{4,3,2,1,0:T(8,128)(2,1)}, u32[]{:S(2)}, u32[]{:S(2)}) collective-permute-start(bf16[2,4,3,48,768]{4,3,2,1,0:T(8,128)(2,1)} %get-tuple-element.156), channel_id=1, source_target_pairs={{0,4},{4,0},{8,12},{12,8},{16,20},{20,16},{24,28},{28,24},{1,5},{5... | collective-permute-start | bytes 5308424 | tf_op jit(solution)/shard_map/ppermute | solution.py:959
  334.9 53.7 %collective-permute-start.23 = (bf16[2,4,3,48,768]{4,3,2,1,0:T(8,128)(2,1)}, bf16[2,4,3,48,768]{4,3,2,1,0:T(8,128)(2,1)}, u32[]{:S(2)}, u32[]{:S(2)}) collective-permute-start(bf16[2,4,3,48,768]{4,3,2,1,0:T(8,128)(2,1)} %get-tuple-element.157), channel_id=1, source_target_pairs={{0,2},{1,3},{2,0},{3,1},{4,6},{5,7},{6,4},{7,5},{8,10},{9,11},{10,... | collective-permute-start | bytes 5308424 | tf_op jit(solution)/shard_map/ppermute | solution.py:959
  394.3 41.5 %collective-permute-start.27 = (f32[4,3,48,768]{3,2,1,0:T(8,128)S(1)}, f32[4,3,48,768]{3,2,1,0:T(8,128)}, u32[]{:S(2)}, u32[]{:S(2)}) collective-permute-start(f32[4,3,48,768]{3,2,1,0:T(8,128)S(1)} %copy-done.17), channel_id=1, source_target_pairs={{0,2},{1,3},{2,0},{3,1},{4,6},{5,7},{6,4},{7,5},{8,10},{9,11},{10,... | collective-permute-start | bytes 5308424 | tf_op jit(solution)/shard_map/ppermute | solution.py:959
  395.0 41.5 %collective-permute-start.28 = (f32[4,3,48,768]{3,2,1,0:T(8,128)S(1)}, f32[4,3,48,768]{3,2,1,0:T(8,128)}, u32[]{:S(2)}, u32[]{:S(2)}) collective-permute-start(f32[4,3,48,768]{3,2,1,0:T(8,128)S(1)} %add_bitcast_fusion.2), channel_id=1, source_target_pairs={{0,4},{4,0},{8,12},{12,8},{16,20},{20,16},{24,28},{28,24},{1,5},{5... | collective-permute-start | bytes 5308424 | tf_op jit(solution)/shard_map/ppermute | solution.py:959
  415.7 79.1 %collective-permute-start.25 = (f32[2,4,128,512]{3,2,1,0:T(8,128)}, f32[2,4,128,512]{3,2,1,0:T(8,128)}, u32[]{:S(2)}, u32[]{:S(2)}) collective-permute-start(f32[2,4,128,512]{3,2,1,0:T(8,128)} %add_bitcast_fusion.1), channel_id=1, source_target_pairs={{0,4},{4,0},{8,12},{12,8},{16,20},{20,16},{24,28},{28,24},{1,5},{5... | collective-permute-start | bytes 6291464 | tf_op jit(solution)/shard_map/ppermute | solution.py:959
  417.6 77.2 %collective-permute-start.26 = (f32[2,4,128,512]{3,2,1,0:T(8,128)}, f32[2,4,128,512]{3,2,1,0:T(8,128)}, u32[]{:S(2)}, u32[]{:S(2)}) collective-permute-start(f32[2,4,128,512]{3,2,1,0:T(8,128)} %add_bitcast_fusion), channel_id=1, source_target_pairs={{0,2},{1,3},{2,0},{3,1},{4,6},{5,7},{6,4},{7,5},{8,10},{9,11},{10,... | collective-permute-start | bytes 6291464 | tf_op jit(solution)/shard_map/ppermute | solution.py:959
  442.5 32.6 %collective-permute-start.29 = (f32[3,96,768]{2,1,0:T(8,128)}, f32[3,96,768]{2,1,0:T(8,128)}, u32[]{:S(2)}, u32[]{:S(2)}) collective-permute-start(f32[3,96,768]{2,1,0:T(8,128)} %get-tuple-element.199), channel_id=1, source_target_pairs={{0,8},{4,12},{1,9},{5,13},{2,10},{6,14},{3,11},{7,15}} | collective-permute-start | bytes 2654216 | tf_op jit(solution)/shard_map/ppermute | solution.py:964
  477.9 31.3 %collective-permute-start.33 = (f32[3,96,768]{2,1,0:T(8,128)}, f32[3,96,768]{2,1,0:T(8,128)}, u32[]{:S(2)}, u32[]{:S(2)}) collective-permute-start(f32[3,96,768]{2,1,0:T(8,128)} %get-tuple-element.211), channel_id=1, source_target_pairs={{0,8},{4,12},{8,16},{12,20},{1,9},{5,13},{9,17},{13,21},{2,10},{6,... | collective-permute-start | bytes 2654216 | tf_op jit(solution)/shard_map/ppermute | solution.py:964
  501.3 31.9 %collective-permute-start.31 = (f32[4,128,512]{2,1,0:T(8,128)}, f32[4,128,512]{2,1,0:T(8,128)}, u32[]{:S(2)}, u32[]{:S(2)}) collective-permute-start(f32[4,128,512]{2,1,0:T(8,128)} %bitcast_add_fusion.4), channel_id=1, source_target_pairs={{0,2},{1,3},{2,0},{3,1},{4,6},{5,7},{6,4},{7,5},{8,10},{9,11},{10,... | collective-permute-start | bytes 3145736 | tf_op jit(solution)/shard_map/ppermute | solution.py:959
  502.8 30.3 %collective-permute-start.32 = (f32[4,128,512]{2,1,0:T(8,128)}, f32[4,128,512]{2,1,0:T(8,128)}, u32[]{:S(2)}, u32[]{:S(2)}) collective-permute-start(f32[4,128,512]{2,1,0:T(8,128)} %bitcast_add_fusion.3), channel_id=1, source_target_pairs={{0,4},{4,0},{8,12},{12,8},{16,20},{20,16},{24,28},{28,24},{1,5},{5... | collective-permute-start | bytes 3145736 | tf_op jit(solution)/shard_map/ppermute | solution.py:959
  (72 other events, 886.9 us)
Sparse Core Ops, SparseCore 0:
  11.5 110.2 all-gather.4
  125.3 128.2 all-gather.6
  393.0 156.4 reduce-scatter.1

commit v4 on v3

--- a/solution.py
+++ b/solution.py
@@ -283,11 +283,29 @@
 
 
 def encode_back_kernel(order, core_ref, grad_ref, unit_ref, scale_ref, small_ref, stack_ref, *refs):
-    value_refs, hidden_refs = refs[:6], refs[6:11]
+    value_sources, hidden_sources = refs[:6], refs[6:11]
     value_tail_ref, hidden_tail_ref = refs[11:13]
     send_ref, keep_ref, second_ref, second_tail_ref, norm_ref = refs[13:18]
     grad_refs = (second_ref,) + refs[18:23]
-    buffer_ref, carry_ref, head_ref, even_ref, sems = refs[23:]
+    buffer_ref, carry_ref, head_ref, even_ref, sems = refs[23:28]
+    value_refs = refs[28:33] + (value_sources[5],)
+    hidden_refs, stack_copy, in_sems = refs[33:38], refs[38], refs[39]
+    each = stack_ref.shape[0] // sum(KERNELS)
+    fetches = [None] * 6
+    first_tap = sum(KERNELS)
+    for layer in range(5, 0, -1):
+        first_tap -= KERNELS[layer]
+        owners = slice(first_tap * each, (first_tap + KERNELS[layer]) * each)
+        fetches[layer] = [
+            pltpu.make_async_copy(source, target, in_sems.at[layer - 1])
+            for source, target in (
+                (stack_ref.at[owners, : CH // each], stack_copy.at[owners]),
+                (hidden_sources[layer - 1], hidden_refs[layer - 1]),
+                (value_sources[layer - 1], value_refs[layer - 1]),
+            )
+        ]
+        for fetch in fetches[layer]:
+            fetch.start()
     frames = grad_ref.shape[0]
     grad, gain, shift = norm_bwd(
         (unit_ref[...], scale_ref[:, :1]), small_ref[10:11, :], grad_ref[...]
@@ -302,7 +320,7 @@
         kernel = KERNELS[layer]
         offset -= kernel * CH
         slot = layer % 2
-        for copy in copies[slot]:
+        for copy in fetches[layer] + copies[slot]:
             copy.wait()
         held = buffer_ref.at[slot, 0 : kernel * CH]
         tail_source = None if tail_grad is None else hidden_tail_ref[layer - 1]
@@ -313,7 +331,7 @@
         values, target = value_refs[layer - 1], grad_refs[layer - 1]
 
         def weight_of(tap, offset=offset):
-            return stack_rows(stack_ref, offset // CH + tap)
+            return stack_rows(stack_copy, offset // CH + tap)
 
         def write(index, size, even, odd, values=values, target=target, kernel=kernel):
             if kernel == 3:
@@ -430,7 +448,7 @@
     part = shape((sum(KERNELS), CH // 2, CH), F32)
     return pl.pallas_call(
         lambda *refs: encode_back_kernel(order, *refs),
-        in_specs=[SMEM] + [VMEM] * 18,
+        in_specs=[SMEM] + [VMEM] * 4 + [ANY] * 6 + [VMEM] + [ANY] * 5 + [VMEM] * 2,
         out_specs=[ANY, ANY, VMEM, VMEM, VMEM],
         out_shape=[
             part,
@@ -446,6 +464,13 @@
             plane,
             plane,
             pltpu.SemaphoreType.DMA((2,)),
+        ]
+        + [pltpu.VMEM(array.shape, array.dtype) for array in outs[:5] + outs[6:11]]
+        + [
+            pltpu.VMEM(
+                (stack.shape[0], sum(KERNELS) * CH // stack.shape[0], CH), BF16
+            ),
+            pltpu.SemaphoreType.DMA((5,)),
         ],
         name="encode_back",
         compiler_params=kernel_params(),
@@ -970,9 +995,13 @@
                 values = lax.psum(values, axis)
                 continue
             bit = 1
+            if (size.bit_length() - 1) % 2:
+                values = values + self.flip(values, axis, bit)
+                bit = 2
             while bit < size:
-                values = values + self.flip(values, axis, bit)
-                bit *= 2
+                near, far, both = (self.flip(values, axis, bit * k) for k in (1, 2, 3))
+                values = (values + near) + (far + both)
+                bit *= 4
         return values
 
     def go(self, requests):
@@ -1266,7 +1295,7 @@
         feed = Stages(links, [links.half_steps(*grads)])
         normed_grad = feed.tie(normed_grad)
         *parts, second, second_tail, norm_grad = encode_back(
-            order, core, outs, small_low, stack, frames, normed_grad
+            order, core, list(outs), small_low, stack, frames, normed_grad
         )
         parts = second_dw(order, core, second, second_tail, hidden, hidden_tail, parts)
         parts = feed.advance(tuple(parts))
@@ -1295,7 +1324,7 @@
         core = jnp.zeros((1,), jnp.int32)
         order = list(range(sum(KERNELS)))
         *parts, second, second_tail, norm_grad = encode_back(
-            order, core, outs, small_low, stack, frames, normed_grad
+            order, core, list(outs), small_low, stack, frames, normed_grad
         )
         parts = second_dw(order, core, second, second_tail, hidden, hidden_tail, parts)
         tap_grad = second_dx(second, second_tail, stack, taps, first_weights, frames)

time: 670 us -> 666 us (level)
  waiting for transfers between devices: 181 us -> 171 us
  starting transfers between devices: 89.3 us -> 98.8 us
    ppermute x37 -> x44, waiting for transfers between devices: 85.1 us -> 74.9 us  [flip(): return lax.ppermute(values, axis, [(i, i ^ bit) for i in range(size)])]
    ppermute x37 -> x44, starting transfers between devices: 41.9 us -> 51.6 us  [flip(): return lax.ppermute(values, axis, [(i, i ^ bit) for i in range(size)])]
  transfers between devices with their start and end apart: 58 -> 65, of which waited for: 25 -> 24; matrix products, arithmetic and copies ran while one was open for 21% -> 21% of each run, Pallas kernels for 24% -> 23%
where the time goes in v4:
time: 666 us; the launch traced here: 656 us
  Pallas kernels  201 us (30%)
  waiting for transfers between devices  171 us (26%)
  starting transfers between devices  98.8 us (15%)
  other arithmetic  81.6 us (12%)
  local copies, waits for them, and re-layouts  72.8 us (11%)
  between operations  20.8 us (3%)
  matrix products  10.6 us (2%)
    ppermute x44, waiting for transfers between devices, flip(): return lax.ppermute(values, axis, [(i, i ^ bit) for i in range(size)])  74.9 us
    ppermute x18, waiting for transfers between devices, step_z(): return lax.ppermute(values, 'dp', pairs)  70 us
    ppermute x44, starting transfers between devices, flip(): return lax.ppermute(values, axis, [(i, i ^ bit) for i in range(size)])  51.6 us
    ppermute x18, starting transfers between devices, step_z(): return lax.ppermute(values, 'dp', pairs)  47.1 us
    pallas_call x1, Pallas kernels, student_step(): pl.pallas_call(student_kernel, in_specs=[SMEM] + [VMEM] * 12 + [ANY] * le...  36.9 us
    pallas_call x1, Pallas kernels, encode_fwd(): pl.pallas_call(encode_kernel, in_specs=[VMEM] * 4, out_specs=[VMEM] * 16,...  34.7 us
    pallas_call x1, Pallas kernels, encode_back(): pl.pallas_call(lambda *refs: encode_back_kernel(order, *refs), in_specs=[...  29.3 us
    pallas_call x1, Pallas kernels, second_dx(): pl.pallas_call(second_dx_kernel, grid=(1,), in_specs=[VMEM, VMEM, pl.Bloc...  26.3 us
  transfers between devices with their start and end apart: 65, of which 24 were waited for; matrix products, arithmetic and copies ran while one was open for 21% of the time, Pallas kernels for 23%

profile of v4, /device:TPU:0, one launch (start us, length us, event | category | flops | bytes accessed | tf_op | source)
XLA Modules:
  0.0 656.0 jit_solution(13510700382656496644)
XLA Ops:
  13.9 6.3 collective-permute-start
  28.7 20.8 %first_layer.1.hidden_ref.refs_3_ = bf16[33,2,128,512]{3,2,1,0:T(8,128)(2,1)} custom-call(bf16[66,128,16]{2,1,0:T(8,128)(2,1)} %copy.118.taps_ref, bf16[16,512]{1,0:T(8,128)(2,1)} %pad.27.weight_ref.first_ref), custom_call_target="tpu_custom_call" | custom-call | tf_op jit(solution)/shard_map/first_layer/pallas_call | solution.py:411
  53.8 20.1 %collective-permute-done.4 = bf16[3,96,768]{2,1,0:T(8,128)(2,1)S(1)} collective-permute-done((bf16[3,96,768]{2,1,0:T(8,128)(2,1)}, bf16[3,96,768]{2,1,0:T(8,128)(2,1)S(1)}, u32[]{:S(2)}, u32[]{:S(2)}) %collective-permute-start.4) | collective-permute-done | bytes 442400 | tf_op jit(solution)/shard_map/ppermute | solution.py:989
  79.4 33.3 %collective-permute-done.5 = bf16[3,96,768]{2,1,0:T(8,128)(2,1)S(1)} collective-permute-done((bf16[3,96,768]{2,1,0:T(8,128)(2,1)S(1)}, bf16[3,96,768]{2,1,0:T(8,128)(2,1)S(1)}, u32[]{:S(2)}, u32[]{:S(2)}) %collective-permute-start.5) | collective-permute-done | bytes 442400 | tf_op jit(solution)/shard_map/ppermute | solution.py:989
  126.2 6.4 collective-permute-start.17
  144.8 10.0 %reshape.181 = bf16[8,4,96,548]{3,2,1,0:T(8,128)(2,1)} reshape(bf16[32,52608]{1,0:T(8,128)(2,1)S(1)} %slice.239) | data formatting | bytes 6733824 | tf_op jit(solution)/shard_map/reshape | solution.py:1228
  154.8 6.2 copy.131
  160.9 6.1 reshape.182
  167.0 34.7 %encode.1 = (f32[32,128,512]{2,1,0:T(8,128)}, f32[16,128,512]{2,1,0:T(8,128)}, f32[8,128,512]{2,1,0:T(8,128)}, f32[4,128,512]{2,1,0:T(8,128)}, f32[2,128,512]{2,...) custom-call(bf16[33,2,128,512]{3,2,1,0:T(8,128)(2,1)} %first_layer.1, ...), custom_call_target="tpu_custom_call" | custom-call | tf_op jit(solution)/shard_map/encode/pallas_call | solution.py:427
  220.2 8.6 %spread.1.spread_ref = bf16[19,768,384]{2,1,0:T(8,128)(2,1)} custom-call(bf16[768,912]{1,0:T(8,128)(2,1)} %slice.219.side_ref, bf16[48,384]{1,0:T(8,128)(2,1)} %constant.486.clone.tile_ref), custom_call_target="tpu_custom_call" | custom-call | tf_op jit(solution)/shard_map/spread/pallas_call | solution.py:901
  230.0 25.8 %all-gather.7.cloned.1.call-done = bf16[96,96,768]{2,1,0:T(8,128)(2,1)} async-done(((bf16[3,96,768]{2,1,0:T(8,128)(2,1)}), bf16[96,96,768]{2,1,0:T(8,128)(2,1)}) %all-gather.7.cloned.1.call-update) | async-done | bytes 14155792 | tf_op jit(solution)/shard_map/all_gather | solution.py:1048
  255.8 16.6 %teacher.1.target_ref = f32[128,768]{1,0:T(8,128)} custom-call(s32[3]{0:T(128)} %pad_add_fusion.place_ref, f32[128,768]{1,0:T(8,128)} %convolution_add_fusion.1.feat_ref, f32[128,32]{1,0:T(8,128)} %pad_convert_fusion.near_ref, s32[128,1]{1,0:T(8,128)} %copy.122.col_ref, s32[1,128]{1,0:T(1,128)} %bitcast.267, bf16[19,768,384]{2,1,0:T(8,128)(2,1)} %spread.1.spread_ref, ...), custom_call_target="tpu_custom_call" | custom-call | tf_op jit(solution)/shard_map/teacher/pallas_call | solution.py:919
  280.2 36.9 %student.1 = (bf16[4,128,768]{2,1,0:T(8,128)(2,1)}, bf16[3,128,3072]{2,1,0:T(8,128)(2,1)}, f32[8,4,96,548]{3,2,1,0:T(8,128)}, f32[10,768]{1,0:T(8,128)}, f32[128,512]{1,0:T(8,128)}, /*index=5*/f32[8,128]{1,0:T(8,128)}) custom-call(s32[3]{0:T(128)} %pad_add_fusion.place_ref, f32[128,768]{1,0:T(8,128)} %convolution_add_fusion.1.feat_ref, ...), custom_call_target="tpu_custom_call" | custom-call | tf_op jit(solution)/shard_map/student/pallas_call | solution.py:935
  325.4 10.7 %block_grads.1 = (bf16[2,4,3,48,768]{4,3,2,1,0:T(8,128)(2,1)}, f32[2,4,3,48,768]{4,3,2,1,0:T(8,128)}, bf16[2,4,3,48,768]{4,3,2,1,0:T(8,128)(2,1)}, f32[2,4,3,48,768]{4,3,2,1,0:T(8,128)}) custom-call(s32[3]{0:T(128)} %pad_add_fusion.place_ref, bf16[4,128,768]{2,1,0:T(8,128)(2,1)} %get-tuple-element.151.left_ref, bf16[4,128,768]{2,1,0:T(8,128)(2,1)} %copy-done.21, ...), custom_call_target="tpu_custom_call" | custom-call | tf_op jit(solution)/shard_map/block_grads/pallas_call | solution.py:870
  337.9 29.3 %encode_back.1 = (f32[16,256,512]{2,1,0:T(8,128)}, f32[16,256,512]{2,1,0:T(8,128)}, bf16[32,128,512]{2,1,0:T(8,128)(2,1)}, bf16[16,512]{1,0:T(8,128)(2,1)}, f32[2,512]{1,0:T(2,128)}) custom-call(s32[1]{0:T(128)} %bitcast.2.refs_0_, f32[128,512]{1,0:T(8,128)} %get-tuple-element.158.refs_1_, f32[128,512]{1,0:T(8,128)} %get-tuple-element.159.refs_2_, ...), custom_call_target="tpu_custom_call" | custom-call | tf_op jit(solution)/shard_map/encode_back/pallas_call | solution.py:449
  367.2 16.9 %second_dw.1 = (f32[16,256,512]{2,1,0:T(8,128)}, f32[16,256,512]{2,1,0:T(8,128)}) custom-call(s32[1]{0:T(128)} %bitcast.2.refs_0_, bf16[32,128,512]{2,1,0:T(8,128)(2,1)} %get-tuple-element.201.refs_1_.grad_ref, bf16[16,512]{1,0:T(8,128)(2,1)} %get-tuple-element.175.refs_2_.tail_grad_ref, ...), custom_call_target="tpu_custom_call", output_to_operand_aliasing={{0}: (5, {}), {1}: (6, {})} | custom-call | tf_op jit(solution)/shard_map/second_dw/pallas_call | solution.py:481
  413.5 17.8 %collective-permute-done.29 = f32[4,3,48,768]{3,2,1,0:T(8,128)} collective-permute-done((f32[4,3,48,768]{3,2,1,0:T(8,128)S(1)}, f32[4,3,48,768]{3,2,1,0:T(8,128)}, u32[]{:S(2)}, u32[]{:S(2)}) %collective-permute-start.29) | collective-permute-done | bytes 1769504 | tf_op jit(solution)/shard_map/ppermute | solution.py:984
  445.0 26.3 %second_dx.1 = f32[16,512]{1,0:T(8,128)} custom-call(bf16[32,128,512]{2,1,0:T(8,128)(2,1)} %get-tuple-element.201.refs_1_.grad_ref, bf16[16,512]{1,0:T(8,128)(2,1)} %get-tuple-element.175.refs_2_.tail_grad_ref, bf16[32,368,512]{2,1,0:T(8,128)(2,1)} %bitcast.250, bf16[66,128,16]{2,1,0:T(8,128)(2,1)} %copy.118.taps_ref, ...), custom_call_target="tpu_custom_call" | custom-call | tf_op jit(solution)/shard_map/second_dx/pallas_call | solution.py:497
  479.5 11.5 %collective-permute-done.27 = f32[2,4,128,512]{3,2,1,0:T(8,128)} collective-permute-done((f32[2,4,128,512]{3,2,1,0:T(8,128)}, f32[2,4,128,512]{3,2,1,0:T(8,128)}, u32[]{:S(2)}, u32[]{:S(2)}) %collective-permute-start.27) | collective-permute-done | bytes 2097184 | tf_op jit(solution)/shard_map/ppermute | solution.py:984
  500.0 5.6 collective-permute-done.35
  508.5 20.7 %collective-permute-done.33 = f32[4,128,512]{2,1,0:T(8,128)} collective-permute-done((f32[4,128,512]{2,1,0:T(8,128)}, f32[4,128,512]{2,1,0:T(8,128)}, u32[]{:S(2)}, u32[]{:S(2)}) %collective-permute-start.33) | collective-permute-done | bytes 1048608 | tf_op jit(solution)/shard_map/ppermute | solution.py:984
  541.9 9.5 %collective-permute-done.46 = f32[256,512]{1,0:T(8,128)} collective-permute-done((f32[256,512]{1,0:T(8,128)}, f32[256,512]{1,0:T(8,128)}, u32[]{:S(2)}, u32[]{:S(2)}) %collective-permute-start.46) | collective-permute-done | bytes 524320 | tf_op jit(solution)/shard_map/ppermute | solution.py:989
  577.3 5.6 collective-permute-start.48
  616.2 6.2 collective-permute-start.57
  (340 shorter events, 243.5 us)
Async XLA Ops:
  7.2 133.9 %all-gather.5.cloned.1.call-start = ((), (), s32[]{:S(2)}) async-start(), calls=%async_computation.2 | async-start | bytes 12435456 | tf_op jit(solution)/shard_map/all_gather | solution.py:1215
  10.8 245.0 %all-gather.7.cloned.1.call-start = ((), (), s32[]{:S(2)}) async-start(), calls=%async_computation.3 | async-start | bytes 14598144 | tf_op jit(solution)/shard_map/all_gather | solution.py:1048
  11.7 572.7 %reduce-scatter.2.cloned.1.call-start = ((), (), s32[]{:S(2)}) async-start(), calls=%async_computation.1 | async-start | bytes 8110080 | tf_op jit(solution)/shard_map/reduce_scatter | solution.py:1288
  12.6 37.0 %collective-permute-start.1 = (bf16[3,96,768]{2,1,0:T(8,128)(2,1)}, bf16[3,96,768]{2,1,0:T(8,128)(2,1)}, u32[]{:S(2)}, u32[]{:S(2)}) collective-permute-start(bf16[3,96,768]{2,1,0:T(8,128)(2,1)} %convert_element_type.82), channel_id=1, source_target_pairs={{8,0},{12,4},{16,8},{20,12},{24,16},{28,20},{9,1},{13,5},{17,9},{2... | collective-permute-start | bytes 1327112 | tf_op jit(solution)/shard_map/ppermute | solution.py:989
  13.9 35.7 %collective-permute-start = (bf16[3,96,768]{2,1,0:T(8,128)(2,1)}, bf16[3,96,768]{2,1,0:T(8,128)(2,1)}, u32[]{:S(2)}, u32[]{:S(2)}) collective-permute-start(bf16[3,96,768]{2,1,0:T(8,128)(2,1)} %convert_element_type.82), channel_id=1, source_target_pairs={{0,8},{4,12},{8,16},{12,20},{16,24},{20,28},{1,9},{5,13},{9,17},{1... | collective-permute-start | bytes 1327112 | tf_op jit(solution)/shard_map/ppermute | solution.py:989
  73.9 38.8 %collective-permute-start.5 = (bf16[3,96,768]{2,1,0:T(8,128)(2,1)S(1)}, bf16[3,96,768]{2,1,0:T(8,128)(2,1)S(1)}, u32[]{:S(2)}, u32[]{:S(2)}) collective-permute-start(bf16[3,96,768]{2,1,0:T(8,128)(2,1)S(1)} %collective-permute-done.4), channel_id=1, source_target_pairs={{8,0},{12,4},{9,1},{13,5},{10,2},{14,6},{11,3},{15,7}} | collective-permute-start | bytes 1327112 | tf_op jit(solution)/shard_map/ppermute | solution.py:989
  115.5 86.2 %collective-permute-start.10 = (bf16[4,3,96,768]{3,2,1,0:T(8,128)(2,1)}, bf16[4,3,96,768]{3,2,1,0:T(8,128)(2,1)}, u32[]{:S(2)}, u32[]{:S(2)}) collective-permute-start(bf16[4,3,96,768]{3,2,1,0:T(8,128)(2,1)} %constant_dynamic-slice_fusion.2.refs_0_), channel_id=1, source_target_pairs={{0,1},{1,0},{2,3},{3,2},{4,5},{5,4},{6,7},{7,6},{8,9},{9,8},{10,11... | collective-permute-start | bytes 5308424 | tf_op jit(solution)/shard_map/ppermute | solution.py:984
  133.1 68.6 %collective-permute-start.6 = (bf16[4,3,96,384]{3,2,1,0:T(8,128)(2,1)}, bf16[4,3,96,384]{3,2,1,0:T(8,128)(2,1)}, u32[]{:S(2)}, u32[]{:S(2)}) collective-permute-start(bf16[4,3,96,384]{3,2,1,0:T(8,128)(2,1)} %get-tuple-element.129), channel_id=1, source_target_pairs={{0,2},{1,3},{2,0},{3,1},{4,6},{5,7},{6,4},{7,5},{8,10},{9,11},{10,... | collective-permute-start | bytes 2654216 | tf_op jit(solution)/shard_map/ppermute | solution.py:984
  134.1 67.7 %collective-permute-start.7 = (bf16[4,3,96,384]{3,2,1,0:T(8,128)(2,1)}, bf16[4,3,96,384]{3,2,1,0:T(8,128)(2,1)}, u32[]{:S(2)}, u32[]{:S(2)}) collective-permute-start(bf16[4,3,96,384]{3,2,1,0:T(8,128)(2,1)} %get-tuple-element.130), channel_id=1, source_target_pairs={{0,4},{4,0},{8,12},{12,8},{16,20},{20,16},{24,28},{28,24},{1,5},{5... | collective-permute-start | bytes 2654216 | tf_op jit(solution)/shard_map/ppermute | solution.py:984
  137.1 64.6 %collective-permute-start.8 = (bf16[4,3,96,384]{3,2,1,0:T(8,128)(2,1)}, bf16[4,3,96,384]{3,2,1,0:T(8,128)(2,1)}, u32[]{:S(2)}, u32[]{:S(2)}) collective-permute-start(bf16[4,3,96,384]{3,2,1,0:T(8,128)(2,1)} %get-tuple-element.129), channel_id=1, source_target_pairs={{0,4},{4,0},{8,12},{12,8},{16,20},{20,16},{24,28},{28,24},{1,5},{5... | collective-permute-start | bytes 2654216 | tf_op jit(solution)/shard_map/ppermute | solution.py:984
  138.6 63.2 %collective-permute-start.9 = (bf16[4,3,96,384]{3,2,1,0:T(8,128)(2,1)}, bf16[4,3,96,384]{3,2,1,0:T(8,128)(2,1)}, u32[]{:S(2)}, u32[]{:S(2)}) collective-permute-start(bf16[4,3,96,384]{3,2,1,0:T(8,128)(2,1)} %get-tuple-element.130), channel_id=1, source_target_pairs={{0,2},{1,3},{2,0},{3,1},{4,6},{5,7},{6,4},{7,5},{8,10},{9,11},{10,... | collective-permute-start | bytes 2654216 | tf_op jit(solution)/shard_map/ppermute | solution.py:984
  205.5 67.0 %collective-permute-start.20 = (bf16[4,4,3,96,384]{4,3,2,1,0:T(8,128)(2,1)}, bf16[4,4,3,96,384]{4,3,2,1,0:T(8,128)(2,1)}, u32[]{:S(2)}, u32[]{:S(2)}) collective-permute-start(bf16[4,4,3,96,384]{4,3,2,1,0:T(8,128)(2,1)} %pad_maximum_fusion), channel_id=1, source_target_pairs={{0,1},{1,0},{2,3},{3,2},{4,5},{5,4},{6,7},{7,6},{8,9},{9,8},{10,11... | collective-permute-start | bytes 10616840 | tf_op jit(solution)/shard_map/ppermute | solution.py:984
  205.5 66.9 %collective-permute-start.18 = (bf16[4,3,96,384]{3,2,1,0:T(8,128)(2,1)}, bf16[4,3,96,384]{3,2,1,0:T(8,128)(2,1)}, u32[]{:S(2)}, u32[]{:S(2)}) collective-permute-start(bf16[4,3,96,384]{3,2,1,0:T(8,128)(2,1)} %collective-permute-done.6.refs_1_), channel_id=1, source_target_pairs={{0,4},{4,0},{8,12},{12,8},{16,20},{20,16},{24,28},{28,24},{1,5},{5... | collective-permute-start | bytes 2654216 | tf_op jit(solution)/shard_map/ppermute | solution.py:984
  206.3 66.1 %collective-permute-start.19 = (bf16[4,3,96,384]{3,2,1,0:T(8,128)(2,1)}, bf16[4,3,96,384]{3,2,1,0:T(8,128)(2,1)}, u32[]{:S(2)}, u32[]{:S(2)}) collective-permute-start(bf16[4,3,96,384]{3,2,1,0:T(8,128)(2,1)} %collective-permute-done.7.refs_2_), channel_id=1, source_target_pairs={{0,2},{1,3},{2,0},{3,1},{4,6},{5,7},{6,4},{7,5},{8,10},{9,11},{10,... | collective-permute-start | bytes 2654216 | tf_op jit(solution)/shard_map/ppermute | solution.py:984
  336.1 48.0 %collective-permute-start.24 = (bf16[2,4,3,48,768]{4,3,2,1,0:T(8,128)(2,1)}, bf16[2,4,3,48,768]{4,3,2,1,0:T(8,128)(2,1)}, u32[]{:S(2)}, u32[]{:S(2)}) collective-permute-start(bf16[2,4,3,48,768]{4,3,2,1,0:T(8,128)(2,1)} %get-tuple-element.156), channel_id=1, source_target_pairs={{0,4},{4,0},{8,12},{12,8},{16,20},{20,16},{24,28},{28,24},{1,5},{5... | collective-permute-start | bytes 5308424 | tf_op jit(solution)/shard_map/ppermute | solution.py:984
  337.3 46.8 %collective-permute-start.25 = (bf16[2,4,3,48,768]{4,3,2,1,0:T(8,128)(2,1)}, bf16[2,4,3,48,768]{4,3,2,1,0:T(8,128)(2,1)}, u32[]{:S(2)}, u32[]{:S(2)}) collective-permute-start(bf16[2,4,3,48,768]{4,3,2,1,0:T(8,128)(2,1)} %get-tuple-element.157), channel_id=1, source_target_pairs={{0,2},{1,3},{2,0},{3,1},{4,6},{5,7},{6,4},{7,5},{8,10},{9,11},{10,... | collective-permute-start | bytes 5308424 | tf_op jit(solution)/shard_map/ppermute | solution.py:984
  389.8 41.5 %collective-permute-start.29 = (f32[4,3,48,768]{3,2,1,0:T(8,128)S(1)}, f32[4,3,48,768]{3,2,1,0:T(8,128)}, u32[]{:S(2)}, u32[]{:S(2)}) collective-permute-start(f32[4,3,48,768]{3,2,1,0:T(8,128)S(1)} %copy-done.17), channel_id=1, source_target_pairs={{0,2},{1,3},{2,0},{3,1},{4,6},{5,7},{6,4},{7,5},{8,10},{9,11},{10,... | collective-permute-start | bytes 5308424 | tf_op jit(solution)/shard_map/ppermute | solution.py:984
  391.2 41.5 %collective-permute-start.30 = (f32[4,3,48,768]{3,2,1,0:T(8,128)S(1)}, f32[4,3,48,768]{3,2,1,0:T(8,128)}, u32[]{:S(2)}, u32[]{:S(2)}) collective-permute-start(f32[4,3,48,768]{3,2,1,0:T(8,128)S(1)} %add_bitcast_fusion.2), channel_id=1, source_target_pairs={{0,4},{4,0},{8,12},{12,8},{16,20},{20,16},{24,28},{28,24},{1,5},{5... | collective-permute-start | bytes 5308424 | tf_op jit(solution)/shard_map/ppermute | solution.py:984
  411.2 79.8 %collective-permute-start.27 = (f32[2,4,128,512]{3,2,1,0:T(8,128)}, f32[2,4,128,512]{3,2,1,0:T(8,128)}, u32[]{:S(2)}, u32[]{:S(2)}) collective-permute-start(f32[2,4,128,512]{3,2,1,0:T(8,128)} %add_bitcast_fusion.1), channel_id=1, source_target_pairs={{0,4},{4,0},{8,12},{12,8},{16,20},{20,16},{24,28},{28,24},{1,5},{5... | collective-permute-start | bytes 6291464 | tf_op jit(solution)/shard_map/ppermute | solution.py:984
  413.1 77.9 %collective-permute-start.28 = (f32[2,4,128,512]{3,2,1,0:T(8,128)}, f32[2,4,128,512]{3,2,1,0:T(8,128)}, u32[]{:S(2)}, u32[]{:S(2)}) collective-permute-start(f32[2,4,128,512]{3,2,1,0:T(8,128)} %add_bitcast_fusion), channel_id=1, source_target_pairs={{0,2},{1,3},{2,0},{3,1},{4,6},{5,7},{6,4},{7,5},{8,10},{9,11},{10,... | collective-permute-start | bytes 6291464 | tf_op jit(solution)/shard_map/ppermute | solution.py:984
  438.7 32.5 %collective-permute-start.31 = (f32[3,96,768]{2,1,0:T(8,128)}, f32[3,96,768]{2,1,0:T(8,128)}, u32[]{:S(2)}, u32[]{:S(2)}) collective-permute-start(f32[3,96,768]{2,1,0:T(8,128)} %get-tuple-element.199), channel_id=1, source_target_pairs={{0,8},{4,12},{1,9},{5,13},{2,10},{6,14},{3,11},{7,15}} | collective-permute-start | bytes 2654216 | tf_op jit(solution)/shard_map/ppermute | solution.py:989
  474.1 31.5 %collective-permute-start.35 = (f32[3,96,768]{2,1,0:T(8,128)}, f32[3,96,768]{2,1,0:T(8,128)}, u32[]{:S(2)}, u32[]{:S(2)}) collective-permute-start(f32[3,96,768]{2,1,0:T(8,128)} %get-tuple-element.211), channel_id=1, source_target_pairs={{0,8},{4,12},{8,16},{12,20},{1,9},{5,13},{9,17},{13,21},{2,10},{6,... | collective-permute-start | bytes 2654216 | tf_op jit(solution)/shard_map/ppermute | solution.py:989
  497.4 31.8 %collective-permute-start.33 = (f32[4,128,512]{2,1,0:T(8,128)}, f32[4,128,512]{2,1,0:T(8,128)}, u32[]{:S(2)}, u32[]{:S(2)}) collective-permute-start(f32[4,128,512]{2,1,0:T(8,128)} %bitcast_add_fusion.4), channel_id=1, source_target_pairs={{0,2},{1,3},{2,0},{3,1},{4,6},{5,7},{6,4},{7,5},{8,10},{9,11},{10,... | collective-permute-start | bytes 3145736 | tf_op jit(solution)/shard_map/ppermute | solution.py:984
  498.2 31.0 %collective-permute-start.34 = (f32[4,128,512]{2,1,0:T(8,128)}, f32[4,128,512]{2,1,0:T(8,128)}, u32[]{:S(2)}, u32[]{:S(2)}) collective-permute-start(f32[4,128,512]{2,1,0:T(8,128)} %bitcast_add_fusion.3), channel_id=1, source_target_pairs={{0,4},{4,0},{8,12},{12,8},{16,20},{20,16},{24,28},{28,24},{1,5},{5... | collective-permute-start | bytes 3145736 | tf_op jit(solution)/shard_map/ppermute | solution.py:984
  (83 other events, 978.0 us)
Sparse Core Ops, SparseCore 0:
  11.5 110.2 all-gather.4
  125.3 130.4 all-gather.6
  388.4 157.3 reduce-scatter.1
